TPU v7x, 32 devices: a whole 2x2x4 slice. The times are simulated.
32 devices in a mesh: vocab: 4 (over z), rows: 8 (over y, x, core).
Axes of the slice: x: 2, y: 2, z: 4, core: 2. Of those that a mesh axis runs over, the one named last changes fastest.
Arguments:
- hidden_pass: bfloat16 [96, 64, 4096], P('rows', None, 'vocab'), may hold values from -6 to 6
- hidden_query: bfloat16 [96, 8, 4096], P('rows', None, 'vocab'), may hold values from -6 to 6
- mask_pass: int32 [96, 64], P('rows'), may hold values 0 or 1
- mask_query: int32 [96, 8], P('rows'), may hold values 0 or 1
- labels: int32 [96], P('rows'), may hold values from 0 to 95, each once
- head_weight: bfloat16 [4096, 16384], P('rows', 'vocab'), may hold values from -1 to 1
Outputs:
- grad_pass: bfloat16 [96, 64, 4096], P('rows', None, 'vocab')
- grad_query: bfloat16 [96, 8, 4096], P('rows', None, 'vocab')
Inputs may be any that keep to these rules, and one draw needn't show every extreme that they name: `labels`: each passage is the positive of exactly one query.
All inputs are finite; a program needn't handle non-finite values. No bound on the sum of `mask_pass` or of `mask_query` on one device may be relied on, other than what follows from the above.
Results may differ from a plain program's by a relative error of at most 0.018.
The roundings to bfloat16 on the way count: a program that leaves them out, or rounds other values in their place, can miss the bound.
Values may be sent and summed in bfloat16 or wider, within the bound.
No kernel may reach another device: no remote copies, remote signals or barrier semaphores. Data moves between devices by JAX's collectives and lax.ppermute only.
A program may use at most 128 MiB of HBM per device.

v0:
```python
import functools

import jax
import jax.numpy as jnp
from jax import lax
from jax.experimental import pallas as pl
from jax.experimental.pallas import tpu as pltpu
from jax.sharding import PartitionSpec as P


MARGIN = 1.0
SHARPNESS = 16.0

CORES = 2


def chip_grid(n_rows):
    chips = n_rows // CORES
    tall = 1
    while (tall * 2) ** 2 <= chips and chips % (tall * 2) == 0:
        tall *= 2
    return tall, chips // tall


def line_gather(block, n):
    found = {0: block}
    left = right = block
    for step in range(1, n):
        left = lax.ppermute(left, "vocab", [(z, z - 1) for z in range(1, n - step + 1)])
        right = lax.ppermute(right, "vocab", [(z, z + 1) for z in range(step - 1, n - 1)])
        found[step] = left
        found[-step] = right
    return found


def two_paths(n_rows, n_vocab):
    return chip_grid(n_rows) == (2, 2) and n_rows == CORES * n_vocab


def row_gather(block, n_rows, n_vocab):
    if not two_paths(n_rows, n_vocab):
        whole = lax.all_gather(block, "rows", axis=0)
        return [whole[r] for r in range(n_rows)]
    x_bit, y_bit = CORES, CORES * 2
    main = [(r, r ^ (x_bit if r % CORES == 0 else y_bit)) for r in range(n_rows)]
    side = [(r, r ^ (y_bit if r % CORES == 0 else x_bit)) for r in range(n_rows)]
    twin = [(r, r ^ 1) for r in range(n_rows)]

    def move(value, pairs):
        return lax.ppermute(value, "rows", pairs)

    by_main = move(block, main)
    by_side = move(block, side)
    own_twin = move(block, twin)
    far = move(by_side, main)
    main_twin = move(by_main, twin)
    side_twin = move(by_side, twin)
    far_twin = move(far, twin)
    return [block, own_twin, by_main, side_twin, by_side, main_twin, far, far_twin]


def row_order(r, n_rows, n_vocab):
    if not two_paths(n_rows, n_vocab):
        return list(range(n_rows))
    x_bit, y_bit = CORES, CORES * 2
    along, across = (x_bit, y_bit) if r % CORES == 0 else (y_bit, x_bit)
    return [r ^ hop ^ core for hop in (0, along, across, x_bit | y_bit) for core in (0, 1)]


class Plan:
    def __init__(self, n_vocab, n_rows, depth):
        share = n_rows // n_vocab
        self.at, self.table = {}, []
        for z in range(n_vocab):
            for r in range(n_rows):
                lists = {}
                order = row_order(r, n_rows, n_vocab)
                lists["order"] = order
                early = n_rows * 3 // 4
                if two_paths(n_rows, n_vocab):
                    late = [i for i in range(3) if abs(order[2 * i] // share - z) == n_vocab - 1]
                    wait = late[0] if late else 2
                    rest = [i for i in range(3) if i != wait]
                    picks = {
                        "soon": [2 * i + core for i in rest for core in range(2)],
                        "then": [2 * wait, 2 * wait + 1],
                    }
                else:
                    picks = {"soon": list(range(early))}
                picks["last"] = list(range(early, n_rows))
                for name, pick in picks.items():
                    lists[name] = (
                        pick
                        + [order[i] // share - z for i in pick]
                        + [order[i] % share * depth for i in pick]
                    )
                place = {row: i for i, row in enumerate(order)}
                for i in range(share):
                    of = lambda block: place[block % n_vocab * share + i]
                    for step in range(1, n_vocab):
                        if 2 * step <= n_vocab:
                            units = [z + step if z + step >= n_vocab else z - step]
                        else:
                            units = [z + step, z - step]
                        lists[f"part{step}_{i}"] = [of(block) for block in units]
                    lists[f"own_{i}"] = [of(z)]
                row = []
                for name, values in lists.items():
                    self.at[name] = len(row)
                    row += values
                self.table.append(row)
        self.n_rows = n_rows

    def row(self):
        index = lax.axis_index("vocab") * self.n_rows + lax.axis_index("rows")
        table = jnp.array(self.table, jnp.int32)
        return lax.dynamic_slice(table, (index, 0), (1, table.shape[1]))[0]


def pooled(x, groups):
    length = x.shape[0] // groups
    u = 1.0 + x
    inverse = 1.0 / u
    act = jnp.log(u) + (x - (u - 1.0)) * inverse
    square = act * act
    total = jnp.sum((square * square).reshape(groups, length, -1), axis=1)
    return total, square * act * inverse


def forward_kernel(spec, plan_ref, *refs):
    at, skip, count, codes, n_pieces, depth, tile, has_total, final, groups, pass_rows = spec
    refs = list(refs)
    sources = [(code, refs.pop(0)) for code in codes]
    pieces = [refs.pop(0) for _ in range(n_pieces)]
    start_ref = refs.pop(0) if has_total else None
    mask_ref = refs.pop(0) if final else None
    if final:
        slope_ref, total_ref, sparse_ref = [refs.pop(0) for _ in range(3)]
    else:
        out_ref = refs.pop(0)
    held, weights, held_sem, weight_sem = refs
    step = pl.program_id(0)

    def weight_copy(j, t, which, slot):
        return pltpu.make_async_copy(
            pieces[which].at[:, pl.ds(pl.multiple_of(j * tile, tile), tile)],
            weights.at[slot, t],
            weight_sem.at[slot, t],
        )

    def fetch(j, slot):
        for t in range(count):
            for which in range(n_pieces):
                pl.when(plan_ref[at + t] == which + skip)(weight_copy(j, t, which, slot).start)

    def hidden_copy(t, ref):
        return pltpu.make_async_copy(
            ref.at[:, pl.ds(pl.multiple_of(plan_ref[at + 2 * count + t], 128), depth)], held.at[t], held_sem.at[t]
        )

    @pl.when(step == 0)
    def _():
        fetch(0, 0)
        for t in range(count):
            for code, ref in sources:
                pl.when(plan_ref[at + count + t] == code)(hidden_copy(t, ref).start)

    slot = lax.rem(step, 2)

    @pl.when(step + 1 < pl.num_programs(0))
    def _():
        fetch(step + 1, 1 - slot)

    @pl.when(step == 0)
    def _():
        for t in range(count):
            hidden_copy(t, sources[0][1]).wait()

    for t in range(count):
        weight_copy(step, t, 0, slot).wait()
    value = start_ref[...] if has_total else None
    for t in range(count):
        term = jnp.dot(held[t], weights[slot, t], preferred_element_type=jnp.float32)
        value = term if value is None else value + term
    if not final:
        out_ref[...] = value
        return
    mask = mask_ref[...]
    mask = jnp.concatenate([mask] * (tile // mask.shape[1]), axis=1)
    x = jnp.maximum(value, 0.0) * mask
    totals = []
    for lower, upper in ((0, pass_rows), (pass_rows, x.shape[0])):
        total, slope = pooled(x[lower:upper], groups)
        slope_ref[lower:upper, :] = slope.astype(slope_ref.dtype)
        totals.append(total)
    total = jnp.concatenate(totals, axis=0)
    total_ref[...] = total
    sparse_ref[...] = (jnp.sqrt(jnp.sqrt(total + 1.0)) - 1.0).astype(sparse_ref.dtype)


def forward(found, pieces, plan, at, count, skip=0, start=None, mask=None, groups=0, pass_rows=0, tile=512):
    rows = found[0].shape[0]
    depth, width = pieces[0].shape
    keys = sorted(found)
    final = mask is not None
    anywhere = pl.BlockSpec(memory_space=pl.ANY)
    column = lambda height: pl.BlockSpec((height, tile), lambda j, *_: (0, j))
    operands = [found[key] for key in keys] + list(pieces)
    in_specs = [anywhere] * len(operands)
    if start is not None:
        operands.append(start)
        in_specs.append(column(rows))
    if final:
        operands.append(mask)
        in_specs.append(pl.BlockSpec(mask.shape, lambda j, *_: (0, 0)))
        out_shape = [
            jax.ShapeDtypeStruct((rows, width), jnp.bfloat16),
            jax.ShapeDtypeStruct((2 * groups, width), jnp.float32),
            jax.ShapeDtypeStruct((2 * groups, width), jnp.bfloat16),
        ]
        out_specs = [column(rows), column(2 * groups), column(2 * groups)]
    else:
        out_shape = jax.ShapeDtypeStruct((rows, width), jnp.float32)
        out_specs = column(rows)
    spec = (at, skip, count, tuple(keys), len(pieces), depth, tile, start is not None, final, groups, pass_rows)
    return pl.pallas_call(
        functools.partial(forward_kernel, spec),
        out_shape=out_shape,
        grid_spec=pltpu.PrefetchScalarGridSpec(
            num_scalar_prefetch=1,
            grid=(width // tile,),
            in_specs=in_specs,
            out_specs=out_specs,
            scratch_shapes=[
                pltpu.VMEM((count, rows, depth), jnp.bfloat16),
                pltpu.VMEM((2, count, depth, tile), jnp.bfloat16),
                pltpu.SemaphoreType.DMA((count,)),
                pltpu.SemaphoreType.DMA((2, count)),
            ],
        ),
        compiler_params=pltpu.CompilerParams(
            dimension_semantics=("arbitrary",), vmem_limit_bytes=50 * 1024 * 1024
        ),
        cost_estimate=pl.CostEstimate(
            flops=2 * rows * depth * count * width,
            bytes_accessed=count * depth * width * 2 + rows * width * 8,
            transcendentals=rows * width if final else 0,
        ),
        name="forward_final" if final else "forward_part",
    )(plan, *operands)


def first_kernel(spec, plan_ref, slope_ref, pass_ref, query_ref, *refs):
    at, count, groups, pass_length, query_length = spec
    pieces, (grad_ref, out_ref, held, total, sem) = refs[:count], refs[count:]
    step = pl.program_id(0)
    tile = slope_ref.shape[1]
    steps = held.shape[0]

    def copy(j, which):
        return pltpu.make_async_copy(pieces[which].at[:, pl.ds(j * tile, tile)], held.at[j], sem.at[j])

    @pl.when(step == 0)
    def _():
        for which in range(count):

            @pl.when(plan_ref[at] == which)
            def _():
                for j in range(steps):
                    copy(j, which).start()

        total[...] = jnp.zeros_like(total)

    lower = 0
    for factor_ref, length in ((pass_ref, pass_length), (query_ref, query_length)):
        for p in range(groups):
            rows = pl.ds(lower, length)
            grad_ref[rows, :] = (slope_ref[rows, :].astype(jnp.float32) * factor_ref[p : p + 1, :]).astype(grad_ref.dtype)
            lower += length
    pltpu.make_async_copy(pieces[0].at[:, pl.ds(0, tile)], held.at[step], sem.at[step]).wait()
    total[...] += lax.dot_general(
        grad_ref[...], held[step], (((1,), (1,)), ((), ())), preferred_element_type=jnp.float32
    )

    @pl.when(step == steps - 1)
    def _():
        out_ref[...] = total[...].astype(out_ref.dtype)


def backward_first(slopes, factor_pass, factor_query, lengths, pieces, plan, at, tile=512):
    rows, width = slopes.shape
    groups = factor_pass.shape[0]
    depth = pieces[0].shape[0]
    count = len(pieces)
    column = lambda height: pl.BlockSpec((height, tile), lambda j, *_: (0, j))
    return pl.pallas_call(
        functools.partial(first_kernel, (at, count, groups) + lengths),
        out_shape=[
            jax.ShapeDtypeStruct((rows, width), jnp.bfloat16),
            jax.ShapeDtypeStruct((rows, depth), jnp.bfloat16),
        ],
        grid_spec=pltpu.PrefetchScalarGridSpec(
            num_scalar_prefetch=1,
            grid=(width // tile,),
            in_specs=[column(rows), column(groups), column(groups)]
            + [pl.BlockSpec(memory_space=pl.ANY)] * count,
            out_specs=[column(rows), pl.BlockSpec((rows, depth), lambda j, *_: (0, 0))],
            scratch_shapes=[
                pltpu.VMEM((width // tile, depth, tile), jnp.bfloat16),
                pltpu.VMEM((rows, depth), jnp.float32),
                pltpu.SemaphoreType.DMA((width // tile,)),
            ],
        ),
        compiler_params=pltpu.CompilerParams(
            dimension_semantics=("arbitrary",), vmem_limit_bytes=50 * 1024 * 1024
        ),
        cost_estimate=pl.CostEstimate(
            flops=2 * rows * depth * width,
            bytes_accessed=(depth * width + 2 * rows * width + rows * depth) * 2,
            transcendentals=0,
        ),
        name="backward_first",
    )(plan, slopes, factor_pass, factor_query, *pieces)


def backward_kernel(spec, plan_ref, slopes_ref, *refs):
    at_plan, count, parts, adds = spec
    units = len(adds)
    n_adds = max([0] + [i + 1 for unit in adds for i in unit])
    pieces, refs = refs[:count], refs[count:]
    running, refs = refs[:n_adds], refs[n_adds:]
    outs, (held, slopes, piece_sem, slope_sem) = refs[:units], refs[units:]
    rows = slopes_ref.shape[0] // parts

    def slope_copy(i):
        at = pl.ds(pl.multiple_of(i * rows, 16), rows)
        return pltpu.make_async_copy(slopes_ref.at[at, :], slopes.at[at, :], slope_sem.at[i])

    for unit in range(units):
        for which in range(count):
            copy = pltpu.make_async_copy(pieces[which], held.at[unit], piece_sem.at[unit])
            pl.when(plan_ref[at_plan + unit] == which)(copy.start)
        if unit == 0:
            for i in range(parts):
                slope_copy(i).start()
    for unit in range(units):
        pltpu.make_async_copy(pieces[0], held.at[unit], piece_sem.at[unit]).wait()

        @pl.loop(0, parts)
        def _(i):
            if unit == 0:
                slope_copy(i).wait()
            at = pl.ds(pl.multiple_of(i * rows, 16), rows)
            value = lax.dot_general(
                slopes[at, :], held[unit], (((1,), (1,)), ((), ())), preferred_element_type=jnp.float32
            ).astype(jnp.bfloat16)
            if adds[unit]:
                value = value.astype(jnp.float32)
                for j in adds[unit]:
                    value = value + running[j][at, :].astype(jnp.float32)
            outs[unit][at, :] = value.astype(outs[unit].dtype)


def backward(slopes, pieces, plan, at, running=(), adds=((),)):
    rows, width = slopes.shape
    depth = pieces[0].shape[0]
    count, units = len(pieces), len(adds)
    parts = 3 if rows % 48 == 0 else 1
    whole = pl.BlockSpec(memory_space=pltpu.VMEM)
    anywhere = pl.BlockSpec(memory_space=pl.ANY)
    return pl.pallas_call(
        functools.partial(backward_kernel, (at, count, parts, adds)),
        out_shape=[jax.ShapeDtypeStruct((rows, depth), jnp.bfloat16)] * units,
        in_specs=[pl.BlockSpec(memory_space=pltpu.SMEM)] + [anywhere] * (1 + count) + [whole] * len(running),
        out_specs=[whole] * units,
        scratch_shapes=[
            pltpu.VMEM((units, depth, width), jnp.bfloat16),
            pltpu.VMEM((rows, width), jnp.bfloat16),
            pltpu.SemaphoreType.DMA((units,)),
            pltpu.SemaphoreType.DMA((parts,)),
        ],
        compiler_params=pltpu.CompilerParams(vmem_limit_bytes=50 * 1024 * 1024),
        cost_estimate=pl.CostEstimate(
            flops=2 * rows * depth * units * width,
            bytes_accessed=(units * depth * width + rows * width + units * rows * depth) * 2,
            transcendentals=0,
        ),
        name="backward_part",
    )(plan, slopes, *pieces, *running)


def line_reduce_scatter(first, product, n, share):
    left, right = [None] * share, [None] * share
    for step in range(1, n):
        for i in range(share):
            name = f"part{step}_{i}"
            if step == 1 and i == 0:
                to_left = to_right = first
            elif 2 * step <= n:
                running = () if step == 1 else (left[i], right[i])
                (to_left,) = product(name, running, (tuple(range(len(running))),))
                to_right = to_left
            else:
                to_left, to_right = product(name, (left[i], right[i]), ((0,), (1,)))
            left[i] = lax.ppermute(to_left, "vocab", [(d, d - 1) for d in range(n - step, n)])
            right[i] = lax.ppermute(to_right, "vocab", [(d, d + 1) for d in range(step)])
    terms = []
    for i in range(share):
        own = product(f"own_{i}", (), ((),))[0]
        terms.append(own.astype(jnp.float32) + left[i].astype(jnp.float32) + right[i].astype(jnp.float32))
    return terms


def shards(n_vocab, n_rows, *arguments):
    return body(n_vocab, n_rows, *arguments)


def body(n_vocab, n_rows, hidden_pass, hidden_query, mask_pass, mask_query, labels, head_weight):
    groups, pass_length, part = hidden_pass.shape
    query_length = hidden_query.shape[1]
    pass_rows = groups * pass_length
    depth, width = head_weight.shape
    share = n_rows // n_vocab
    plans = Plan(n_vocab, n_rows, depth)
    plan = plans.row()
    order = plan[plans.at["order"] : plans.at["order"] + n_rows]
    tokens = jnp.concatenate(
        [hidden_pass.reshape(pass_rows, part), hidden_query.reshape(groups * query_length, part)], axis=0
    )
    mask = jnp.concatenate([mask_pass.reshape(-1), mask_query.reshape(-1)]).astype(jnp.float32)
    mask = jnp.broadcast_to(mask[:, None], (mask.shape[0], 128))
    found = line_gather(tokens, n_vocab)
    pieces = row_gather(head_weight, n_rows, n_vocab)
    all_labels = lax.all_gather(labels, "rows", axis=0)[order].reshape(-1)
    passages = (order[:, None] * groups + jnp.arange(groups, dtype=jnp.int32)[None, :]).reshape(-1)
    onehot = (all_labels[:, None] == passages[None, :]).astype(jnp.float32)

    early = n_rows * 3 // 4
    if two_paths(n_rows, n_vocab):
        near = {code: block for code, block in found.items() if abs(code) < n_vocab - 1}
        logits = forward(near, pieces[:early], plan, plans.at["soon"], 4)
        logits = forward(found, pieces[:early], plan, plans.at["then"], 2, start=logits)
    else:
        logits = forward(found, pieces[:early], plan, plans.at["soon"], early)
    slopes, totals, sparse = forward(
        found,
        pieces[early:],
        plan,
        plans.at["last"],
        n_rows - early,
        skip=early,
        start=logits,
        mask=mask,
        groups=groups,
        pass_rows=pass_rows,
    )
    all_sparse = jnp.stack(row_gather(sparse, n_rows, n_vocab))
    all_pass = all_sparse[:, :groups].reshape(-1, width)
    all_query = all_sparse[:, groups:].reshape(-1, width)
    scaling = SHARPNESS * (width * n_vocab) ** (-0.5)
    scores = lax.dot_general(all_query, all_pass, (((1,), (1,)), ((), ())), preferred_element_type=jnp.float32)
    shifted = [
        lax.ppermute(scores, "vocab", [(d, (d + s) % n_vocab) for d in range(n_vocab)]) for s in range(1, n_vocab)
    ]
    for other in shifted:
        scores = scores + other
    scores = scores * scaling
    positive = jnp.sum(scores * onehot, axis=1, keepdims=True)
    weights = jax.nn.sigmoid(MARGIN + scores - positive) * (1.0 - onehot)
    score_grad = ((weights - onehot * jnp.sum(weights, axis=1, keepdims=True)) * scaling).astype(jnp.bfloat16)
    if two_paths(n_rows, n_vocab):
        of_query, of_pass = score_grad[:groups], score_grad[:, :groups]
    else:
        row = lax.axis_index("rows") * groups
        of_query = lax.dynamic_slice_in_dim(score_grad, row, groups, 0)
        of_pass = lax.dynamic_slice_in_dim(score_grad, row, groups, 1)
    query_grad = jnp.dot(of_query, all_pass, preferred_element_type=jnp.float32)
    pass_grad = lax.dot_general(of_pass, all_query, (((0,), (0,)), ((), ())), preferred_element_type=jnp.float32)
    root = jnp.sqrt(jnp.sqrt(totals + 1.0))
    cube = root * root * root
    logit_grad, first = backward_first(
        slopes,
        pass_grad / cube[:groups],
        query_grad / cube[groups:],
        (pass_length, query_length),
        pieces,
        plan,
        plans.at["part1_0"],
    )

    def product(name, running, adds):
        return backward(logit_grad, pieces, plan, plans.at[name], running, adds)

    summed = line_reduce_scatter(first, product, n_vocab, share)
    summed = jnp.concatenate(summed, axis=1).astype(jnp.bfloat16)
    return (
        summed[:pass_rows].reshape(groups, pass_length, part),
        summed[pass_rows:].reshape(groups, query_length, part),
    )


def solution(mesh):
    n_vocab, n_rows = mesh.shape["vocab"], mesh.shape["rows"]
    return jax.shard_map(
        functools.partial(shards, n_vocab, n_rows),
        mesh=mesh,
        in_specs=(
            P("rows", None, "vocab"),
            P("rows", None, "vocab"),
            P("rows", None),
            P("rows", None),
            P("rows"),
            P("rows", "vocab"),
        ),
        out_specs=(P("rows", None, "vocab"), P("rows", None, "vocab")),
        check_vma=False,
    )
```

profile of v0, /device:TPU:0, one launch (start us, length us, event | category | flops | bytes accessed | tf_op | source)
XLA Modules:
  0.0 467.5 jit_solution(3498510591683439427)
XLA Ops:
  0.6 3.1 collective-permute-start.6
  3.7 1.5 collective-permute-start.10
  5.2 89.7 %collective-permute-done.6.refs_9_.refs_11_.refs_4_ = bf16[512,4096]{1,0:T(8,128)(2,1)} collective-permute-done((bf16[512,4096]{1,0:T(8,128)(2,1)}, bf16[512,4096]{1,0:T(8,128)(2,1)}, u32[]{:S(2)}, u32[]{:S(2)}) %collective-permute-start.6) | collective-permute-done | bytes 4194336 | tf_op jit(solution)/shard_map/ppermute | solution.py:50
  94.9 1.5 collective-permute-start.7
  96.4 1.7 pad_maximum_fusion.refs_2_.refs_3_
  98.1 3.7 collective-permute-start
  101.8 1.3 collective-permute-start.3
  103.2 34.5 %collective-permute-done.refs_1_.refs_2_ = bf16[864,1024]{1,0:T(8,128)(2,1)S(1)} collective-permute-done((bf16[864,1024]{1,0:T(8,128)(2,1)S(1)}, bf16[864,1024]{1,0:T(8,128)(2,1)S(1)}, u32[]{:S(2)}, u32[]{:S(2)}) %collective-permute-start) | collective-permute-done | bytes 1769504 | tf_op jit(solution)/shard_map/ppermute | solution.py:30
  138.2 3.8 collective-permute-done.3.refs_3_.refs_4_
  142.8 1.3 collective-permute-start.4
  145.7 1.2 dynamic-slice
  147.9 14.3 %all-reduce = s32[96]{0:T(128)S(1)} all-reduce(s32[96]{0:T(128)S(1)} %dynamic-update-slice), channel_id=2, replica_groups=mesh['vocab'=4,'rows'=8] {'rows'}, use_global_device_ids=true, to_apply=%add | all-reduce | flops 96 | bytes 768
  163.5 56.2 %collective-permute-done.4.refs_4_.refs_5_ = bf16[864,1024]{1,0:T(8,128)(2,1)} collective-permute-done((bf16[864,1024]{1,0:T(8,128)(2,1)}, bf16[864,1024]{1,0:T(8,128)(2,1)}, u32[]{:S(2)}, u32[]{:S(2)}) %collective-permute-start.4) | collective-permute-done | bytes 1769504 | tf_op jit(solution)/shard_map/ppermute | solution.py:29
  219.7 1.9 collective-permute-start.2
  221.6 1.3 collective-permute-start.5
  226.2 21.1 %forward_part.2.refs_13_ = f32[864,4096]{1,0:T(8,128)} custom-call(s32[42]{0:T(128)S(1)} %get-tuple-element.27.plan_ref, bf16[864,1024]{1,0:T(8,128)(2,1)S(1)} %collective-permute-done.1.refs_0_.refs_1_, bf16[864,1024]{1,0:T(8,128)(2,1)S(1)} %collective-permute-done.refs_1_.refs_2_, bf16[864,1024]{1,0:T(8,128)(2,1)} %copy-done.2, ...), custom_call_target="tpu_custom_call" | custom-call | flops 14495514624 | bytes 45088768 | tf_op jit(solution)/shard_map/forward_part/pallas_call | solution.py:226
  247.4 13.4 %collective-permute-done.5.refs_6_ = bf16[864,1024]{1,0:T(8,128)(2,1)} collective-permute-done((bf16[864,1024]{1,0:T(8,128)(2,1)}, bf16[864,1024]{1,0:T(8,128)(2,1)}, u32[]{:S(2)}, u32[]{:S(2)}) %collective-permute-start.5) | collective-permute-done | bytes 1769504 | tf_op jit(solution)/shard_map/ppermute | solution.py:29
  260.8 19.8 %forward_part.3.refs_9_ = f32[864,4096]{1,0:T(8,128)} custom-call(s32[42]{0:T(128)S(1)} %get-tuple-element.27.plan_ref, bf16[864,1024]{1,0:T(8,128)(2,1)} %collective-permute-done.2.refs_0_, bf16[864,1024]{1,0:T(8,128)(2,1)S(1)} %collective-permute-done.1.refs_0_.refs_1_, bf16[864,1024]{1,0:T(8,128)(2,1)} %copy-done, bf16[864,1024]{1,0:T(8,128)(2,1)} %copy-done.2, ...), custom_call_target="tpu_custom_call" | custom-call | flops 7247757312 | bytes 36700160 | tf_op jit(solution)/shard_map/forward_part/pallas_call | solution.py:226
  280.8 20.7 %forward_final.1 = (bf16[864,4096]{1,0:T(8,128)(2,1)}, f32[24,4096]{1,0:T(8,128)S(1)}, bf16[24,4096]{1,0:T(8,128)(2,1)S(1)}) custom-call(s32[42]{0:T(128)S(1)} %get-tuple-element.27.plan_ref, bf16[864,1024]{1,0:T(8,128)(2,1)} %collective-permute-done.2.refs_0_, bf16[864,1024]{1,0:T(8,128)(2,1)} %copy-done.1, bf16[864,1024]{1,0:T(8,128)(2,1)} %copy-done, ...), custom_call_target="tpu_custom_call" | custom-call | flops 7247757312 | bytes 36700160 | tf_op jit(solution)/shard_map/forward_final/pallas_call | solution.py:226
  301.6 1.6 collective-permute-start.14
  303.5 5.4 %collective-permute-done.15 = bf16[24,4096]{1,0:T(8,128)(2,1)S(1)} collective-permute-done((bf16[24,4096]{1,0:T(8,128)(2,1)S(1)}, bf16[24,4096]{1,0:T(8,128)(2,1)S(1)}, u32[]{:S(2)}, u32[]{:S(2)}) %collective-permute-start.15) | collective-permute-done | bytes 196640 | tf_op jit(solution)/shard_map/ppermute | solution.py:50
  308.9 1.5 collective-permute-start.18
  310.5 4.1 collective-permute-done.18
  314.6 1.4 collective-permute-done.19
  319.0 3.7 collective-permute-start.22
  323.0 2.4 collective-permute-done.20
  325.3 1.2 collective-permute-done.21
  327.3 12.7 %backward_first.1 = (bf16[864,4096]{1,0:T(8,128)(2,1)}, bf16[864,512]{1,0:T(8,128)(2,1)S(1)}) custom-call(s32[42]{0:T(128)S(1)} %get-tuple-element.27.plan_ref, bf16[864,4096]{1,0:T(8,128)(2,1)} %get-tuple-element.11.slope_ref, f32[12,4096]{1,0:T(8,128)S(1)} %convolution_divide_fusion.1.pass_ref, f32[12,4096]{1,0:T(8,128)S(1)} %convolution_divide_fusion.query_ref, ...), custom_call_target="tpu_custom_call" | custom-call | flops 3623878656 | bytes 19234816 | tf_op jit(solution)/shard_map/backward_first/pallas_call | solution.py:296
  340.0 8.4 %backward_part.11 = bf16[864,512]{1,0:T(8,128)(2,1)S(1)} custom-call(s32[42]{0:T(128)S(1)} %get-tuple-element.27.plan_ref, bf16[864,4096]{1,0:T(8,128)(2,1)} %get-tuple-element.14.slopes_ref, bf16[512,4096]{1,0:T(8,128)(2,1)} %refs_0_.15, bf16[512,4096]{1,0:T(8,128)(2,1)} %collective-permute-done.9.refs_6_.refs_8_.refs_1_, ...), custom_call_target="tpu_custom_call" | custom-call | flops 3623878656 | bytes 12156928 | tf_op jit(solution)/shard_map/backward_part/pallas_call | solution.py:371
  349.2 2.4 collective-permute-start.30
  352.3 1.5 collective-permute-start.24
  353.9 17.7 %collective-permute-done.30.refs_9_ = bf16[864,512]{1,0:T(8,128)(2,1)S(1)} collective-permute-done((bf16[864,512]{1,0:T(8,128)(2,1)S(1)}, bf16[864,512]{1,0:T(8,128)(2,1)S(1)}, u32[]{:S(2)}, u32[]{:S(2)}) %collective-permute-start.30) | collective-permute-done | bytes 884768 | tf_op jit(solution)/shard_map/ppermute | solution.py:406
  371.6 7.9 %backward_part.12 = bf16[864,512]{1,0:T(8,128)(2,1)S(1)} custom-call(s32[42]{0:T(128)S(1)} %get-tuple-element.27.plan_ref, bf16[864,4096]{1,0:T(8,128)(2,1)} %get-tuple-element.14.slopes_ref, bf16[512,4096]{1,0:T(8,128)(2,1)} %refs_0_.15, bf16[512,4096]{1,0:T(8,128)(2,1)} %collective-permute-done.9.refs_6_.refs_8_.refs_1_, ...), custom_call_target="tpu_custom_call" | custom-call | flops 3623878656 | bytes 12156928 | tf_op jit(solution)/shard_map/backward_part/pallas_call | solution.py:371
  380.2 5.7 %collective-permute-start.32 = (bf16[864,512]{1,0:T(8,128)(2,1)S(1)}, bf16[864,512]{1,0:T(8,128)(2,1)S(1)}, u32[]{:S(2)}, u32[]{:S(2)}) collective-permute-start(bf16[864,512]{1,0:T(8,128)(2,1)S(1)} %backward_part.12), channel_id=1, source_target_pairs={{0,8},{8,16},{1,9},{9,17},{2,10},{10,18},{3,11},{11,19},{4,12},{12... | collective-permute-start | bytes 2654216 | tf_op jit(solution)/shard_map/ppermute | solution.py:406
  385.9 4.6 collective-permute-done.24.refs_9_
  390.5 7.9 %backward_part.8 = bf16[864,512]{1,0:T(8,128)(2,1)S(1)} custom-call(s32[42]{0:T(128)S(1)} %get-tuple-element.27.plan_ref, bf16[864,4096]{1,0:T(8,128)(2,1)} %get-tuple-element.14.slopes_ref, bf16[512,4096]{1,0:T(8,128)(2,1)} %refs_0_.15, bf16[512,4096]{1,0:T(8,128)(2,1)} %collective-permute-done.9.refs_6_.refs_8_.refs_1_, ...), custom_call_target="tpu_custom_call" | custom-call | flops 3623878656 | bytes 12156928 | tf_op jit(solution)/shard_map/backward_part/pallas_call | solution.py:371
  399.1 5.0 %collective-permute-start.26 = (bf16[864,512]{1,0:T(8,128)(2,1)S(1)}, bf16[864,512]{1,0:T(8,128)(2,1)S(1)}, u32[]{:S(2)}, u32[]{:S(2)}) collective-permute-start(bf16[864,512]{1,0:T(8,128)(2,1)S(1)} %backward_part.8), channel_id=1, source_target_pairs={{0,8},{8,16},{1,9},{9,17},{2,10},{10,18},{3,11},{11,19},{4,12},{12... | collective-permute-start | bytes 2654216 | tf_op jit(solution)/shard_map/ppermute | solution.py:406
  404.1 5.3 %collective-permute-done.32.refs_9_ = bf16[864,512]{1,0:T(8,128)(2,1)S(1)} collective-permute-done((bf16[864,512]{1,0:T(8,128)(2,1)S(1)}, bf16[864,512]{1,0:T(8,128)(2,1)S(1)}, u32[]{:S(2)}, u32[]{:S(2)}) %collective-permute-start.32) | collective-permute-done | bytes 884768 | tf_op jit(solution)/shard_map/ppermute | solution.py:406
  409.5 12.5 %backward_part.13 = (bf16[864,512]{1,0:T(8,128)(2,1)S(1)}, bf16[864,512]{1,0:T(8,128)(2,1)S(1)}) custom-call(s32[42]{0:T(128)S(1)} %get-tuple-element.27.plan_ref, bf16[864,4096]{1,0:T(8,128)(2,1)} %get-tuple-element.14.slopes_ref, bf16[512,4096]{1,0:T(8,128)(2,1)} %refs_0_.15, bf16[512,4096]{1,0:T(8,128)(2,1)} %collective-permute-done.9.refs_6_.refs_8_.refs_1_, ...), custom_call_target="tpu_custom_call" | custom-call | flops 7247757312 | bytes 17235968 | tf_op jit(solution)/shard_map/backward_part/pallas_call | solution.py:371
  421.9 1.3 collective-permute-start.33
  423.2 5.1 %collective-permute-start.34 = (bf16[864,512]{1,0:T(8,128)(2,1)S(1)}, bf16[864,512]{1,0:T(8,128)(2,1)S(1)}, u32[]{:S(2)}, u32[]{:S(2)}) collective-permute-start(bf16[864,512]{1,0:T(8,128)(2,1)S(1)} %get-tuple-element.19), channel_id=1, source_target_pairs={{0,8},{8,16},{16,24},{1,9},{9,17},{17,25},{2,10},{10,18},{18,26},{... | collective-permute-start | bytes 2654216 | tf_op jit(solution)/shard_map/ppermute | solution.py:406
  428.4 12.5 %backward_part.9 = (bf16[864,512]{1,0:T(8,128)(2,1)S(1)}, bf16[864,512]{1,0:T(8,128)(2,1)S(1)}) custom-call(s32[42]{0:T(128)S(1)} %get-tuple-element.27.plan_ref, bf16[864,4096]{1,0:T(8,128)(2,1)} %get-tuple-element.14.slopes_ref, bf16[512,4096]{1,0:T(8,128)(2,1)} %refs_0_.15, bf16[512,4096]{1,0:T(8,128)(2,1)} %collective-permute-done.9.refs_6_.refs_8_.refs_1_, ...), custom_call_target="tpu_custom_call" | custom-call | flops 7247757312 | bytes 17235968 | tf_op jit(solution)/shard_map/backward_part/pallas_call | solution.py:371
  440.9 1.3 collective-permute-start.27
  442.2 5.1 %collective-permute-start.28 = (bf16[864,512]{1,0:T(8,128)(2,1)S(1)}, bf16[864,512]{1,0:T(8,128)(2,1)S(1)}, u32[]{:S(2)}, u32[]{:S(2)}) collective-permute-start(bf16[864,512]{1,0:T(8,128)(2,1)S(1)} %get-tuple-element.17), channel_id=1, source_target_pairs={{0,8},{8,16},{16,24},{1,9},{9,17},{17,25},{2,10},{10,18},{18,26},{... | collective-permute-start | bytes 2654216 | tf_op jit(solution)/shard_map/ppermute | solution.py:406
  447.3 7.7 %backward_part.10 = bf16[864,512]{1,0:T(8,128)(2,1)S(1)} custom-call(s32[42]{0:T(128)S(1)} %get-tuple-element.27.plan_ref, bf16[864,4096]{1,0:T(8,128)(2,1)} %get-tuple-element.14.slopes_ref, bf16[512,4096]{1,0:T(8,128)(2,1)} %refs_0_.15, bf16[512,4096]{1,0:T(8,128)(2,1)} %collective-permute-done.9.refs_6_.refs_8_.refs_1_, ...), custom_call_target="tpu_custom_call" | custom-call | flops 3623878656 | bytes 12156928 | tf_op jit(solution)/shard_map/backward_part/pallas_call | solution.py:371
  455.0 7.7 %backward_part.7 = bf16[864,512]{1,0:T(8,128)(2,1)S(1)} custom-call(s32[42]{0:T(128)S(1)} %get-tuple-element.27.plan_ref, bf16[864,4096]{1,0:T(8,128)(2,1)} %get-tuple-element.14.slopes_ref, bf16[512,4096]{1,0:T(8,128)(2,1)} %refs_0_.15, bf16[512,4096]{1,0:T(8,128)(2,1)} %collective-permute-done.9.refs_6_.refs_8_.refs_1_, ...), custom_call_target="tpu_custom_call" | custom-call | flops 3623878656 | bytes 12156928 | tf_op jit(solution)/shard_map/backward_part/pallas_call | solution.py:371
  463.1 1.9 collective-permute-done.28
  466.2 1.4 fusion
  (88 shorter events, 16.8 us)
Async XLA Ops:
  0.6 94.3 %collective-permute-start.6 = (bf16[512,4096]{1,0:T(8,128)(2,1)}, bf16[512,4096]{1,0:T(8,128)(2,1)}, u32[]{:S(2)}, u32[]{:S(2)}) collective-permute-start(bf16[512,4096]{1,0:T(8,128)(2,1)} %refs_0_.15), channel_id=1, source_target_pairs={{0,4},{1,3},{2,6},{3,1},{4,0},{5,7},{6,2},{7,5},{8,12},{9,11},{10,... | collective-permute-start | bytes 12582920 | tf_op jit(solution)/shard_map/ppermute | solution.py:50
  3.7 134.0 %collective-permute-start.10 = (bf16[512,4096]{1,0:T(8,128)(2,1)}, bf16[512,4096]{1,0:T(8,128)(2,1)}, u32[]{:S(2)}, u32[]{:S(2)}) collective-permute-start(bf16[512,4096]{1,0:T(8,128)(2,1)} %refs_0_.15), channel_id=1, source_target_pairs={{0,2},{1,5},{2,0},{3,7},{4,6},{5,1},{6,4},{7,3},{8,10},{9,13},{10,... | collective-permute-start | bytes 12582920 | tf_op jit(solution)/shard_map/ppermute | solution.py:50
  94.9 49.3 %collective-permute-start.7 = (bf16[512,4096]{1,0:T(8,128)(2,1)}, bf16[512,4096]{1,0:T(8,128)(2,1)}, u32[]{:S(2)}, u32[]{:S(2)}) collective-permute-start(bf16[512,4096]{1,0:T(8,128)(2,1)} %collective-permute-done.6.refs_9_.refs_11_.refs_4_), channel_id=1, source_target_pairs={{0,2},{1,5},{2,0},{3,7},{4,6},{5,1},{6,4},{7,3},{8,10},{9,13},{10,... | collective-permute-start | bytes 12582920 | tf_op jit(solution)/shard_map/ppermute | solution.py:50
  96.4 47.9 %copy-start.5 = (s32[12,8]{0,1:T(8,128)S(1)}, s32[12,8]{0,1:T(8,128)}, u32[]{:S(2)}) copy-start(s32[12,8]{0,1:T(8,128)} %param.10) | copy-start | bytes 1156
  96.4 51.2 %copy-start.6 = (s32[12]{0:T(128)S(1)}, s32[12]{0:T(128)}, u32[]{:S(2)}) copy-start(s32[12]{0:T(128)} %param.11) | copy-start | bytes 148
  98.1 44.7 %copy-start.2 = (bf16[864,1024]{1,0:T(8,128)(2,1)}, bf16[864,1024]{1,0:T(8,128)(2,1)S(1)}, u32[]{:S(2)}) copy-start(bf16[864,1024]{1,0:T(8,128)(2,1)S(1)} %pad_maximum_fusion.refs_2_.refs_3_) | copy-start | bytes 5308420
  98.1 39.6 %collective-permute-start = (bf16[864,1024]{1,0:T(8,128)(2,1)S(1)}, bf16[864,1024]{1,0:T(8,128)(2,1)S(1)}, u32[]{:S(2)}, u32[]{:S(2)}) collective-permute-start(bf16[864,1024]{1,0:T(8,128)(2,1)S(1)} %pad_maximum_fusion.refs_2_.refs_3_), channel_id=1, source_target_pairs={{0,8},{8,16},{16,24},{1,9},{9,17},{17,25},{2,10},{10,18},{18,26},{... | collective-permute-start | bytes 5308424 | tf_op jit(solution)/shard_map/ppermute | solution.py:30
  101.8 40.2 %collective-permute-start.3 = (bf16[864,1024]{1,0:T(8,128)(2,1)S(1)}, bf16[864,1024]{1,0:T(8,128)(2,1)}, u32[]{:S(2)}, u32[]{:S(2)}) collective-permute-start(bf16[864,1024]{1,0:T(8,128)(2,1)S(1)} %pad_maximum_fusion.refs_2_.refs_3_), channel_id=1, source_target_pairs={{8,0},{16,8},{24,16},{9,1},{17,9},{25,17},{10,2},{18,10},{26,18},{... | collective-permute-start | bytes 5308424 | tf_op jit(solution)/shard_map/ppermute | solution.py:29
  103.2 118.4 %collective-permute-start.9 = (bf16[512,4096]{1,0:T(8,128)(2,1)}, bf16[512,4096]{1,0:T(8,128)(2,1)}, u32[]{:S(2)}, u32[]{:S(2)}) collective-permute-start(bf16[512,4096]{1,0:T(8,128)(2,1)} %refs_0_.15), channel_id=1, source_target_pairs={{0,1},{1,0},{2,3},{3,2},{4,5},{5,4},{6,7},{7,6},{8,9},{9,8},{10,11... | collective-permute-start | bytes 12582920 | tf_op jit(solution)/shard_map/ppermute | solution.py:50
  137.7 109.6 %copy-start = (bf16[864,1024]{1,0:T(8,128)(2,1)}, bf16[864,1024]{1,0:T(8,128)(2,1)S(1)}, u32[]{:S(2)}) copy-start(bf16[864,1024]{1,0:T(8,128)(2,1)S(1)} %collective-permute-done.refs_1_.refs_2_) | copy-start | bytes 5308420
  137.7 88.5 %collective-permute-start.11 = (bf16[512,4096]{1,0:T(8,128)(2,1)}, bf16[512,4096]{1,0:T(8,128)(2,1)}, u32[]{:S(2)}, u32[]{:S(2)}) collective-permute-start(bf16[512,4096]{1,0:T(8,128)(2,1)} %collective-permute-done.6.refs_9_.refs_11_.refs_4_), channel_id=1, source_target_pairs={{0,1},{1,0},{2,3},{3,2},{4,5},{5,4},{6,7},{7,6},{8,9},{9,8},{10,11... | collective-permute-start | bytes 12582920 | tf_op jit(solution)/shard_map/ppermute | solution.py:50
  137.7 88.5 %collective-permute-start.12 = (bf16[512,4096]{1,0:T(8,128)(2,1)}, bf16[512,4096]{1,0:T(8,128)(2,1)}, u32[]{:S(2)}, u32[]{:S(2)}) collective-permute-start(bf16[512,4096]{1,0:T(8,128)(2,1)} %collective-permute-done.10.refs_7_.refs_9_.refs_2_), channel_id=1, source_target_pairs={{0,1},{1,0},{2,3},{3,2},{4,5},{5,4},{6,7},{7,6},{8,9},{9,8},{10,11... | collective-permute-start | bytes 12582920 | tf_op jit(solution)/shard_map/ppermute | solution.py:50
  142.0 0.8 collective-permute-start.1
  142.8 118.0 %copy-start.1 = (bf16[864,1024]{1,0:T(8,128)(2,1)}, bf16[864,1024]{1,0:T(8,128)(2,1)S(1)}, u32[]{:S(2)}) copy-start(bf16[864,1024]{1,0:T(8,128)(2,1)S(1)} %collective-permute-done.1.refs_0_.refs_1_) | copy-start | bytes 5308420
  142.8 76.8 %collective-permute-start.4 = (bf16[864,1024]{1,0:T(8,128)(2,1)}, bf16[864,1024]{1,0:T(8,128)(2,1)}, u32[]{:S(2)}, u32[]{:S(2)}) collective-permute-start(bf16[864,1024]{1,0:T(8,128)(2,1)} %collective-permute-done.3.refs_3_.refs_4_), channel_id=1, source_target_pairs={{8,0},{16,8},{9,1},{17,9},{10,2},{18,10},{11,3},{19,11},{12,4},{20... | collective-permute-start | bytes 5308424 | tf_op jit(solution)/shard_map/ppermute | solution.py:29
  144.2 136.4 %collective-permute-start.8 = (bf16[512,4096]{1,0:T(8,128)(2,1)}, bf16[512,4096]{1,0:T(8,128)(2,1)}, u32[]{:S(2)}, u32[]{:S(2)}) collective-permute-start(bf16[512,4096]{1,0:T(8,128)(2,1)} %collective-permute-done.7.refs_7_.refs_6_), channel_id=1, source_target_pairs={{0,1},{1,0},{2,3},{3,2},{4,5},{5,4},{6,7},{7,6},{8,9},{9,8},{10,11... | collective-permute-start | bytes 12582920 | tf_op jit(solution)/shard_map/ppermute | solution.py:50
  219.7 27.7 %collective-permute-start.2 = (bf16[864,1024]{1,0:T(8,128)(2,1)S(1)}, bf16[864,1024]{1,0:T(8,128)(2,1)}, u32[]{:S(2)}, u32[]{:S(2)}) collective-permute-start(bf16[864,1024]{1,0:T(8,128)(2,1)S(1)} %collective-permute-done.1.refs_0_.refs_1_), channel_id=1, source_target_pairs={{16,24},{17,25},{18,26},{19,27},{20,28},{21,29},{22,30},{23,31}} | collective-permute-start | bytes 5308424 | tf_op jit(solution)/shard_map/ppermute | solution.py:30
  221.6 39.2 %collective-permute-start.5 = (bf16[864,1024]{1,0:T(8,128)(2,1)}, bf16[864,1024]{1,0:T(8,128)(2,1)}, u32[]{:S(2)}, u32[]{:S(2)}) collective-permute-start(bf16[864,1024]{1,0:T(8,128)(2,1)} %collective-permute-done.4.refs_4_.refs_5_), channel_id=1, source_target_pairs={{8,0},{9,1},{10,2},{11,3},{12,4},{13,5},{14,6},{15,7}} | collective-permute-start | bytes 5308424 | tf_op jit(solution)/shard_map/ppermute | solution.py:29
  301.5 8.9 %collective-permute-start.13 = (bf16[24,4096]{1,0:T(8,128)(2,1)S(1)}, bf16[24,4096]{1,0:T(8,128)(2,1)S(1)}, u32[]{:S(2)}, u32[]{:S(2)}) collective-permute-start(bf16[24,4096]{1,0:T(8,128)(2,1)S(1)} %get-tuple-element.12), channel_id=1, source_target_pairs={{0,1},{1,0},{2,3},{3,2},{4,5},{5,4},{6,7},{7,6},{8,9},{9,8},{10,11... | collective-permute-start | bytes 589832 | tf_op jit(solution)/shard_map/ppermute | solution.py:50
  301.6 8.8 %collective-permute-start.14 = (bf16[24,4096]{1,0:T(8,128)(2,1)S(1)}, bf16[24,4096]{1,0:T(8,128)(2,1)S(1)}, u32[]{:S(2)}, u32[]{:S(2)}) collective-permute-start(bf16[24,4096]{1,0:T(8,128)(2,1)S(1)} %get-tuple-element.12), channel_id=1, source_target_pairs={{0,2},{1,5},{2,0},{3,7},{4,6},{5,1},{6,4},{7,3},{8,10},{9,13},{10,... | collective-permute-start | bytes 589832 | tf_op jit(solution)/shard_map/ppermute | solution.py:50
  303.2 5.7 %collective-permute-start.15 = (bf16[24,4096]{1,0:T(8,128)(2,1)S(1)}, bf16[24,4096]{1,0:T(8,128)(2,1)S(1)}, u32[]{:S(2)}, u32[]{:S(2)}) collective-permute-start(bf16[24,4096]{1,0:T(8,128)(2,1)S(1)} %get-tuple-element.12), channel_id=1, source_target_pairs={{0,4},{1,3},{2,6},{3,1},{4,0},{5,7},{6,2},{7,5},{8,12},{9,11},{10,... | collective-permute-start | bytes 589832 | tf_op jit(solution)/shard_map/ppermute | solution.py:50
  308.9 1.6 collective-permute-start.16
  308.9 5.7 %collective-permute-start.18 = (bf16[24,4096]{1,0:T(8,128)(2,1)S(1)}, bf16[24,4096]{1,0:T(8,128)(2,1)S(1)}, u32[]{:S(2)}, u32[]{:S(2)}) collective-permute-start(bf16[24,4096]{1,0:T(8,128)(2,1)S(1)} %collective-permute-done.15), channel_id=1, source_target_pairs={{0,2},{1,5},{2,0},{3,7},{4,6},{5,1},{6,4},{7,3},{8,10},{9,13},{10,... | collective-permute-start | bytes 589832 | tf_op jit(solution)/shard_map/ppermute | solution.py:50
  310.4 4.2 collective-permute-start.17
  314.6 1.4 collective-permute-start.19
  317.4 1.1 copy-start.3
  317.4 9.1 %copy-start.4 = (s32[96]{0:T(128)S(1)}, s32[96]{0:T(128)}, u32[]{:S(2)}) copy-start(s32[96]{0:T(128)} %eq.15) | copy-start | bytes 1156
  318.9 6.5 %collective-permute-start.20 = (f32[96,96]{0,1:T(8,128)S(1)}, f32[96,96]{0,1:T(8,128)S(1)}, u32[]{:S(2)}, u32[]{:S(2)}) collective-permute-start(f32[96,96]{0,1:T(8,128)S(1)} %fusion.15), channel_id=1, source_target_pairs={{0,8},{8,16},{16,24},{24,0},{1,9},{9,17},{17,25},{25,1},{2,10},{10... | collective-permute-start | bytes 110600 | tf_op jit(solution)/shard_map/ppermute | solution.py:463
  318.9 7.6 %collective-permute-start.21 = (f32[96,96]{0,1:T(8,128)S(1)}, f32[96,96]{0,1:T(8,128)S(1)}, u32[]{:S(2)}, u32[]{:S(2)}) collective-permute-start(f32[96,96]{0,1:T(8,128)S(1)} %fusion.15), channel_id=1, source_target_pairs={{0,16},{8,24},{16,0},{24,8},{1,17},{9,25},{17,1},{25,9},{2,18},{10... | collective-permute-start | bytes 110600 | tf_op jit(solution)/shard_map/ppermute | solution.py:463
  319.0 7.5 %collective-permute-start.22 = (f32[96,96]{0,1:T(8,128)S(1)}, f32[96,96]{0,1:T(8,128)S(1)}, u32[]{:S(2)}, u32[]{:S(2)}) collective-permute-start(f32[96,96]{0,1:T(8,128)S(1)} %fusion.15), channel_id=1, source_target_pairs={{0,24},{8,0},{16,8},{24,16},{1,25},{9,1},{17,9},{25,17},{2,26},{10... | collective-permute-start | bytes 110600 | tf_op jit(solution)/shard_map/ppermute | solution.py:463
  348.5 5.4 %collective-permute-start.29 = (bf16[864,512]{1,0:T(8,128)(2,1)S(1)}, bf16[864,512]{1,0:T(8,128)(2,1)S(1)}, u32[]{:S(2)}, u32[]{:S(2)}) collective-permute-start(bf16[864,512]{1,0:T(8,128)(2,1)S(1)} %backward_part.11), channel_id=1, source_target_pairs={{24,16},{25,17},{26,18},{27,19},{28,20},{29,21},{30,22},{31,23}} | collective-permute-start | bytes 2654216 | tf_op jit(solution)/shard_map/ppermute | solution.py:405
  349.2 22.4 %collective-permute-start.30 = (bf16[864,512]{1,0:T(8,128)(2,1)S(1)}, bf16[864,512]{1,0:T(8,128)(2,1)S(1)}, u32[]{:S(2)}, u32[]{:S(2)}) collective-permute-start(bf16[864,512]{1,0:T(8,128)(2,1)S(1)} %backward_part.11), channel_id=1, source_target_pairs={{0,8},{1,9},{2,10},{3,11},{4,12},{5,13},{6,14},{7,15}} | collective-permute-start | bytes 2654216 | tf_op jit(solution)/shard_map/ppermute | solution.py:406
  351.6 34.3 %collective-permute-start.23 = (bf16[864,512]{1,0:T(8,128)(2,1)S(1)}, bf16[864,512]{1,0:T(8,128)(2,1)S(1)}, u32[]{:S(2)}, u32[]{:S(2)}) collective-permute-start(bf16[864,512]{1,0:T(8,128)(2,1)S(1)} %get-tuple-element.15), channel_id=1, source_target_pairs={{24,16},{25,17},{26,18},{27,19},{28,20},{29,21},{30,22},{31,23}} | collective-permute-start | bytes 2654216 | tf_op jit(solution)/shard_map/ppermute | solution.py:405
  352.3 38.2 %collective-permute-start.24 = (bf16[864,512]{1,0:T(8,128)(2,1)S(1)}, bf16[864,512]{1,0:T(8,128)(2,1)S(1)}, u32[]{:S(2)}, u32[]{:S(2)}) collective-permute-start(bf16[864,512]{1,0:T(8,128)(2,1)S(1)} %get-tuple-element.15), channel_id=1, source_target_pairs={{0,8},{1,9},{2,10},{3,11},{4,12},{5,13},{6,14},{7,15}} | collective-permute-start | bytes 2654216 | tf_op jit(solution)/shard_map/ppermute | solution.py:406
  379.4 24.7 %collective-permute-start.31 = (bf16[864,512]{1,0:T(8,128)(2,1)S(1)}, bf16[864,512]{1,0:T(8,128)(2,1)S(1)}, u32[]{:S(2)}, u32[]{:S(2)}) collective-permute-start(bf16[864,512]{1,0:T(8,128)(2,1)S(1)} %backward_part.12), channel_id=1, source_target_pairs={{16,8},{24,16},{17,9},{25,17},{18,10},{26,18},{19,11},{27,19},{20,... | collective-permute-start | bytes 2654216 | tf_op jit(solution)/shard_map/ppermute | solution.py:405
  380.2 29.3 %collective-permute-start.32 = (bf16[864,512]{1,0:T(8,128)(2,1)S(1)}, bf16[864,512]{1,0:T(8,128)(2,1)S(1)}, u32[]{:S(2)}, u32[]{:S(2)}) collective-permute-start(bf16[864,512]{1,0:T(8,128)(2,1)S(1)} %backward_part.12), channel_id=1, source_target_pairs={{0,8},{8,16},{1,9},{9,17},{2,10},{10,18},{3,11},{11,19},{4,12},{12... | collective-permute-start | bytes 2654216 | tf_op jit(solution)/shard_map/ppermute | solution.py:406
  398.4 29.9 %collective-permute-start.25 = (bf16[864,512]{1,0:T(8,128)(2,1)S(1)}, bf16[864,512]{1,0:T(8,128)(2,1)S(1)}, u32[]{:S(2)}, u32[]{:S(2)}) collective-permute-start(bf16[864,512]{1,0:T(8,128)(2,1)S(1)} %backward_part.8), channel_id=1, source_target_pairs={{16,8},{24,16},{17,9},{25,17},{18,10},{26,18},{19,11},{27,19},{20,... | collective-permute-start | bytes 2654216 | tf_op jit(solution)/shard_map/ppermute | solution.py:405
  399.1 29.3 %collective-permute-start.26 = (bf16[864,512]{1,0:T(8,128)(2,1)S(1)}, bf16[864,512]{1,0:T(8,128)(2,1)S(1)}, u32[]{:S(2)}, u32[]{:S(2)}) collective-permute-start(bf16[864,512]{1,0:T(8,128)(2,1)S(1)} %backward_part.8), channel_id=1, source_target_pairs={{0,8},{8,16},{1,9},{9,17},{2,10},{10,18},{3,11},{11,19},{4,12},{12... | collective-permute-start | bytes 2654216 | tf_op jit(solution)/shard_map/ppermute | solution.py:406
  421.9 40.8 %collective-permute-start.33 = (bf16[864,512]{1,0:T(8,128)(2,1)S(1)}, bf16[864,512]{1,0:T(8,128)(2,1)S(1)}, u32[]{:S(2)}, u32[]{:S(2)}) collective-permute-start(bf16[864,512]{1,0:T(8,128)(2,1)S(1)} %get-tuple-element.18), channel_id=1, source_target_pairs={{8,0},{16,8},{24,16},{9,1},{17,9},{25,17},{10,2},{18,10},{26,18},{... | collective-permute-start | bytes 2654216 | tf_op jit(solution)/shard_map/ppermute | solution.py:405
  423.2 39.5 %collective-permute-start.34 = (bf16[864,512]{1,0:T(8,128)(2,1)S(1)}, bf16[864,512]{1,0:T(8,128)(2,1)S(1)}, u32[]{:S(2)}, u32[]{:S(2)}) collective-permute-start(bf16[864,512]{1,0:T(8,128)(2,1)S(1)} %get-tuple-element.19), channel_id=1, source_target_pairs={{0,8},{8,16},{16,24},{1,9},{9,17},{17,25},{2,10},{10,18},{18,26},{... | collective-permute-start | bytes 2654216 | tf_op jit(solution)/shard_map/ppermute | solution.py:406
  440.9 22.3 %collective-permute-start.27 = (bf16[864,512]{1,0:T(8,128)(2,1)S(1)}, bf16[864,512]{1,0:T(8,128)(2,1)S(1)}, u32[]{:S(2)}, u32[]{:S(2)}) collective-permute-start(bf16[864,512]{1,0:T(8,128)(2,1)S(1)} %get-tuple-element.16), channel_id=1, source_target_pairs={{8,0},{16,8},{24,16},{9,1},{17,9},{25,17},{10,2},{18,10},{26,18},{... | collective-permute-start | bytes 2654216 | tf_op jit(solution)/shard_map/ppermute | solution.py:405
  442.2 22.9 %collective-permute-start.28 = (bf16[864,512]{1,0:T(8,128)(2,1)S(1)}, bf16[864,512]{1,0:T(8,128)(2,1)S(1)}, u32[]{:S(2)}, u32[]{:S(2)}) collective-permute-start(bf16[864,512]{1,0:T(8,128)(2,1)S(1)} %get-tuple-element.17), channel_id=1, source_target_pairs={{0,8},{8,16},{16,24},{1,9},{9,17},{17,25},{2,10},{10,18},{18,26},{... | collective-permute-start | bytes 2654216 | tf_op jit(solution)/shard_map/ppermute | solution.py:406
where the time goes:
time: 469 us; the launch traced here: 468 us
  waiting for transfers between devices  242 us (52%)
  Pallas kernels  139 us (30%)
  starting transfers between devices  54.5 us (12%)
  blocking collectives  14.3 us (3%)
  local copies, waits for them, and re-layouts  7.81 us (2%)
  other arithmetic  7.53 us (2%)
    ppermute x14, waiting for transfers between devices, move(): return lax.ppermute(value, 'rows', pairs)  101 us
    ppermute x3, waiting for transfers between devices, line_gather(): lax.ppermute(left, 'vocab', [(z, z - 1) for z in range(1, n - step + 1)])  73.4 us
    pallas_call x7, Pallas kernels, backward(): pl.pallas_call(functools.partial(backward_kernel, (at, count, parts, adds...  64.5 us
    pallas_call x3, Pallas kernels, forward(): pl.pallas_call(functools.partial(forward_kernel, spec), out_shape=out_sha...  61.7 us
    ppermute x3, waiting for transfers between devices, line_gather(): lax.ppermute(right, 'vocab', [(z, z + 1) for z in range(step - 1, n - 1)])  34.5 us
    ppermute x6, waiting for transfers between devices, line_reduce_scatter(): lax.ppermute(to_right, 'vocab', [(d, d + 1) for d in range(step)])  29.7 us
    ppermute x6, starting transfers between devices, line_reduce_scatter(): lax.ppermute(to_right, 'vocab', [(d, d + 1) for d in range(step)])  24.8 us
    unnamed x1, blocking collectives  14.3 us
  transfers between devices with their start and end apart: 35, of which 15 were waited for; matrix products, arithmetic and copies ran while one was open for 2% of the time, Pallas kernels for 21%

commit v1 on v0

--- a/solution.py
+++ b/solution.py
@@ -11,6 +11,7 @@
 MARGIN = 1.0
 SHARPNESS = 16.0
 
+VMEM_BYTES = 62 * 1024 * 1024
 CORES = 2
 
 
@@ -76,18 +77,15 @@
                 lists = {}
                 order = row_order(r, n_rows, n_vocab)
                 lists["order"] = order
-                early = n_rows * 3 // 4
+                half = n_rows // 2
+                picks = {"soon": list(range(half)), "last": list(range(half, n_rows))}
                 if two_paths(n_rows, n_vocab):
                     late = [i for i in range(3) if abs(order[2 * i] // share - z) == n_vocab - 1]
                     wait = late[0] if late else 2
-                    rest = [i for i in range(3) if i != wait]
-                    picks = {
-                        "soon": [2 * i + core for i in rest for core in range(2)],
-                        "then": [2 * wait, 2 * wait + 1],
-                    }
-                else:
-                    picks = {"soon": list(range(early))}
-                picks["last"] = list(range(early, n_rows))
+                    rest = [i for i in range(4) if i != wait]
+                    rest = rest[:2] + [wait, rest[2]]
+                    pick = [2 * i + core for i in rest for core in range(2)]
+                    picks = {"soon": pick[:half], "last": pick[half:]}
                 for name, pick in picks.items():
                     lists[name] = (
                         pick
@@ -128,13 +126,13 @@
 
 
 def forward_kernel(spec, plan_ref, *refs):
-    at, skip, count, codes, n_pieces, depth, tile, has_total, final, groups, pass_rows = spec
+    at, count, codes, n_pieces, depth, tile, final, groups, pass_rows, kept = spec
     refs = list(refs)
     sources = [(code, refs.pop(0)) for code in codes]
     pieces = [refs.pop(0) for _ in range(n_pieces)]
-    start_ref = refs.pop(0) if has_total else None
-    mask_ref = refs.pop(0) if final else None
     if final:
+        start_ref, mask_ref = refs.pop(0), refs.pop(0)
+        del refs[:kept]
         slope_ref, total_ref, sparse_ref = [refs.pop(0) for _ in range(3)]
     else:
         out_ref = refs.pop(0)
@@ -144,18 +142,20 @@
     def weight_copy(j, t, which, slot):
         return pltpu.make_async_copy(
             pieces[which].at[:, pl.ds(pl.multiple_of(j * tile, tile), tile)],
-            weights.at[slot, t],
+            weights.at[slot, pl.ds(t * depth, depth)],
             weight_sem.at[slot, t],
         )
 
     def fetch(j, slot):
         for t in range(count):
             for which in range(n_pieces):
-                pl.when(plan_ref[at + t] == which + skip)(weight_copy(j, t, which, slot).start)
+                pl.when(plan_ref[at + t] == which)(weight_copy(j, t, which, slot).start)
 
     def hidden_copy(t, ref):
         return pltpu.make_async_copy(
-            ref.at[:, pl.ds(pl.multiple_of(plan_ref[at + 2 * count + t], 128), depth)], held.at[t], held_sem.at[t]
+            ref.at[:, pl.ds(pl.multiple_of(plan_ref[at + 2 * count + t], 128), depth)],
+            held.at[:, pl.ds(t * depth, depth)],
+            held_sem.at[t],
         )
 
     @pl.when(step == 0)
@@ -178,16 +178,13 @@
 
     for t in range(count):
         weight_copy(step, t, 0, slot).wait()
-    value = start_ref[...] if has_total else None
-    for t in range(count):
-        term = jnp.dot(held[t], weights[slot, t], preferred_element_type=jnp.float32)
-        value = term if value is None else value + term
+    value = jnp.dot(held[...], weights[slot], preferred_element_type=jnp.float32)
     if not final:
         out_ref[...] = value
         return
     mask = mask_ref[...]
     mask = jnp.concatenate([mask] * (tile // mask.shape[1]), axis=1)
-    x = jnp.maximum(value, 0.0) * mask
+    x = jnp.maximum(value + start_ref[...], 0.0) * mask
     totals = []
     for lower, upper in ((0, pass_rows), (pass_rows, x.shape[0])):
         total, slope = pooled(x[lower:upper], groups)
@@ -198,31 +195,33 @@
     sparse_ref[...] = (jnp.sqrt(jnp.sqrt(total + 1.0)) - 1.0).astype(sparse_ref.dtype)
 
 
-def forward(found, pieces, plan, at, count, skip=0, start=None, mask=None, groups=0, pass_rows=0, tile=512):
+def forward(found, pieces, plan, at, count, tile=512, pool=None):
     rows = found[0].shape[0]
     depth, width = pieces[0].shape
     keys = sorted(found)
-    final = mask is not None
     anywhere = pl.BlockSpec(memory_space=pl.ANY)
-    column = lambda height: pl.BlockSpec((height, tile), lambda j, *_: (0, j))
     operands = [found[key] for key in keys] + list(pieces)
     in_specs = [anywhere] * len(operands)
-    if start is not None:
-        operands.append(start)
-        in_specs.append(column(rows))
-    if final:
-        operands.append(mask)
+    groups = pass_rows = 0
+    filled = ()
+    if pool is not None:
+        start, mask, groups, pass_rows, whole, first, filled = pool
+        skip = first // tile
+        column = lambda height: pl.BlockSpec((height, tile), lambda j, *_: (0, j + skip))
+        operands += [start, mask]
+        in_specs.append(pl.BlockSpec((rows, tile), lambda j, *_: (0, j)))
         in_specs.append(pl.BlockSpec(mask.shape, lambda j, *_: (0, 0)))
+        in_specs += [anywhere] * len(filled)
         out_shape = [
-            jax.ShapeDtypeStruct((rows, width), jnp.bfloat16),
-            jax.ShapeDtypeStruct((2 * groups, width), jnp.float32),
-            jax.ShapeDtypeStruct((2 * groups, width), jnp.bfloat16),
+            jax.ShapeDtypeStruct((rows, whole), jnp.bfloat16),
+            jax.ShapeDtypeStruct((2 * groups, whole), jnp.float32),
+            jax.ShapeDtypeStruct((2 * groups, whole), jnp.bfloat16),
         ]
         out_specs = [column(rows), column(2 * groups), column(2 * groups)]
     else:
         out_shape = jax.ShapeDtypeStruct((rows, width), jnp.float32)
-        out_specs = column(rows)
-    spec = (at, skip, count, tuple(keys), len(pieces), depth, tile, start is not None, final, groups, pass_rows)
+        out_specs = pl.BlockSpec((rows, tile), lambda j, *_: (0, j))
+    spec = (at, count, tuple(keys), len(pieces), depth, tile, pool is not None, groups, pass_rows, len(filled))
     return pl.pallas_call(
         functools.partial(forward_kernel, spec),
         out_shape=out_shape,
@@ -232,33 +231,48 @@
             in_specs=in_specs,
             out_specs=out_specs,
             scratch_shapes=[
-                pltpu.VMEM((count, rows, depth), jnp.bfloat16),
-                pltpu.VMEM((2, count, depth, tile), jnp.bfloat16),
+                pltpu.VMEM((rows, count * depth), jnp.bfloat16),
+                pltpu.VMEM((2, count * depth, tile), jnp.bfloat16),
                 pltpu.SemaphoreType.DMA((count,)),
                 pltpu.SemaphoreType.DMA((2, count)),
             ],
         ),
+        input_output_aliases={1 + len(operands) + i: i for i in range(len(filled))},
         compiler_params=pltpu.CompilerParams(
-            dimension_semantics=("arbitrary",), vmem_limit_bytes=50 * 1024 * 1024
+            dimension_semantics=("arbitrary",), vmem_limit_bytes=VMEM_BYTES
         ),
         cost_estimate=pl.CostEstimate(
             flops=2 * rows * depth * count * width,
             bytes_accessed=count * depth * width * 2 + rows * width * 8,
-            transcendentals=rows * width if final else 0,
-        ),
-        name="forward_final" if final else "forward_part",
-    )(plan, *operands)
+            transcendentals=rows * width if pool is not None else 0,
+        ),
+        name="forward_part" if pool is None else "forward_final",
+    )(plan, *operands, *filled)
+
+
+def spans(parts):
+    found, lower = [], 0
+    for part in parts:
+        found.append((lower, part[0].shape[1]))
+        lower += part[0].shape[1]
+    return found
 
 
 def first_kernel(spec, plan_ref, slope_ref, pass_ref, query_ref, *refs):
-    at, count, groups, pass_length, query_length = spec
-    pieces, (grad_ref, out_ref, held, total, sem) = refs[:count], refs[count:]
+    at, count, ranges, groups, pass_length, query_length, keep = spec
+    parts = [refs[i * count : (i + 1) * count] for i in range(len(ranges))]
+    refs = refs[count * len(ranges) :]
+    (grad_ref, out_ref) = refs[:2] if keep else (refs[1], refs[0])
+    held, total, sem = refs[2:]
     step = pl.program_id(0)
     tile = slope_ref.shape[1]
     steps = held.shape[0]
 
     def copy(j, which):
-        return pltpu.make_async_copy(pieces[which].at[:, pl.ds(j * tile, tile)], held.at[j], sem.at[j])
+        i = [i for i, (lower, width) in enumerate(ranges) if lower <= j * tile < lower + width][0]
+        return pltpu.make_async_copy(
+            parts[i][which].at[:, pl.ds(j * tile - ranges[i][0], tile)], held.at[j], sem.at[j]
+        )
 
     @pl.when(step == 0)
     def _():
@@ -277,7 +291,7 @@
             rows = pl.ds(lower, length)
             grad_ref[rows, :] = (slope_ref[rows, :].astype(jnp.float32) * factor_ref[p : p + 1, :]).astype(grad_ref.dtype)
             lower += length
-    pltpu.make_async_copy(pieces[0].at[:, pl.ds(0, tile)], held.at[step], sem.at[step]).wait()
+    pltpu.make_async_copy(parts[0][0].at[:, pl.ds(0, tile)], held.at[step], sem.at[step]).wait()
     total[...] += lax.dot_general(
         grad_ref[...], held[step], (((1,), (1,)), ((), ())), preferred_element_type=jnp.float32
     )
@@ -287,32 +301,37 @@
         out_ref[...] = total[...].astype(out_ref.dtype)
 
 
-def backward_first(slopes, factor_pass, factor_query, lengths, pieces, plan, at, tile=512):
+def backward_first(slopes, factor_pass, factor_query, lengths, parts, plan, at, keep, tile=1024):
     rows, width = slopes.shape
     groups = factor_pass.shape[0]
-    depth = pieces[0].shape[0]
-    count = len(pieces)
+    depth = parts[0][0].shape[0]
+    count = len(parts[0])
+    pieces = [piece for part in parts for piece in part]
     column = lambda height: pl.BlockSpec((height, tile), lambda j, *_: (0, j))
+    out_shape = [jax.ShapeDtypeStruct((rows, depth), jnp.bfloat16)]
+    out_specs = [pl.BlockSpec((rows, depth), lambda j, *_: (0, 0))]
+    scratch = [] if keep else [pltpu.VMEM((rows, tile), jnp.bfloat16)]
+    if keep:
+        out_shape.insert(0, jax.ShapeDtypeStruct((rows, width), jnp.bfloat16))
+        out_specs.insert(0, column(rows))
     return pl.pallas_call(
-        functools.partial(first_kernel, (at, count, groups) + lengths),
-        out_shape=[
-            jax.ShapeDtypeStruct((rows, width), jnp.bfloat16),
-            jax.ShapeDtypeStruct((rows, depth), jnp.bfloat16),
-        ],
+        functools.partial(first_kernel, (at, count, spans(parts), groups) + lengths + (keep,)),
+        out_shape=out_shape,
         grid_spec=pltpu.PrefetchScalarGridSpec(
             num_scalar_prefetch=1,
             grid=(width // tile,),
             in_specs=[column(rows), column(groups), column(groups)]
-            + [pl.BlockSpec(memory_space=pl.ANY)] * count,
-            out_specs=[column(rows), pl.BlockSpec((rows, depth), lambda j, *_: (0, 0))],
-            scratch_shapes=[
+            + [pl.BlockSpec(memory_space=pl.ANY)] * len(pieces),
+            out_specs=out_specs,
+            scratch_shapes=scratch
+            + [
                 pltpu.VMEM((width // tile, depth, tile), jnp.bfloat16),
                 pltpu.VMEM((rows, depth), jnp.float32),
                 pltpu.SemaphoreType.DMA((width // tile,)),
             ],
         ),
         compiler_params=pltpu.CompilerParams(
-            dimension_semantics=("arbitrary",), vmem_limit_bytes=50 * 1024 * 1024
+            dimension_semantics=("arbitrary",), vmem_limit_bytes=VMEM_BYTES
         ),
         cost_estimate=pl.CostEstimate(
             flops=2 * rows * depth * width,
@@ -324,10 +343,11 @@
 
 
 def backward_kernel(spec, plan_ref, slopes_ref, *refs):
-    at_plan, count, parts, adds = spec
+    at_plan, count, ranges, parts, adds = spec
     units = len(adds)
     n_adds = max([0] + [i + 1 for unit in adds for i in unit])
-    pieces, refs = refs[:count], refs[count:]
+    groups = [refs[i * count : (i + 1) * count] for i in range(len(ranges))]
+    refs = refs[count * len(ranges) :]
     running, refs = refs[:n_adds], refs[n_adds:]
     outs, (held, slopes, piece_sem, slope_sem) = refs[:units], refs[units:]
     rows = slopes_ref.shape[0] // parts
@@ -336,15 +356,22 @@
         at = pl.ds(pl.multiple_of(i * rows, 16), rows)
         return pltpu.make_async_copy(slopes_ref.at[at, :], slopes.at[at, :], slope_sem.at[i])
 
+    def piece_copy(unit, i, which):
+        lower, width = ranges[i]
+        return pltpu.make_async_copy(
+            groups[i][which], held.at[unit, :, pl.ds(lower, width)], piece_sem.at[unit, i]
+        )
+
     for unit in range(units):
-        for which in range(count):
-            copy = pltpu.make_async_copy(pieces[which], held.at[unit], piece_sem.at[unit])
-            pl.when(plan_ref[at_plan + unit] == which)(copy.start)
+        for i in range(len(ranges)):
+            for which in range(count):
+                pl.when(plan_ref[at_plan + unit] == which)(piece_copy(unit, i, which).start)
         if unit == 0:
             for i in range(parts):
                 slope_copy(i).start()
     for unit in range(units):
-        pltpu.make_async_copy(pieces[0], held.at[unit], piece_sem.at[unit]).wait()
+        for i in range(len(ranges)):
+            piece_copy(unit, i, 0).wait()
 
         @pl.loop(0, parts)
         def _(i):
@@ -361,25 +388,26 @@
             outs[unit][at, :] = value.astype(outs[unit].dtype)
 
 
-def backward(slopes, pieces, plan, at, running=(), adds=((),)):
+def backward(slopes, groups, plan, at, running=(), adds=((),)):
     rows, width = slopes.shape
-    depth = pieces[0].shape[0]
-    count, units = len(pieces), len(adds)
+    depth = groups[0][0].shape[0]
+    pieces = [piece for group in groups for piece in group]
+    count, units = len(groups[0]), len(adds)
     parts = 3 if rows % 48 == 0 else 1
     whole = pl.BlockSpec(memory_space=pltpu.VMEM)
     anywhere = pl.BlockSpec(memory_space=pl.ANY)
     return pl.pallas_call(
-        functools.partial(backward_kernel, (at, count, parts, adds)),
+        functools.partial(backward_kernel, (at, count, spans(groups), parts, adds)),
         out_shape=[jax.ShapeDtypeStruct((rows, depth), jnp.bfloat16)] * units,
-        in_specs=[pl.BlockSpec(memory_space=pltpu.SMEM)] + [anywhere] * (1 + count) + [whole] * len(running),
+        in_specs=[pl.BlockSpec(memory_space=pltpu.SMEM)] + [anywhere] * (1 + len(pieces)) + [whole] * len(running),
         out_specs=[whole] * units,
         scratch_shapes=[
             pltpu.VMEM((units, depth, width), jnp.bfloat16),
             pltpu.VMEM((rows, width), jnp.bfloat16),
-            pltpu.SemaphoreType.DMA((units,)),
+            pltpu.SemaphoreType.DMA((units, len(groups))),
             pltpu.SemaphoreType.DMA((parts,)),
         ],
-        compiler_params=pltpu.CompilerParams(vmem_limit_bytes=50 * 1024 * 1024),
+        compiler_params=pltpu.CompilerParams(vmem_limit_bytes=VMEM_BYTES),
         cost_estimate=pl.CostEstimate(
             flops=2 * rows * depth * units * width,
             bytes_accessed=(units * depth * width + rows * width + units * rows * depth) * 2,
@@ -394,8 +422,8 @@
     for step in range(1, n):
         for i in range(share):
             name = f"part{step}_{i}"
-            if step == 1 and i == 0:
-                to_left = to_right = first
+            if step == 1 and i < 2:
+                to_left = to_right = first(name, i)
             elif 2 * step <= n:
                 running = () if step == 1 else (left[i], right[i])
                 (to_left,) = product(name, running, (tuple(range(len(running))),))
@@ -430,30 +458,31 @@
     mask = jnp.concatenate([mask_pass.reshape(-1), mask_query.reshape(-1)]).astype(jnp.float32)
     mask = jnp.broadcast_to(mask[:, None], (mask.shape[0], 128))
     found = line_gather(tokens, n_vocab)
-    pieces = row_gather(head_weight, n_rows, n_vocab)
-    all_labels = lax.all_gather(labels, "rows", axis=0)[order].reshape(-1)
+    halves = 2 if two_paths(n_rows, n_vocab) and width % 2048 == 0 else 1
+    part_width = width // halves
+    parts = []
+    for i in range(halves):
+        own = head_weight
+        if i > 0:
+            own, _ = lax.optimization_barrier((head_weight, tokens))
+        own = own[:, i * part_width : (i + 1) * part_width]
+        parts.append(row_gather(own, n_rows, n_vocab))
+    all_labels = jnp.stack(row_gather(labels, n_rows, n_vocab)).reshape(-1)
     passages = (order[:, None] * groups + jnp.arange(groups, dtype=jnp.int32)[None, :]).reshape(-1)
     onehot = (all_labels[:, None] == passages[None, :]).astype(jnp.float32)
 
-    early = n_rows * 3 // 4
+    half = n_rows // 2
+    near, soon = found, n_rows
     if two_paths(n_rows, n_vocab):
         near = {code: block for code, block in found.items() if abs(code) < n_vocab - 1}
-        logits = forward(near, pieces[:early], plan, plans.at["soon"], 4)
-        logits = forward(found, pieces[:early], plan, plans.at["then"], 2, start=logits)
-    else:
-        logits = forward(found, pieces[:early], plan, plans.at["soon"], early)
-    slopes, totals, sparse = forward(
-        found,
-        pieces[early:],
-        plan,
-        plans.at["last"],
-        n_rows - early,
-        skip=early,
-        start=logits,
-        mask=mask,
-        groups=groups,
-        pass_rows=pass_rows,
-    )
+        soon = n_rows - 2
+    logits, filled = [], ()
+    for i in range(halves):
+        logits.append(forward(near, parts[i][:soon], plan, plans.at["soon"], half))
+    for i in range(halves):
+        pool = (logits[i], mask, groups, pass_rows, width, i * part_width, filled)
+        filled = forward(found, parts[i], plan, plans.at["last"], half, pool=pool)
+    slopes, totals, sparse = filled
     all_sparse = jnp.stack(row_gather(sparse, n_rows, n_vocab))
     all_pass = all_sparse[:, :groups].reshape(-1, width)
     all_query = all_sparse[:, groups:].reshape(-1, width)
@@ -478,18 +507,17 @@
     pass_grad = lax.dot_general(of_pass, all_query, (((0,), (0,)), ((), ())), preferred_element_type=jnp.float32)
     root = jnp.sqrt(jnp.sqrt(totals + 1.0))
     cube = root * root * root
-    logit_grad, first = backward_first(
-        slopes,
-        pass_grad / cube[:groups],
-        query_grad / cube[groups:],
-        (pass_length, query_length),
-        pieces,
-        plan,
-        plans.at["part1_0"],
-    )
+    factors = (pass_grad / cube[:groups], query_grad / cube[groups:], (pass_length, query_length))
+    logit_grad = []
+
+    def first(name, i):
+        keep = i == 1 or share == 1
+        *grad, block = backward_first(slopes, *factors, parts, plan, plans.at[name], keep)
+        logit_grad.extend(grad)
+        return block
 
     def product(name, running, adds):
-        return backward(logit_grad, pieces, plan, plans.at[name], running, adds)
+        return backward(logit_grad[0], parts, plan, plans.at[name], running, adds)
 
     summed = line_reduce_scatter(first, product, n_vocab, share)
     summed = jnp.concatenate(summed, axis=1).astype(jnp.bfloat16)

time: 469 us -> 399 us (0.85)
  waiting for transfers between devices: 242 us -> 155 us
  starting transfers between devices: 54.5 us -> 73.4 us
  blocking collectives: 14.3 us -> 0 us
  Pallas kernels: 139 us -> 150 us
    ppermute x3, waiting for transfers between devices: 73.4 us -> 0.01 us  [line_gather(): lax.ppermute(left, 'vocab', [(z, z - 1) for z in range(1, n - step + 1)])]
    ppermute x14 -> x28, waiting for transfers between devices: 101 us -> 141 us  [move(): return lax.ppermute(value, 'rows', pairs)]
    ppermute x3, waiting for transfers between devices: 34.5 us -> 0.01 us  [line_gather(): lax.ppermute(right, 'vocab', [(z, z + 1) for z in range(step - 1, n - 1)])]
    ppermute x6, waiting for transfers between devices: 29.7 us -> 11.3 us  [line_reduce_scatter(): lax.ppermute(to_right, 'vocab', [(d, d + 1) for d in range(step)])]
    unnamed x1 -> x0, blocking collectives: 14.3 us -> none
    pallas_call x8, Pallas kernels: 77.2 us -> 89.2 us  [the longest x6 67.4 us: backward(): pl.pallas_call(functools.partial(backward_kernel, (at, count, spans(group...]
    ppermute x14 -> x28, starting transfers between devices: 10.1 us -> 21.9 us  [move(): return lax.ppermute(value, 'rows', pairs)]
    pallas_call x3 -> x4, Pallas kernels: 61.7 us -> 60.9 us  [forward(): pl.pallas_call(functools.partial(forward_kernel, spec), out_shape=out_sha...]
  transfers between devices with their start and end apart: 35 -> 49, of which waited for: 15 -> 19; matrix products, arithmetic and copies ran while one was open for 2% -> 2% of each run, Pallas kernels for 21% -> 30%
where the time goes in v1:
time: 399 us; the launch traced here: 398 us
  waiting for transfers between devices  155 us (39%)
  Pallas kernels  150 us (38%)
  starting transfers between devices  73.4 us (18%)
  local copies, waits for them, and re-layouts  8.17 us (2%)
  other arithmetic  7.73 us (2%)
    ppermute x28, waiting for transfers between devices, move(): return lax.ppermute(value, 'rows', pairs)  141 us
    pallas_call x6, Pallas kernels, backward(): pl.pallas_call(functools.partial(backward_kernel, (at, count, spans(group...  67.4 us
    pallas_call x4, Pallas kernels, forward(): pl.pallas_call(functools.partial(forward_kernel, spec), out_shape=out_sha...  60.9 us
    ppermute x6, starting transfers between devices, line_reduce_scatter(): lax.ppermute(to_right, 'vocab', [(d, d + 1) for d in range(step)])  27.7 us
    ppermute x28, starting transfers between devices, move(): return lax.ppermute(value, 'rows', pairs)  21.9 us
    pallas_call x2, Pallas kernels, backward_first(): pl.pallas_call(functools.partial(first_kernel, (at, count, spans(parts),...  21.8 us
    ppermute x6, waiting for transfers between devices, line_reduce_scatter(): lax.ppermute(to_right, 'vocab', [(d, d + 1) for d in range(step)])  11.3 us
    ppermute x3, starting transfers between devices, line_gather(): lax.ppermute(right, 'vocab', [(z, z + 1) for z in range(step - 1, n - 1)])  7.98 us
  transfers between devices with their start and end apart: 49, of which 19 were waited for; matrix products, arithmetic and copies ran while one was open for 2% of the time, Pallas kernels for 30%

profile of v1, /device:TPU:0, one launch (start us, length us, event | category | flops | bytes accessed | tf_op | source)
XLA Modules:
  0.0 398.0 jit_solution(15094814057054363015)
XLA Ops:
  0.6 1.7 pad_maximum_fusion.refs_2_.refs_3_
  2.3 5.3 %collective-permute-start = (bf16[864,1024]{1,0:T(8,128)(2,1)S(1)}, bf16[864,1024]{1,0:T(8,128)(2,1)S(1)}, u32[]{:S(2)}, u32[]{:S(2)}) collective-permute-start(bf16[864,1024]{1,0:T(8,128)(2,1)S(1)} %pad_maximum_fusion.refs_2_.refs_3_), channel_id=1, source_target_pairs={{0,8},{8,16},{16,24},{1,9},{9,17},{17,25},{2,10},{10,18},{18,26},{... | collective-permute-start | bytes 5308424 | tf_op jit(solution)/shard_map/ppermute | solution.py:31
  7.7 1.7 slice.35.refs_5_.refs_7_.refs_0_
  9.4 1.6 collective-permute-start.15
  12.3 1.6 collective-permute-start.14
  14.4 42.6 %collective-permute-done.32 = s32[12]{0:T(128)S(1)} collective-permute-done((s32[12]{0:T(128)S(1)}, s32[12]{0:T(128)S(1)}, u32[]{:S(2)}, u32[]{:S(2)}) %collective-permute-start.32) | collective-permute-done | bytes 80 | tf_op jit(solution)/shard_map/ppermute | solution.py:51
  57.0 2.5 collective-permute-start.31
  59.4 1.5 collective-permute-done.31
  62.1 2.0 collective-permute-start.35
  64.1 1.5 collective-permute-done.35
  69.6 1.6 collective-permute-start.8
  71.2 2.0 collective-permute-start.7
  75.4 41.6 %collective-permute-done.8.refs_9_.refs_11_.refs_12_ = bf16[512,2048]{1,0:T(8,128)(2,1)S(1)} collective-permute-done((bf16[512,2048]{1,0:T(8,128)(2,1)S(1)}, bf16[512,2048]{1,0:T(8,128)(2,1)S(1)}, u32[]{:S(2)}, u32[]{:S(2)}) %collective-permute-start.8) | collective-permute-done | bytes 2097184 | tf_op jit(solution)/shard_map/ppermute | solution.py:51
  118.0 1.8 collective-permute-start.18
  121.8 22.3 %collective-permute-done.18.refs_13_.refs_6_ = bf16[512,2048]{1,0:T(8,128)(2,1)} collective-permute-done((bf16[512,2048]{1,0:T(8,128)(2,1)S(1)}, bf16[512,2048]{1,0:T(8,128)(2,1)}, u32[]{:S(2)}, u32[]{:S(2)}) %collective-permute-start.18) | collective-permute-done | bytes 2097184 | tf_op jit(solution)/shard_map/ppermute | solution.py:51
  145.4 1.9 collective-permute-start.2
  149.1 17.4 %collective-permute-done.11.refs_13_.refs_14_ = bf16[512,2048]{1,0:T(8,128)(2,1)} collective-permute-done((bf16[512,2048]{1,0:T(8,128)(2,1)S(1)}, bf16[512,2048]{1,0:T(8,128)(2,1)}, u32[]{:S(2)}, u32[]{:S(2)}) %collective-permute-start.11) | collective-permute-done | bytes 2097184 | tf_op jit(solution)/shard_map/ppermute | solution.py:51
  166.7 12.9 %forward_part.3.refs_15_ = f32[864,2048]{1,0:T(8,128)} custom-call(s32[42]{0:T(128)} %get-tuple-element.35.plan_ref, bf16[864,1024]{1,0:T(8,128)(2,1)} %copy-done.10, bf16[864,1024]{1,0:T(8,128)(2,1)} %copy-done.8, bf16[864,1024]{1,0:T(8,128)(2,1)} %copy-done.7, bf16[864,1024]{1,0:T(8,128)(2,1)} %copy-done.9, bf16[864,1024]{1,0:T(8,128)(2,1)} %copy-done.11, ...), custom_call_target="tpu_custom_call" | custom-call | flops 7247757312 | bytes 22544384 | tf_op jit(solution)/shard_map/forward_part/pallas_call | solution.py:225
  179.6 12.9 %forward_part.2.refs_15_ = f32[864,2048]{1,0:T(8,128)} custom-call(s32[42]{0:T(128)} %get-tuple-element.35.plan_ref, bf16[864,1024]{1,0:T(8,128)(2,1)} %copy-done.10, bf16[864,1024]{1,0:T(8,128)(2,1)} %copy-done.8, bf16[864,1024]{1,0:T(8,128)(2,1)} %copy-done.7, bf16[864,1024]{1,0:T(8,128)(2,1)} %copy-done.9, bf16[864,1024]{1,0:T(8,128)(2,1)} %copy-done.11, ...), custom_call_target="tpu_custom_call" | custom-call | flops 7247757312 | bytes 22544384 | tf_op jit(solution)/shard_map/forward_part/pallas_call | solution.py:225
  193.5 17.6 %forward_final.2 = (bf16[864,4096]{1,0:T(8,128)(2,1)}, f32[24,4096]{1,0:T(8,128)}, bf16[24,4096]{1,0:T(8,128)(2,1)}) custom-call(s32[42]{0:T(128)} %get-tuple-element.35.plan_ref, bf16[864,1024]{1,0:T(8,128)(2,1)} %collective-permute-done.2.refs_0_, bf16[864,1024]{1,0:T(8,128)(2,1)} %copy-done.10, bf16[864,1024]{1,0:T(8,128)(2,1)} %copy-done.8, ...), custom_call_target="tpu_custom_call" | custom-call | flops 7247757312 | bytes 22544384 | tf_op jit(solution)/shard_map/forward_final/pallas_call | solution.py:225
  211.1 17.6 %forward_final.3 = (bf16[864,4096]{1,0:T(8,128)(2,1)}, f32[24,4096]{1,0:T(8,128)}, bf16[24,4096]{1,0:T(8,128)(2,1)}) custom-call(s32[42]{0:T(128)} %get-tuple-element.35.plan_ref, bf16[864,1024]{1,0:T(8,128)(2,1)} %collective-permute-done.2.refs_0_, bf16[864,1024]{1,0:T(8,128)(2,1)} %copy-done.10, ...), custom_call_target="tpu_custom_call", output_to_operand_aliasing={{0}: (18, {}), {1}: (19, {}), {2}: (20, {})} | custom-call | flops 7247757312 | bytes 22544384 | tf_op jit(solution)/shard_map/forward_final/pallas_call | solution.py:225
  229.2 1.7 collective-permute-start.21
  230.9 1.6 collective-permute-start.22
  233.5 3.3 collective-permute-done.22
  237.0 1.7 collective-permute-start.25
  238.9 3.9 collective-permute-done.25
  247.0 2.8 collective-permute-start.29
  250.1 1.6 collective-permute-done.27
  255.0 11.6 %backward_first.2 = (bf16[864,4096]{1,0:T(8,128)(2,1)}, bf16[864,512]{1,0:T(8,128)(2,1)}) custom-call(s32[42]{0:T(128)} %get-tuple-element.35.plan_ref, bf16[864,4096]{1,0:T(8,128)(2,1)} %get-tuple-element.19.slope_ref, f32[12,4096]{1,0:T(8,128)} %convolution_divide_fusion.1.pass_ref, f32[12,4096]{1,0:T(8,128)} %convolution_divide_fusion.query_ref, ...), custom_call_target="tpu_custom_call" | custom-call | flops 3623878656 | bytes 19234816 | tf_op jit(solution)/shard_map/backward_first/pallas_call | solution.py:317
  266.6 1.6 collective-permute-start.43
  268.2 4.0 %collective-permute-start.44 = (bf16[864,512]{1,0:T(8,128)(2,1)}, bf16[864,512]{1,0:T(8,128)(2,1)}, u32[]{:S(2)}, u32[]{:S(2)}) collective-permute-start(bf16[864,512]{1,0:T(8,128)(2,1)} %get-tuple-element.25), channel_id=1, source_target_pairs={{0,8},{1,9},{2,10},{3,11},{4,12},{5,13},{6,14},{7,15}} | collective-permute-start | bytes 2654216 | tf_op jit(solution)/shard_map/ppermute | solution.py:434
  272.2 10.2 %backward_first.3 = bf16[864,512]{1,0:T(8,128)(2,1)} custom-call(s32[42]{0:T(128)} %get-tuple-element.35.plan_ref, bf16[864,4096]{1,0:T(8,128)(2,1)} %get-tuple-element.19.slope_ref, f32[12,4096]{1,0:T(8,128)} %convolution_divide_fusion.1.pass_ref, f32[12,4096]{1,0:T(8,128)} %convolution_divide_fusion.query_ref, bf16[512,2048]{1,0:T(8,128)(2,1)} %copy-done.1, ...), custom_call_target="tpu_custom_call" | custom-call | flops 3623878656 | bytes 19234816 | tf_op jit(solution)/shard_map/backward_first/pallas_call | solution.py:317
  284.5 7.1 %collective-permute-done.44.refs_17_ = bf16[864,512]{1,0:T(8,128)(2,1)} collective-permute-done((bf16[864,512]{1,0:T(8,128)(2,1)}, bf16[864,512]{1,0:T(8,128)(2,1)}, u32[]{:S(2)}, u32[]{:S(2)}) %collective-permute-start.44) | collective-permute-done | bytes 884768 | tf_op jit(solution)/shard_map/ppermute | solution.py:434
  291.6 9.8 %backward_part.10 = bf16[864,512]{1,0:T(8,128)(2,1)} custom-call(s32[42]{0:T(128)} %get-tuple-element.35.plan_ref, bf16[864,4096]{1,0:T(8,128)(2,1)} %get-tuple-element.22.slopes_ref, bf16[512,2048]{1,0:T(8,128)(2,1)} %copy-done.1, bf16[512,2048]{1,0:T(8,128)(2,1)} %copy-done.5, bf16[512,2048]{1,0:T(8,128)(2,1)} %collective-permute-done.14.refs_7_.refs_9_.refs_2_, ...), custom_call_target="tpu_custom_call" | custom-call | flops 3623878656 | bytes 12156928 | tf_op jit(solution)/shard_map/backward_part/pallas_call | solution.py:399
  301.4 1.6 collective-permute-start.45
  303.0 5.0 %collective-permute-start.46 = (bf16[864,512]{1,0:T(8,128)(2,1)}, bf16[864,512]{1,0:T(8,128)(2,1)}, u32[]{:S(2)}, u32[]{:S(2)}) collective-permute-start(bf16[864,512]{1,0:T(8,128)(2,1)} %backward_part.10), channel_id=1, source_target_pairs={{0,8},{8,16},{1,9},{9,17},{2,10},{10,18},{3,11},{11,19},{4,12},{12... | collective-permute-start | bytes 2654216 | tf_op jit(solution)/shard_map/ppermute | solution.py:434
  308.0 2.6 collective-permute-done.38.refs_17_
  311.5 9.7 %backward_part.7 = bf16[864,512]{1,0:T(8,128)(2,1)} custom-call(s32[42]{0:T(128)} %get-tuple-element.35.plan_ref, bf16[864,4096]{1,0:T(8,128)(2,1)} %get-tuple-element.22.slopes_ref, bf16[512,2048]{1,0:T(8,128)(2,1)} %copy-done.1, bf16[512,2048]{1,0:T(8,128)(2,1)} %copy-done.5, bf16[512,2048]{1,0:T(8,128)(2,1)} %collective-permute-done.14.refs_7_.refs_9_.refs_2_, ...), custom_call_target="tpu_custom_call" | custom-call | flops 3623878656 | bytes 12156928 | tf_op jit(solution)/shard_map/backward_part/pallas_call | solution.py:399
  321.9 5.9 %collective-permute-start.40 = (bf16[864,512]{1,0:T(8,128)(2,1)}, bf16[864,512]{1,0:T(8,128)(2,1)}, u32[]{:S(2)}, u32[]{:S(2)}) collective-permute-start(bf16[864,512]{1,0:T(8,128)(2,1)} %backward_part.7), channel_id=1, source_target_pairs={{0,8},{8,16},{1,9},{9,17},{2,10},{10,18},{3,11},{11,19},{4,12},{12... | collective-permute-start | bytes 2654216 | tf_op jit(solution)/shard_map/ppermute | solution.py:434
  327.8 1.7 collective-permute-done.46.refs_17_
  329.5 15.1 %backward_part.11 = (bf16[864,512]{1,0:T(8,128)(2,1)}, bf16[864,512]{1,0:T(8,128)(2,1)}) custom-call(s32[42]{0:T(128)} %get-tuple-element.35.plan_ref, bf16[864,4096]{1,0:T(8,128)(2,1)} %get-tuple-element.22.slopes_ref, bf16[512,2048]{1,0:T(8,128)(2,1)} %copy-done.1, bf16[512,2048]{1,0:T(8,128)(2,1)} %copy-done.5, ...), custom_call_target="tpu_custom_call" | custom-call | flops 7247757312 | bytes 17235968 | tf_op jit(solution)/shard_map/backward_part/pallas_call | solution.py:399
  345.9 5.9 %collective-permute-start.48 = (bf16[864,512]{1,0:T(8,128)(2,1)}, bf16[864,512]{1,0:T(8,128)(2,1)}, u32[]{:S(2)}, u32[]{:S(2)}) collective-permute-start(bf16[864,512]{1,0:T(8,128)(2,1)} %get-tuple-element.27), channel_id=1, source_target_pairs={{0,8},{8,16},{16,24},{1,9},{9,17},{17,25},{2,10},{10,18},{18,26},{... | collective-permute-start | bytes 2654216 | tf_op jit(solution)/shard_map/ppermute | solution.py:434
  352.8 15.1 %backward_part.8 = (bf16[864,512]{1,0:T(8,128)(2,1)}, bf16[864,512]{1,0:T(8,128)(2,1)}) custom-call(s32[42]{0:T(128)} %get-tuple-element.35.plan_ref, bf16[864,4096]{1,0:T(8,128)(2,1)} %get-tuple-element.22.slopes_ref, bf16[512,2048]{1,0:T(8,128)(2,1)} %copy-done.1, bf16[512,2048]{1,0:T(8,128)(2,1)} %copy-done.5, ...), custom_call_target="tpu_custom_call" | custom-call | flops 7247757312 | bytes 17235968 | tf_op jit(solution)/shard_map/backward_part/pallas_call | solution.py:399
  369.2 5.6 %collective-permute-start.42 = (bf16[864,512]{1,0:T(8,128)(2,1)}, bf16[864,512]{1,0:T(8,128)(2,1)}, u32[]{:S(2)}, u32[]{:S(2)}) collective-permute-start(bf16[864,512]{1,0:T(8,128)(2,1)} %get-tuple-element.24), channel_id=1, source_target_pairs={{0,8},{8,16},{16,24},{1,9},{9,17},{17,25},{2,10},{10,18},{18,26},{... | collective-permute-start | bytes 2654216 | tf_op jit(solution)/shard_map/ppermute | solution.py:434
  374.7 8.8 %backward_part.9 = bf16[864,512]{1,0:T(8,128)(2,1)} custom-call(s32[42]{0:T(128)} %get-tuple-element.35.plan_ref, bf16[864,4096]{1,0:T(8,128)(2,1)} %get-tuple-element.22.slopes_ref, bf16[512,2048]{1,0:T(8,128)(2,1)} %copy-done.1, bf16[512,2048]{1,0:T(8,128)(2,1)} %copy-done.5, bf16[512,2048]{1,0:T(8,128)(2,1)} %collective-permute-done.14.refs_7_.refs_9_.refs_2_, ...), custom_call_target="tpu_custom_call" | custom-call | flops 3623878656 | bytes 12156928 | tf_op jit(solution)/shard_map/backward_part/pallas_call | solution.py:399
  383.5 8.9 %backward_part.6 = bf16[864,512]{1,0:T(8,128)(2,1)} custom-call(s32[42]{0:T(128)} %get-tuple-element.35.plan_ref, bf16[864,4096]{1,0:T(8,128)(2,1)} %get-tuple-element.22.slopes_ref, bf16[512,2048]{1,0:T(8,128)(2,1)} %copy-done.1, bf16[512,2048]{1,0:T(8,128)(2,1)} %copy-done.5, bf16[512,2048]{1,0:T(8,128)(2,1)} %collective-permute-done.14.refs_7_.refs_9_.refs_2_, ...), custom_call_target="tpu_custom_call" | custom-call | flops 3623878656 | bytes 12156928 | tf_op jit(solution)/shard_map/backward_part/pallas_call | solution.py:399
  392.5 1.6 add_convert_fusion
  394.2 1.8 add_convert_fusion.1
  (142 shorter events, 35.0 us)
Async XLA Ops:
  2.3 67.3 %collective-permute-start = (bf16[864,1024]{1,0:T(8,128)(2,1)S(1)}, bf16[864,1024]{1,0:T(8,128)(2,1)S(1)}, u32[]{:S(2)}, u32[]{:S(2)}) collective-permute-start(bf16[864,1024]{1,0:T(8,128)(2,1)S(1)} %pad_maximum_fusion.refs_2_.refs_3_), channel_id=1, source_target_pairs={{0,8},{8,16},{16,24},{1,9},{9,17},{17,25},{2,10},{10,18},{18,26},{... | collective-permute-start | bytes 5308424 | tf_op jit(solution)/shard_map/ppermute | solution.py:31
  9.4 63.8 %collective-permute-start.15 = (bf16[512,2048]{1,0:T(8,128)(2,1)S(1)}, bf16[512,2048]{1,0:T(8,128)(2,1)S(1)}, u32[]{:S(2)}, u32[]{:S(2)}) collective-permute-start(bf16[512,2048]{1,0:T(8,128)(2,1)S(1)} %slice.35.refs_5_.refs_7_.refs_0_), channel_id=1, source_target_pairs={{0,4},{1,3},{2,6},{3,1},{4,0},{5,7},{6,2},{7,5},{8,12},{9,11},{10,... | collective-permute-start | bytes 6291464 | tf_op jit(solution)/shard_map/ppermute | solution.py:51
  11.0 60.2 %collective-permute-start.3 = (bf16[864,1024]{1,0:T(8,128)(2,1)S(1)}, bf16[864,1024]{1,0:T(8,128)(2,1)S(1)}, u32[]{:S(2)}, u32[]{:S(2)}) collective-permute-start(bf16[864,1024]{1,0:T(8,128)(2,1)S(1)} %pad_maximum_fusion.refs_2_.refs_3_), channel_id=1, source_target_pairs={{8,0},{16,8},{24,16},{9,1},{17,9},{25,17},{10,2},{18,10},{26,18},{... | collective-permute-start | bytes 5308424 | tf_op jit(solution)/shard_map/ppermute | solution.py:30
  12.3 61.0 %collective-permute-start.14 = (bf16[512,2048]{1,0:T(8,128)(2,1)S(1)}, bf16[512,2048]{1,0:T(8,128)(2,1)}, u32[]{:S(2)}, u32[]{:S(2)}) collective-permute-start(bf16[512,2048]{1,0:T(8,128)(2,1)S(1)} %slice.35.refs_5_.refs_7_.refs_0_), channel_id=1, source_target_pairs={{0,2},{1,5},{2,0},{3,7},{4,6},{5,1},{6,4},{7,3},{8,10},{9,13},{10,... | collective-permute-start | bytes 6291464 | tf_op jit(solution)/shard_map/ppermute | solution.py:51
  13.9 43.1 %collective-permute-start.32 = (s32[12]{0:T(128)S(1)}, s32[12]{0:T(128)S(1)}, u32[]{:S(2)}, u32[]{:S(2)}) collective-permute-start(s32[12]{0:T(128)S(1)} %copy-done.21), channel_id=1, source_target_pairs={{0,4},{1,3},{2,6},{3,1},{4,0},{5,7},{6,2},{7,5},{8,12},{9,11},{10,... | collective-permute-start | bytes 152 | tf_op jit(solution)/shard_map/ppermute | solution.py:51
  57.0 4.0 %collective-permute-start.31 = (s32[12]{0:T(128)S(1)}, s32[12]{0:T(128)S(1)}, u32[]{:S(2)}, u32[]{:S(2)}) collective-permute-start(s32[12]{0:T(128)S(1)} %copy-done.21), channel_id=1, source_target_pairs={{0,2},{1,5},{2,0},{3,7},{4,6},{5,1},{6,4},{7,3},{8,10},{9,13},{10,... | collective-permute-start | bytes 152 | tf_op jit(solution)/shard_map/ppermute | solution.py:51
  60.9 1.2 collective-permute-start.30
  62.1 3.6 collective-permute-start.35
  65.7 1.2 collective-permute-start.33
  66.8 1.2 collective-permute-start.34
  69.2 4.9 %collective-permute-start.13 = (bf16[512,2048]{1,0:T(8,128)(2,1)S(1)}, bf16[512,2048]{1,0:T(8,128)(2,1)S(1)}, u32[]{:S(2)}, u32[]{:S(2)}) collective-permute-start(bf16[512,2048]{1,0:T(8,128)(2,1)S(1)} %slice.35.refs_5_.refs_7_.refs_0_), channel_id=1, source_target_pairs={{0,1},{1,0},{2,3},{3,2},{4,5},{5,4},{6,7},{7,6},{8,9},{9,8},{10,11... | collective-permute-start | bytes 6291464 | tf_op jit(solution)/shard_map/ppermute | solution.py:51
  69.6 47.4 %collective-permute-start.8 = (bf16[512,2048]{1,0:T(8,128)(2,1)S(1)}, bf16[512,2048]{1,0:T(8,128)(2,1)S(1)}, u32[]{:S(2)}, u32[]{:S(2)}) collective-permute-start(bf16[512,2048]{1,0:T(8,128)(2,1)S(1)} %slice.34.refs_5_.refs_7_.refs_8_), channel_id=1, source_target_pairs={{0,4},{1,3},{2,6},{3,1},{4,0},{5,7},{6,2},{7,5},{8,12},{9,11},{10,... | collective-permute-start | bytes 6291464 | tf_op jit(solution)/shard_map/ppermute | solution.py:51
  71.2 46.7 %collective-permute-start.7 = (bf16[512,2048]{1,0:T(8,128)(2,1)S(1)}, bf16[512,2048]{1,0:T(8,128)(2,1)}, u32[]{:S(2)}, u32[]{:S(2)}) collective-permute-start(bf16[512,2048]{1,0:T(8,128)(2,1)S(1)} %slice.34.refs_5_.refs_7_.refs_8_), channel_id=1, source_target_pairs={{0,2},{1,5},{2,0},{3,7},{4,6},{5,1},{6,4},{7,3},{8,10},{9,13},{10,... | collective-permute-start | bytes 6291464 | tf_op jit(solution)/shard_map/ppermute | solution.py:51
  73.2 46.5 %collective-permute-start.6 = (bf16[512,2048]{1,0:T(8,128)(2,1)S(1)}, bf16[512,2048]{1,0:T(8,128)(2,1)S(1)}, u32[]{:S(2)}, u32[]{:S(2)}) collective-permute-start(bf16[512,2048]{1,0:T(8,128)(2,1)S(1)} %slice.34.refs_5_.refs_7_.refs_8_), channel_id=1, source_target_pairs={{0,1},{1,0},{2,3},{3,2},{4,5},{5,4},{6,7},{7,6},{8,9},{9,8},{10,11... | collective-permute-start | bytes 6291464 | tf_op jit(solution)/shard_map/ppermute | solution.py:51
  73.3 46.4 %collective-permute-start.1 = (bf16[864,1024]{1,0:T(8,128)(2,1)S(1)}, bf16[864,1024]{1,0:T(8,128)(2,1)S(1)}, u32[]{:S(2)}, u32[]{:S(2)}) collective-permute-start(bf16[864,1024]{1,0:T(8,128)(2,1)S(1)} %collective-permute-done.refs_1_.refs_2_), channel_id=1, source_target_pairs={{8,16},{16,24},{9,17},{17,25},{10,18},{18,26},{11,19},{19,27},{12,... | collective-permute-start | bytes 5308424 | tf_op jit(solution)/shard_map/ppermute | solution.py:31
  74.1 46.2 %collective-permute-start.4 = (bf16[864,1024]{1,0:T(8,128)(2,1)S(1)}, bf16[864,1024]{1,0:T(8,128)(2,1)S(1)}, u32[]{:S(2)}, u32[]{:S(2)}) collective-permute-start(bf16[864,1024]{1,0:T(8,128)(2,1)S(1)} %collective-permute-done.3.refs_3_.refs_4_), channel_id=1, source_target_pairs={{8,0},{16,8},{9,1},{17,9},{10,2},{18,10},{11,3},{19,11},{12,4},{20... | collective-permute-start | bytes 5308424 | tf_op jit(solution)/shard_map/ppermute | solution.py:30
  117.1 4.5 %collective-permute-start.16 = (bf16[512,2048]{1,0:T(8,128)(2,1)S(1)}, bf16[512,2048]{1,0:T(8,128)(2,1)S(1)}, u32[]{:S(2)}, u32[]{:S(2)}) collective-permute-start(bf16[512,2048]{1,0:T(8,128)(2,1)S(1)} %collective-permute-done.15.refs_9_.refs_11_.refs_4_), channel_id=1, source_target_pairs={{0,1},{1,0},{2,3},{3,2},{4,5},{5,4},{6,7},{7,6},{8,9},{9,8},{10,11... | collective-permute-start | bytes 6291464 | tf_op jit(solution)/shard_map/ppermute | solution.py:51
  118.0 26.1 %collective-permute-start.18 = (bf16[512,2048]{1,0:T(8,128)(2,1)S(1)}, bf16[512,2048]{1,0:T(8,128)(2,1)}, u32[]{:S(2)}, u32[]{:S(2)}) collective-permute-start(bf16[512,2048]{1,0:T(8,128)(2,1)S(1)} %collective-permute-done.15.refs_9_.refs_11_.refs_4_), channel_id=1, source_target_pairs={{0,2},{1,5},{2,0},{3,7},{4,6},{5,1},{6,4},{7,3},{8,10},{9,13},{10,... | collective-permute-start | bytes 6291464 | tf_op jit(solution)/shard_map/ppermute | solution.py:51
  119.8 25.6 %collective-permute-start.17 = (bf16[512,2048]{1,0:T(8,128)(2,1)}, bf16[512,2048]{1,0:T(8,128)(2,1)}, u32[]{:S(2)}, u32[]{:S(2)}) collective-permute-start(bf16[512,2048]{1,0:T(8,128)(2,1)} %collective-permute-done.14.refs_7_.refs_9_.refs_2_), channel_id=1, source_target_pairs={{0,1},{1,0},{2,3},{3,2},{4,5},{5,4},{6,7},{7,6},{8,9},{9,8},{10,11... | collective-permute-start | bytes 6291464 | tf_op jit(solution)/shard_map/ppermute | solution.py:51
  119.8 27.5 %collective-permute-start.9 = (bf16[512,2048]{1,0:T(8,128)(2,1)S(1)}, bf16[512,2048]{1,0:T(8,128)(2,1)}, u32[]{:S(2)}, u32[]{:S(2)}) collective-permute-start(bf16[512,2048]{1,0:T(8,128)(2,1)S(1)} %collective-permute-done.8.refs_9_.refs_11_.refs_12_), channel_id=1, source_target_pairs={{0,1},{1,0},{2,3},{3,2},{4,5},{5,4},{6,7},{7,6},{8,9},{9,8},{10,11... | collective-permute-start | bytes 6291464 | tf_op jit(solution)/shard_map/ppermute | solution.py:51
  120.3 46.3 %collective-permute-start.11 = (bf16[512,2048]{1,0:T(8,128)(2,1)S(1)}, bf16[512,2048]{1,0:T(8,128)(2,1)}, u32[]{:S(2)}, u32[]{:S(2)}) collective-permute-start(bf16[512,2048]{1,0:T(8,128)(2,1)S(1)} %collective-permute-done.8.refs_9_.refs_11_.refs_12_), channel_id=1, source_target_pairs={{0,2},{1,5},{2,0},{3,7},{4,6},{5,1},{6,4},{7,3},{8,10},{9,13},{10,... | collective-permute-start | bytes 6291464 | tf_op jit(solution)/shard_map/ppermute | solution.py:51
  121.6 57.9 %collective-permute-start.10 = (bf16[512,2048]{1,0:T(8,128)(2,1)}, bf16[512,2048]{1,0:T(8,128)(2,1)}, u32[]{:S(2)}, u32[]{:S(2)}) collective-permute-start(bf16[512,2048]{1,0:T(8,128)(2,1)} %collective-permute-done.7.refs_7_.refs_9_.refs_10_), channel_id=1, source_target_pairs={{0,1},{1,0},{2,3},{3,2},{4,5},{5,4},{6,7},{7,6},{8,9},{9,8},{10,11... | collective-permute-start | bytes 6291464 | tf_op jit(solution)/shard_map/ppermute | solution.py:51
  144.1 48.4 %collective-permute-start.19 = (bf16[512,2048]{1,0:T(8,128)(2,1)}, bf16[512,2048]{1,0:T(8,128)(2,1)}, u32[]{:S(2)}, u32[]{:S(2)}) collective-permute-start(bf16[512,2048]{1,0:T(8,128)(2,1)} %collective-permute-done.18.refs_13_.refs_6_), channel_id=1, source_target_pairs={{0,1},{1,0},{2,3},{3,2},{4,5},{5,4},{6,7},{7,6},{8,9},{9,8},{10,11... | collective-permute-start | bytes 6291464 | tf_op jit(solution)/shard_map/ppermute | solution.py:51
  145.4 47.1 %collective-permute-start.2 = (bf16[864,1024]{1,0:T(8,128)(2,1)}, bf16[864,1024]{1,0:T(8,128)(2,1)}, u32[]{:S(2)}, u32[]{:S(2)}) collective-permute-start(bf16[864,1024]{1,0:T(8,128)(2,1)} %copy-done.10), channel_id=1, source_target_pairs={{16,24},{17,25},{18,26},{19,27},{20,28},{21,29},{22,30},{23,31}} | collective-permute-start | bytes 5308424 | tf_op jit(solution)/shard_map/ppermute | solution.py:31
  147.2 45.2 %collective-permute-start.5 = (bf16[864,1024]{1,0:T(8,128)(2,1)}, bf16[864,1024]{1,0:T(8,128)(2,1)}, u32[]{:S(2)}, u32[]{:S(2)}) collective-permute-start(bf16[864,1024]{1,0:T(8,128)(2,1)} %copy-done.11), channel_id=1, source_target_pairs={{8,0},{9,1},{10,2},{11,3},{12,4},{13,5},{14,6},{15,7}} | collective-permute-start | bytes 5308424 | tf_op jit(solution)/shard_map/ppermute | solution.py:30
  166.6 44.5 %collective-permute-start.12 = (bf16[512,2048]{1,0:T(8,128)(2,1)}, bf16[512,2048]{1,0:T(8,128)(2,1)}, u32[]{:S(2)}, u32[]{:S(2)}) collective-permute-start(bf16[512,2048]{1,0:T(8,128)(2,1)} %collective-permute-done.11.refs_13_.refs_14_), channel_id=1, source_target_pairs={{0,1},{1,0},{2,3},{3,2},{4,5},{5,4},{6,7},{7,6},{8,9},{9,8},{10,11... | collective-permute-start | bytes 6291464 | tf_op jit(solution)/shard_map/ppermute | solution.py:51
  228.7 10.1 %collective-permute-start.20 = (bf16[24,4096]{1,0:T(8,128)(2,1)}, bf16[24,4096]{1,0:T(8,128)(2,1)S(1)}, u32[]{:S(2)}, u32[]{:S(2)}) collective-permute-start(bf16[24,4096]{1,0:T(8,128)(2,1)} %get-tuple-element.20), channel_id=1, source_target_pairs={{0,1},{1,0},{2,3},{3,2},{4,5},{5,4},{6,7},{7,6},{8,9},{9,8},{10,11... | collective-permute-start | bytes 589832 | tf_op jit(solution)/shard_map/ppermute | solution.py:51
  229.2 9.5 %collective-permute-start.21 = (bf16[24,4096]{1,0:T(8,128)(2,1)}, bf16[24,4096]{1,0:T(8,128)(2,1)S(1)}, u32[]{:S(2)}, u32[]{:S(2)}) collective-permute-start(bf16[24,4096]{1,0:T(8,128)(2,1)} %get-tuple-element.20), channel_id=1, source_target_pairs={{0,2},{1,5},{2,0},{3,7},{4,6},{5,1},{6,4},{7,3},{8,10},{9,13},{10,... | collective-permute-start | bytes 589832 | tf_op jit(solution)/shard_map/ppermute | solution.py:51
  230.9 5.9 %collective-permute-start.22 = (bf16[24,4096]{1,0:T(8,128)(2,1)}, bf16[24,4096]{1,0:T(8,128)(2,1)S(1)}, u32[]{:S(2)}, u32[]{:S(2)}) collective-permute-start(bf16[24,4096]{1,0:T(8,128)(2,1)} %get-tuple-element.20), channel_id=1, source_target_pairs={{0,4},{1,3},{2,6},{3,1},{4,0},{5,7},{6,2},{7,5},{8,12},{9,11},{10,... | collective-permute-start | bytes 589832 | tf_op jit(solution)/shard_map/ppermute | solution.py:51
  236.8 2.0 collective-permute-start.23
  237.0 5.7 %collective-permute-start.25 = (bf16[24,4096]{1,0:T(8,128)(2,1)S(1)}, bf16[24,4096]{1,0:T(8,128)(2,1)S(1)}, u32[]{:S(2)}, u32[]{:S(2)}) collective-permute-start(bf16[24,4096]{1,0:T(8,128)(2,1)S(1)} %collective-permute-done.22), channel_id=1, source_target_pairs={{0,2},{1,5},{2,0},{3,7},{4,6},{5,1},{6,4},{7,3},{8,10},{9,13},{10,... | collective-permute-start | bytes 589832 | tf_op jit(solution)/shard_map/ppermute | solution.py:51
  238.7 4.0 collective-permute-start.24
  242.7 1.4 collective-permute-start.26
  245.2 6.5 %collective-permute-start.27 = (f32[96,96]{0,1:T(8,128)S(1)}, f32[96,96]{0,1:T(8,128)S(1)}, u32[]{:S(2)}, u32[]{:S(2)}) collective-permute-start(f32[96,96]{0,1:T(8,128)S(1)} %fusion.14), channel_id=1, source_target_pairs={{0,8},{8,16},{16,24},{24,0},{1,9},{9,17},{17,25},{25,1},{2,10},{10... | collective-permute-start | bytes 110600 | tf_op jit(solution)/shard_map/ppermute | solution.py:492
  245.8 7.0 %collective-permute-start.28 = (f32[96,96]{0,1:T(8,128)S(1)}, f32[96,96]{0,1:T(8,128)S(1)}, u32[]{:S(2)}, u32[]{:S(2)}) collective-permute-start(f32[96,96]{0,1:T(8,128)S(1)} %fusion.14), channel_id=1, source_target_pairs={{0,16},{8,24},{16,0},{24,8},{1,17},{9,25},{17,1},{25,9},{2,18},{10... | collective-permute-start | bytes 110600 | tf_op jit(solution)/shard_map/ppermute | solution.py:492
  247.0 5.9 %collective-permute-start.29 = (f32[96,96]{0,1:T(8,128)S(1)}, f32[96,96]{0,1:T(8,128)S(1)}, u32[]{:S(2)}, u32[]{:S(2)}) collective-permute-start(f32[96,96]{0,1:T(8,128)S(1)} %fusion.14), channel_id=1, source_target_pairs={{0,24},{8,0},{16,8},{24,16},{1,25},{9,1},{17,9},{25,17},{2,26},{10... | collective-permute-start | bytes 110600 | tf_op jit(solution)/shard_map/ppermute | solution.py:492
  266.6 17.9 %collective-permute-start.43 = (bf16[864,512]{1,0:T(8,128)(2,1)}, bf16[864,512]{1,0:T(8,128)(2,1)}, u32[]{:S(2)}, u32[]{:S(2)}) collective-permute-start(bf16[864,512]{1,0:T(8,128)(2,1)} %get-tuple-element.25), channel_id=1, source_target_pairs={{24,16},{25,17},{26,18},{27,19},{28,20},{29,21},{30,22},{31,23}} | collective-permute-start | bytes 2654216 | tf_op jit(solution)/shard_map/ppermute | solution.py:433
  268.2 23.4 %collective-permute-start.44 = (bf16[864,512]{1,0:T(8,128)(2,1)}, bf16[864,512]{1,0:T(8,128)(2,1)}, u32[]{:S(2)}, u32[]{:S(2)}) collective-permute-start(bf16[864,512]{1,0:T(8,128)(2,1)} %get-tuple-element.25), channel_id=1, source_target_pairs={{0,8},{1,9},{2,10},{3,11},{4,12},{5,13},{6,14},{7,15}} | collective-permute-start | bytes 2654216 | tf_op jit(solution)/shard_map/ppermute | solution.py:434
  282.4 25.6 %collective-permute-start.37 = (bf16[864,512]{1,0:T(8,128)(2,1)}, bf16[864,512]{1,0:T(8,128)(2,1)S(1)}, u32[]{:S(2)}, u32[]{:S(2)}) collective-permute-start(bf16[864,512]{1,0:T(8,128)(2,1)} %backward_first.3), channel_id=1, source_target_pairs={{24,16},{25,17},{26,18},{27,19},{28,20},{29,21},{30,22},{31,23}} | collective-permute-start | bytes 2654216 | tf_op jit(solution)/shard_map/ppermute | solution.py:433
  283.2 27.4 %collective-permute-start.38 = (bf16[864,512]{1,0:T(8,128)(2,1)}, bf16[864,512]{1,0:T(8,128)(2,1)S(1)}, u32[]{:S(2)}, u32[]{:S(2)}) collective-permute-start(bf16[864,512]{1,0:T(8,128)(2,1)} %backward_first.3), channel_id=1, source_target_pairs={{0,8},{1,9},{2,10},{3,11},{4,12},{5,13},{6,14},{7,15}} | collective-permute-start | bytes 2654216 | tf_op jit(solution)/shard_map/ppermute | solution.py:434
  301.4 26.4 %collective-permute-start.45 = (bf16[864,512]{1,0:T(8,128)(2,1)}, bf16[864,512]{1,0:T(8,128)(2,1)}, u32[]{:S(2)}, u32[]{:S(2)}) collective-permute-start(bf16[864,512]{1,0:T(8,128)(2,1)} %backward_part.10), channel_id=1, source_target_pairs={{16,8},{24,16},{17,9},{25,17},{18,10},{26,18},{19,11},{27,19},{20,... | collective-permute-start | bytes 2654216 | tf_op jit(solution)/shard_map/ppermute | solution.py:433
  303.0 26.5 %collective-permute-start.46 = (bf16[864,512]{1,0:T(8,128)(2,1)}, bf16[864,512]{1,0:T(8,128)(2,1)}, u32[]{:S(2)}, u32[]{:S(2)}) collective-permute-start(bf16[864,512]{1,0:T(8,128)(2,1)} %backward_part.10), channel_id=1, source_target_pairs={{0,8},{8,16},{1,9},{9,17},{2,10},{10,18},{3,11},{11,19},{4,12},{12... | collective-permute-start | bytes 2654216 | tf_op jit(solution)/shard_map/ppermute | solution.py:434
  321.2 30.6 %collective-permute-start.39 = (bf16[864,512]{1,0:T(8,128)(2,1)}, bf16[864,512]{1,0:T(8,128)(2,1)S(1)}, u32[]{:S(2)}, u32[]{:S(2)}) collective-permute-start(bf16[864,512]{1,0:T(8,128)(2,1)} %backward_part.7), channel_id=1, source_target_pairs={{16,8},{24,16},{17,9},{25,17},{18,10},{26,18},{19,11},{27,19},{20,... | collective-permute-start | bytes 2654216 | tf_op jit(solution)/shard_map/ppermute | solution.py:433
  321.9 29.9 %collective-permute-start.40 = (bf16[864,512]{1,0:T(8,128)(2,1)}, bf16[864,512]{1,0:T(8,128)(2,1)}, u32[]{:S(2)}, u32[]{:S(2)}) collective-permute-start(bf16[864,512]{1,0:T(8,128)(2,1)} %backward_part.7), channel_id=1, source_target_pairs={{0,8},{8,16},{1,9},{9,17},{2,10},{10,18},{3,11},{11,19},{4,12},{12... | collective-permute-start | bytes 2654216 | tf_op jit(solution)/shard_map/ppermute | solution.py:434
  344.6 47.9 %collective-permute-start.47 = (bf16[864,512]{1,0:T(8,128)(2,1)}, bf16[864,512]{1,0:T(8,128)(2,1)S(1)}, u32[]{:S(2)}, u32[]{:S(2)}) collective-permute-start(bf16[864,512]{1,0:T(8,128)(2,1)} %get-tuple-element.26), channel_id=1, source_target_pairs={{8,0},{16,8},{24,16},{9,1},{17,9},{25,17},{10,2},{18,10},{26,18},{... | collective-permute-start | bytes 2654216 | tf_op jit(solution)/shard_map/ppermute | solution.py:433
  345.9 46.6 %collective-permute-start.48 = (bf16[864,512]{1,0:T(8,128)(2,1)}, bf16[864,512]{1,0:T(8,128)(2,1)}, u32[]{:S(2)}, u32[]{:S(2)}) collective-permute-start(bf16[864,512]{1,0:T(8,128)(2,1)} %get-tuple-element.27), channel_id=1, source_target_pairs={{0,8},{8,16},{16,24},{1,9},{9,17},{17,25},{2,10},{10,18},{18,26},{... | collective-permute-start | bytes 2654216 | tf_op jit(solution)/shard_map/ppermute | solution.py:434
  367.9 26.3 %collective-permute-start.41 = (bf16[864,512]{1,0:T(8,128)(2,1)}, bf16[864,512]{1,0:T(8,128)(2,1)}, u32[]{:S(2)}, u32[]{:S(2)}) collective-permute-start(bf16[864,512]{1,0:T(8,128)(2,1)} %get-tuple-element.23), channel_id=1, source_target_pairs={{8,0},{16,8},{24,16},{9,1},{17,9},{25,17},{10,2},{18,10},{26,18},{... | collective-permute-start | bytes 2654216 | tf_op jit(solution)/shard_map/ppermute | solution.py:433
  369.2 25.0 %collective-permute-start.42 = (bf16[864,512]{1,0:T(8,128)(2,1)}, bf16[864,512]{1,0:T(8,128)(2,1)}, u32[]{:S(2)}, u32[]{:S(2)}) collective-permute-start(bf16[864,512]{1,0:T(8,128)(2,1)} %get-tuple-element.24), channel_id=1, source_target_pairs={{0,8},{8,16},{16,24},{1,9},{9,17},{17,25},{2,10},{10,18},{18,26},{... | collective-permute-start | bytes 2654216 | tf_op jit(solution)/shard_map/ppermute | solution.py:434
  (23 other events, 794.5 us)

commit v2 on v1

--- a/solution.py
+++ b/solution.py
@@ -12,6 +12,8 @@
 SHARPNESS = 16.0
 
 VMEM_BYTES = 62 * 1024 * 1024
+FIRST_VMEM_BYTES = 24 * 1024 * 1024
+SMALL_VMEM_BYTES = 48 * 1024 * 1024
 CORES = 2
 
 
@@ -146,10 +148,9 @@
             weight_sem.at[slot, t],
         )
 
-    def fetch(j, slot):
-        for t in range(count):
-            for which in range(n_pieces):
-                pl.when(plan_ref[at + t] == which)(weight_copy(j, t, which, slot).start)
+    def fetch(j, slot, t):
+        for which in range(n_pieces):
+            pl.when(plan_ref[at + t] == which)(weight_copy(j, t, which, slot).start)
 
     def hidden_copy(t, ref):
         return pltpu.make_async_copy(
@@ -160,25 +161,29 @@
 
     @pl.when(step == 0)
     def _():
-        fetch(0, 0)
         for t in range(count):
             for code, ref in sources:
                 pl.when(plan_ref[at + count + t] == code)(hidden_copy(t, ref).start)
+            fetch(0, 0, t)
 
     slot = lax.rem(step, 2)
 
     @pl.when(step + 1 < pl.num_programs(0))
     def _():
-        fetch(step + 1, 1 - slot)
-
-    @pl.when(step == 0)
-    def _():
         for t in range(count):
+            fetch(step + 1, 1 - slot, t)
+
+    value = None
+    for t in range(count):
+        block = pl.ds(t * depth, depth)
+
+        @pl.when(step == 0)
+        def _():
             hidden_copy(t, sources[0][1]).wait()
 
-    for t in range(count):
         weight_copy(step, t, 0, slot).wait()
-    value = jnp.dot(held[...], weights[slot], preferred_element_type=jnp.float32)
+        term = jnp.dot(held[:, block], weights[slot, block], preferred_element_type=jnp.float32)
+        value = term if value is None else value + term
     if not final:
         out_ref[...] = value
         return
@@ -331,7 +336,7 @@
             ],
         ),
         compiler_params=pltpu.CompilerParams(
-            dimension_semantics=("arbitrary",), vmem_limit_bytes=VMEM_BYTES
+            dimension_semantics=("arbitrary",), vmem_limit_bytes=FIRST_VMEM_BYTES
         ),
         cost_estimate=pl.CostEstimate(
             flops=2 * rows * depth * width,
@@ -407,7 +412,7 @@
             pltpu.SemaphoreType.DMA((units, len(groups))),
             pltpu.SemaphoreType.DMA((parts,)),
         ],
-        compiler_params=pltpu.CompilerParams(vmem_limit_bytes=VMEM_BYTES),
+        compiler_params=pltpu.CompilerParams(vmem_limit_bytes=SMALL_VMEM_BYTES),
         cost_estimate=pl.CostEstimate(
             flops=2 * rows * depth * units * width,
             bytes_accessed=(units * depth * width + rows * width + units * rows * depth) * 2,

time: 399 us -> 396 us (level)
  Pallas kernels: 150 us -> 136 us
  waiting for transfers between devices: 155 us -> 165 us
  local copies, waits for them, and re-layouts: 8.17 us -> 15.9 us
  starting transfers between devices: 73.4 us -> 69.3 us
    pallas_call x6, Pallas kernels: 67.4 us -> 55.3 us  [backward(): pl.pallas_call(functools.partial(backward_kernel, (at, count, spans(group...]
    ppermute x6, waiting for transfers between devices: 11.3 us -> 21.4 us  [line_reduce_scatter(): lax.ppermute(to_right, 'vocab', [(d, d + 1) for d in range(step)])]
    unnamed x52 -> x60, local copies, waits for them, and re-layouts: 3.07 us -> 7.6 us
  transfers between devices with their start and end apart: 49 -> 49, of which waited for: 19 -> 21; matrix products, arithmetic and copies ran while one was open for 2% -> 2% of each run, Pallas kernels for 30% -> 27%
where the time goes in v2:
time: 396 us; the launch traced here: 395 us
  waiting for transfers between devices  165 us (42%)
  Pallas kernels  136 us (34%)
  starting transfers between devices  69.3 us (18%)
  local copies, waits for them, and re-layouts  15.9 us (4%)
  other arithmetic  5.07 us (1%)
    ppermute x28, waiting for transfers between devices, move(): return lax.ppermute(value, 'rows', pairs)  141 us
    pallas_call x4, Pallas kernels, forward(): pl.pallas_call(functools.partial(forward_kernel, spec), out_shape=out_sha...  60.1 us
    pallas_call x6, Pallas kernels, backward(): pl.pallas_call(functools.partial(backward_kernel, (at, count, spans(group...  55.3 us
    ppermute x6, starting transfers between devices, line_reduce_scatter(): lax.ppermute(to_right, 'vocab', [(d, d + 1) for d in range(step)])  25.3 us
    ppermute x28, starting transfers between devices, move(): return lax.ppermute(value, 'rows', pairs)  21.9 us
    ppermute x6, waiting for transfers between devices, line_reduce_scatter(): lax.ppermute(to_right, 'vocab', [(d, d + 1) for d in range(step)])  21.4 us
    pallas_call x2, Pallas kernels, backward_first(): pl.pallas_call(functools.partial(first_kernel, (at, count, spans(parts),...  20.2 us
    ppermute x3, starting transfers between devices, line_gather(): lax.ppermute(right, 'vocab', [(z, z + 1) for z in range(step - 1, n - 1)])  7.98 us
  transfers between devices with their start and end apart: 49, of which 21 were waited for; matrix products, arithmetic and copies ran while one was open for 2% of the time, Pallas kernels for 27%

profile of v2, /device:TPU:0, one launch (start us, length us, event | category | flops | bytes accessed | tf_op | source)
XLA Modules:
  0.0 395.4 jit_solution(12238248880375736668)
XLA Ops:
  0.6 1.7 pad_maximum_fusion.refs_2_.refs_3_
  2.3 5.3 %collective-permute-start = (bf16[864,1024]{1,0:T(8,128)(2,1)S(1)}, bf16[864,1024]{1,0:T(8,128)(2,1)S(1)}, u32[]{:S(2)}, u32[]{:S(2)}) collective-permute-start(bf16[864,1024]{1,0:T(8,128)(2,1)S(1)} %pad_maximum_fusion.refs_2_.refs_3_), channel_id=1, source_target_pairs={{0,8},{8,16},{16,24},{1,9},{9,17},{17,25},{2,10},{10,18},{18,26},{... | collective-permute-start | bytes 5308424 | tf_op jit(solution)/shard_map/ppermute | solution.py:33
  7.7 1.7 slice.35.refs_5_.refs_7_.refs_0_
  9.4 1.6 collective-permute-start.15
  12.3 1.6 collective-permute-start.14
  14.4 42.6 %collective-permute-done.32 = s32[12]{0:T(128)S(1)} collective-permute-done((s32[12]{0:T(128)S(1)}, s32[12]{0:T(128)S(1)}, u32[]{:S(2)}, u32[]{:S(2)}) %collective-permute-start.32) | collective-permute-done | bytes 80 | tf_op jit(solution)/shard_map/ppermute | solution.py:53
  57.0 2.5 collective-permute-start.31
  62.1 2.0 collective-permute-start.35
  69.6 1.6 collective-permute-start.8
  71.2 2.0 collective-permute-start.7
  75.4 41.6 %collective-permute-done.8.refs_9_.refs_11_.refs_12_ = bf16[512,2048]{1,0:T(8,128)(2,1)S(1)} collective-permute-done((bf16[512,2048]{1,0:T(8,128)(2,1)S(1)}, bf16[512,2048]{1,0:T(8,128)(2,1)S(1)}, u32[]{:S(2)}, u32[]{:S(2)}) %collective-permute-start.8) | collective-permute-done | bytes 2097184 | tf_op jit(solution)/shard_map/ppermute | solution.py:53
  118.0 1.8 collective-permute-start.18
  121.8 22.3 %collective-permute-done.18.refs_13_.refs_6_ = bf16[512,2048]{1,0:T(8,128)(2,1)} collective-permute-done((bf16[512,2048]{1,0:T(8,128)(2,1)S(1)}, bf16[512,2048]{1,0:T(8,128)(2,1)}, u32[]{:S(2)}, u32[]{:S(2)}) %collective-permute-start.18) | collective-permute-done | bytes 2097184 | tf_op jit(solution)/shard_map/ppermute | solution.py:53
  145.4 1.9 collective-permute-start.2
  149.2 17.4 %collective-permute-done.11.refs_13_.refs_14_ = bf16[512,2048]{1,0:T(8,128)(2,1)} collective-permute-done((bf16[512,2048]{1,0:T(8,128)(2,1)S(1)}, bf16[512,2048]{1,0:T(8,128)(2,1)}, u32[]{:S(2)}, u32[]{:S(2)}) %collective-permute-start.11) | collective-permute-done | bytes 2097184 | tf_op jit(solution)/shard_map/ppermute | solution.py:53
  166.7 12.6 %forward_part.3.refs_15_ = f32[864,2048]{1,0:T(8,128)} custom-call(s32[42]{0:T(128)} %get-tuple-element.35.plan_ref, bf16[864,1024]{1,0:T(8,128)(2,1)} %copy-done.19, bf16[864,1024]{1,0:T(8,128)(2,1)} %copy-done.17, bf16[864,1024]{1,0:T(8,128)(2,1)} %copy-done.16, bf16[864,1024]{1,0:T(8,128)(2,1)} %copy-done.18, bf16[864,1024]{1,0:T(8,128)(2,1)} %copy-done.20, ...), custom_call_target="tpu_custom_call" | custom-call | flops 7247757312 | bytes 22544384 | tf_op jit(solution)/shard_map/forward_part/pallas_call | solution.py:230
  179.3 12.6 %forward_part.2.refs_15_ = f32[864,2048]{1,0:T(8,128)} custom-call(s32[42]{0:T(128)} %get-tuple-element.35.plan_ref, bf16[864,1024]{1,0:T(8,128)(2,1)} %copy-done.19, bf16[864,1024]{1,0:T(8,128)(2,1)} %copy-done.17, bf16[864,1024]{1,0:T(8,128)(2,1)} %copy-done.16, bf16[864,1024]{1,0:T(8,128)(2,1)} %copy-done.18, bf16[864,1024]{1,0:T(8,128)(2,1)} %copy-done.20, ...), custom_call_target="tpu_custom_call" | custom-call | flops 7247757312 | bytes 22544384 | tf_op jit(solution)/shard_map/forward_part/pallas_call | solution.py:230
  192.9 17.5 %forward_final.2 = (bf16[864,4096]{1,0:T(8,128)(2,1)}, f32[24,4096]{1,0:T(8,128)}, bf16[24,4096]{1,0:T(8,128)(2,1)}) custom-call(s32[42]{0:T(128)} %get-tuple-element.35.plan_ref, bf16[864,1024]{1,0:T(8,128)(2,1)} %collective-permute-done.2.refs_0_, bf16[864,1024]{1,0:T(8,128)(2,1)} %copy-done.19, bf16[864,1024]{1,0:T(8,128)(2,1)} %copy-done.17, ...), custom_call_target="tpu_custom_call" | custom-call | flops 7247757312 | bytes 22544384 | tf_op jit(solution)/shard_map/forward_final/pallas_call | solution.py:230
  210.4 17.5 %forward_final.3 = (bf16[864,4096]{1,0:T(8,128)(2,1)}, f32[24,4096]{1,0:T(8,128)}, bf16[24,4096]{1,0:T(8,128)(2,1)}) custom-call(s32[42]{0:T(128)} %get-tuple-element.35.plan_ref, bf16[864,1024]{1,0:T(8,128)(2,1)} %collective-permute-done.2.refs_0_, bf16[864,1024]{1,0:T(8,128)(2,1)} %copy-done.19, ...), custom_call_target="tpu_custom_call", output_to_operand_aliasing={{0}: (18, {}), {1}: (19, {}), {2}: (20, {})} | custom-call | flops 7247757312 | bytes 22544384 | tf_op jit(solution)/shard_map/forward_final/pallas_call | solution.py:230
  228.4 1.8 collective-permute-start.21
  232.7 3.4 collective-permute-done.22
  236.2 1.8 collective-permute-start.25
  238.2 3.7 collective-permute-done.25
  244.8 2.4 reshape.72
  247.2 1.6 fusion.14
  250.6 2.8 collective-permute-start.29
  253.7 1.6 collective-permute-done.27
  258.4 1.6 copy-done.7
  260.0 1.6 copy-done.9
  261.6 1.6 copy-done.11
  263.2 1.6 copy-done.14
  264.8 11.1 %backward_first.2 = (bf16[864,4096]{1,0:T(8,128)(2,1)}, bf16[864,512]{1,0:T(8,128)(2,1)S(1)}) custom-call(s32[42]{0:T(128)S(1)} %copy-done.15, bf16[864,4096]{1,0:T(8,128)(2,1)} %get-tuple-element.19.slope_ref, f32[12,4096]{1,0:T(8,128)S(1)} %convolution_divide_fusion.1.pass_ref, f32[12,4096]{1,0:T(8,128)S(1)} %convolution_divide_fusion.query_ref, ...), custom_call_target="tpu_custom_call" | custom-call | flops 3623878656 | bytes 19234816 | tf_op jit(solution)/shard_map/backward_first/pallas_call | solution.py:322
  276.6 3.1 collective-permute-start.44
  279.7 9.1 %backward_first.3 = bf16[864,512]{1,0:T(8,128)(2,1)S(1)} custom-call(s32[42]{0:T(128)S(1)} %copy-done.15, bf16[864,4096]{1,0:T(8,128)(2,1)} %get-tuple-element.19.slope_ref, f32[12,4096]{1,0:T(8,128)S(1)} %convolution_divide_fusion.1.pass_ref, f32[12,4096]{1,0:T(8,128)S(1)} %convolution_divide_fusion.query_ref, bf16[512,2048]{1,0:T(8,128)(2,1)S(1)} %copy-done.3, ...), custom_call_target="tpu_custom_call" | custom-call | flops 3623878656 | bytes 19234816 | tf_op jit(solution)/shard_map/backward_first/pallas_call | solution.py:322
  290.9 8.6 %collective-permute-done.44.refs_17_ = bf16[864,512]{1,0:T(8,128)(2,1)S(1)} collective-permute-done((bf16[864,512]{1,0:T(8,128)(2,1)S(1)}, bf16[864,512]{1,0:T(8,128)(2,1)S(1)}, u32[]{:S(2)}, u32[]{:S(2)}) %collective-permute-start.44) | collective-permute-done | bytes 884768 | tf_op jit(solution)/shard_map/ppermute | solution.py:439
  299.4 7.9 %backward_part.10 = bf16[864,512]{1,0:T(8,128)(2,1)S(1)} custom-call(s32[42]{0:T(128)S(1)} %copy-done.15, bf16[864,4096]{1,0:T(8,128)(2,1)} %get-tuple-element.22.slopes_ref, bf16[512,2048]{1,0:T(8,128)(2,1)S(1)} %copy-done.3, bf16[512,2048]{1,0:T(8,128)(2,1)} %copy-done.10, bf16[512,2048]{1,0:T(8,128)(2,1)} %collective-permute-done.14.refs_7_.refs_9_.refs_2_, ...), custom_call_target="tpu_custom_call" | custom-call | flops 3623878656 | bytes 12156928 | tf_op jit(solution)/shard_map/backward_part/pallas_call | solution.py:404
  308.1 5.7 %collective-permute-start.46 = (bf16[864,512]{1,0:T(8,128)(2,1)S(1)}, bf16[864,512]{1,0:T(8,128)(2,1)S(1)}, u32[]{:S(2)}, u32[]{:S(2)}) collective-permute-start(bf16[864,512]{1,0:T(8,128)(2,1)S(1)} %backward_part.10), channel_id=1, source_target_pairs={{0,8},{8,16},{1,9},{9,17},{2,10},{10,18},{3,11},{11,19},{4,12},{12... | collective-permute-start | bytes 2654216 | tf_op jit(solution)/shard_map/ppermute | solution.py:439
  313.8 4.6 %collective-permute-done.38.refs_17_ = bf16[864,512]{1,0:T(8,128)(2,1)S(1)} collective-permute-done((bf16[864,512]{1,0:T(8,128)(2,1)S(1)}, bf16[864,512]{1,0:T(8,128)(2,1)S(1)}, u32[]{:S(2)}, u32[]{:S(2)}) %collective-permute-start.38) | collective-permute-done | bytes 884768 | tf_op jit(solution)/shard_map/ppermute | solution.py:439
  318.4 7.9 %backward_part.7 = bf16[864,512]{1,0:T(8,128)(2,1)S(1)} custom-call(s32[42]{0:T(128)S(1)} %copy-done.15, bf16[864,4096]{1,0:T(8,128)(2,1)} %get-tuple-element.22.slopes_ref, bf16[512,2048]{1,0:T(8,128)(2,1)S(1)} %copy-done.3, bf16[512,2048]{1,0:T(8,128)(2,1)} %copy-done.10, bf16[512,2048]{1,0:T(8,128)(2,1)} %collective-permute-done.14.refs_7_.refs_9_.refs_2_, ...), custom_call_target="tpu_custom_call" | custom-call | flops 3623878656 | bytes 12156928 | tf_op jit(solution)/shard_map/backward_part/pallas_call | solution.py:404
  327.0 5.0 %collective-permute-start.40 = (bf16[864,512]{1,0:T(8,128)(2,1)S(1)}, bf16[864,512]{1,0:T(8,128)(2,1)S(1)}, u32[]{:S(2)}, u32[]{:S(2)}) collective-permute-start(bf16[864,512]{1,0:T(8,128)(2,1)S(1)} %backward_part.7), channel_id=1, source_target_pairs={{0,8},{8,16},{1,9},{9,17},{2,10},{10,18},{3,11},{11,19},{4,12},{12... | collective-permute-start | bytes 2654216 | tf_op jit(solution)/shard_map/ppermute | solution.py:439
  332.1 5.3 %collective-permute-done.46.refs_17_ = bf16[864,512]{1,0:T(8,128)(2,1)S(1)} collective-permute-done((bf16[864,512]{1,0:T(8,128)(2,1)S(1)}, bf16[864,512]{1,0:T(8,128)(2,1)S(1)}, u32[]{:S(2)}, u32[]{:S(2)}) %collective-permute-start.46) | collective-permute-done | bytes 884768 | tf_op jit(solution)/shard_map/ppermute | solution.py:439
  337.4 12.1 %backward_part.11 = (bf16[864,512]{1,0:T(8,128)(2,1)S(1)}, bf16[864,512]{1,0:T(8,128)(2,1)S(1)}) custom-call(s32[42]{0:T(128)S(1)} %copy-done.15, bf16[864,4096]{1,0:T(8,128)(2,1)} %get-tuple-element.22.slopes_ref, bf16[512,2048]{1,0:T(8,128)(2,1)S(1)} %copy-done.3, bf16[512,2048]{1,0:T(8,128)(2,1)} %copy-done.10, ...), custom_call_target="tpu_custom_call" | custom-call | flops 7247757312 | bytes 17235968 | tf_op jit(solution)/shard_map/backward_part/pallas_call | solution.py:404
  350.7 5.2 %collective-permute-start.48 = (bf16[864,512]{1,0:T(8,128)(2,1)S(1)}, bf16[864,512]{1,0:T(8,128)(2,1)S(1)}, u32[]{:S(2)}, u32[]{:S(2)}) collective-permute-start(bf16[864,512]{1,0:T(8,128)(2,1)S(1)} %get-tuple-element.27), channel_id=1, source_target_pairs={{0,8},{8,16},{16,24},{1,9},{9,17},{17,25},{2,10},{10,18},{18,26},{... | collective-permute-start | bytes 2654216 | tf_op jit(solution)/shard_map/ppermute | solution.py:439
  356.3 12.1 %backward_part.8 = (bf16[864,512]{1,0:T(8,128)(2,1)S(1)}, bf16[864,512]{1,0:T(8,128)(2,1)S(1)}) custom-call(s32[42]{0:T(128)S(1)} %copy-done.15, bf16[864,4096]{1,0:T(8,128)(2,1)} %get-tuple-element.22.slopes_ref, bf16[512,2048]{1,0:T(8,128)(2,1)S(1)} %copy-done.3, bf16[512,2048]{1,0:T(8,128)(2,1)} %copy-done.10, ...), custom_call_target="tpu_custom_call" | custom-call | flops 7247757312 | bytes 17235968 | tf_op jit(solution)/shard_map/backward_part/pallas_call | solution.py:404
  369.7 4.9 %collective-permute-start.42 = (bf16[864,512]{1,0:T(8,128)(2,1)S(1)}, bf16[864,512]{1,0:T(8,128)(2,1)S(1)}, u32[]{:S(2)}, u32[]{:S(2)}) collective-permute-start(bf16[864,512]{1,0:T(8,128)(2,1)S(1)} %get-tuple-element.24), channel_id=1, source_target_pairs={{0,8},{8,16},{16,24},{1,9},{9,17},{17,25},{2,10},{10,18},{18,26},{... | collective-permute-start | bytes 2654216 | tf_op jit(solution)/shard_map/ppermute | solution.py:439
  374.6 7.7 %backward_part.9 = bf16[864,512]{1,0:T(8,128)(2,1)S(1)} custom-call(s32[42]{0:T(128)S(1)} %copy-done.15, bf16[864,4096]{1,0:T(8,128)(2,1)} %get-tuple-element.22.slopes_ref, bf16[512,2048]{1,0:T(8,128)(2,1)S(1)} %copy-done.3, bf16[512,2048]{1,0:T(8,128)(2,1)S(1)} %copy-done.12, bf16[512,2048]{1,0:T(8,128)(2,1)} %collective-permute-done.14.refs_7_.refs_9_.refs_2_, ...), custom_call_target="tpu_custom_call" | custom-call | flops 3623878656 | bytes 12156928 | tf_op jit(solution)/shard_map/backward_part/pallas_call | solution.py:404
  382.3 7.6 %backward_part.6 = bf16[864,512]{1,0:T(8,128)(2,1)S(1)} custom-call(s32[42]{0:T(128)S(1)} %copy-done.15, bf16[864,4096]{1,0:T(8,128)(2,1)} %get-tuple-element.22.slopes_ref, bf16[512,2048]{1,0:T(8,128)(2,1)S(1)} %copy-done.3, bf16[512,2048]{1,0:T(8,128)(2,1)S(1)} %copy-done.12, bf16[512,2048]{1,0:T(8,128)(2,1)} %collective-permute-done.14.refs_7_.refs_9_.refs_2_, ...), custom_call_target="tpu_custom_call" | custom-call | flops 3623878656 | bytes 12156928 | tf_op jit(solution)/shard_map/backward_part/pallas_call | solution.py:404
  390.4 2.6 collective-permute-done.42
  (150 shorter events, 40.5 us)
Async XLA Ops:
  2.3 67.3 %collective-permute-start = (bf16[864,1024]{1,0:T(8,128)(2,1)S(1)}, bf16[864,1024]{1,0:T(8,128)(2,1)S(1)}, u32[]{:S(2)}, u32[]{:S(2)}) collective-permute-start(bf16[864,1024]{1,0:T(8,128)(2,1)S(1)} %pad_maximum_fusion.refs_2_.refs_3_), channel_id=1, source_target_pairs={{0,8},{8,16},{16,24},{1,9},{9,17},{17,25},{2,10},{10,18},{18,26},{... | collective-permute-start | bytes 5308424 | tf_op jit(solution)/shard_map/ppermute | solution.py:33
  9.4 63.8 %collective-permute-start.15 = (bf16[512,2048]{1,0:T(8,128)(2,1)S(1)}, bf16[512,2048]{1,0:T(8,128)(2,1)S(1)}, u32[]{:S(2)}, u32[]{:S(2)}) collective-permute-start(bf16[512,2048]{1,0:T(8,128)(2,1)S(1)} %slice.35.refs_5_.refs_7_.refs_0_), channel_id=1, source_target_pairs={{0,4},{1,3},{2,6},{3,1},{4,0},{5,7},{6,2},{7,5},{8,12},{9,11},{10,... | collective-permute-start | bytes 6291464 | tf_op jit(solution)/shard_map/ppermute | solution.py:53
  11.0 60.2 %collective-permute-start.3 = (bf16[864,1024]{1,0:T(8,128)(2,1)S(1)}, bf16[864,1024]{1,0:T(8,128)(2,1)S(1)}, u32[]{:S(2)}, u32[]{:S(2)}) collective-permute-start(bf16[864,1024]{1,0:T(8,128)(2,1)S(1)} %pad_maximum_fusion.refs_2_.refs_3_), channel_id=1, source_target_pairs={{8,0},{16,8},{24,16},{9,1},{17,9},{25,17},{10,2},{18,10},{26,18},{... | collective-permute-start | bytes 5308424 | tf_op jit(solution)/shard_map/ppermute | solution.py:32
  12.3 61.0 %collective-permute-start.14 = (bf16[512,2048]{1,0:T(8,128)(2,1)S(1)}, bf16[512,2048]{1,0:T(8,128)(2,1)}, u32[]{:S(2)}, u32[]{:S(2)}) collective-permute-start(bf16[512,2048]{1,0:T(8,128)(2,1)S(1)} %slice.35.refs_5_.refs_7_.refs_0_), channel_id=1, source_target_pairs={{0,2},{1,5},{2,0},{3,7},{4,6},{5,1},{6,4},{7,3},{8,10},{9,13},{10,... | collective-permute-start | bytes 6291464 | tf_op jit(solution)/shard_map/ppermute | solution.py:53
  13.9 43.1 %collective-permute-start.32 = (s32[12]{0:T(128)S(1)}, s32[12]{0:T(128)S(1)}, u32[]{:S(2)}, u32[]{:S(2)}) collective-permute-start(s32[12]{0:T(128)S(1)} %copy-done.25), channel_id=1, source_target_pairs={{0,4},{1,3},{2,6},{3,1},{4,0},{5,7},{6,2},{7,5},{8,12},{9,11},{10,... | collective-permute-start | bytes 152 | tf_op jit(solution)/shard_map/ppermute | solution.py:53
  57.0 4.0 %collective-permute-start.31 = (s32[12]{0:T(128)S(1)}, s32[12]{0:T(128)S(1)}, u32[]{:S(2)}, u32[]{:S(2)}) collective-permute-start(s32[12]{0:T(128)S(1)} %copy-done.25), channel_id=1, source_target_pairs={{0,2},{1,5},{2,0},{3,7},{4,6},{5,1},{6,4},{7,3},{8,10},{9,13},{10,... | collective-permute-start | bytes 152 | tf_op jit(solution)/shard_map/ppermute | solution.py:53
  60.9 1.2 collective-permute-start.30
  62.1 3.6 collective-permute-start.35
  65.7 1.2 collective-permute-start.33
  66.8 1.2 collective-permute-start.34
  69.2 4.9 %collective-permute-start.13 = (bf16[512,2048]{1,0:T(8,128)(2,1)S(1)}, bf16[512,2048]{1,0:T(8,128)(2,1)S(1)}, u32[]{:S(2)}, u32[]{:S(2)}) collective-permute-start(bf16[512,2048]{1,0:T(8,128)(2,1)S(1)} %slice.35.refs_5_.refs_7_.refs_0_), channel_id=1, source_target_pairs={{0,1},{1,0},{2,3},{3,2},{4,5},{5,4},{6,7},{7,6},{8,9},{9,8},{10,11... | collective-permute-start | bytes 6291464 | tf_op jit(solution)/shard_map/ppermute | solution.py:53
  69.6 47.4 %collective-permute-start.8 = (bf16[512,2048]{1,0:T(8,128)(2,1)S(1)}, bf16[512,2048]{1,0:T(8,128)(2,1)S(1)}, u32[]{:S(2)}, u32[]{:S(2)}) collective-permute-start(bf16[512,2048]{1,0:T(8,128)(2,1)S(1)} %slice.34.refs_5_.refs_7_.refs_8_), channel_id=1, source_target_pairs={{0,4},{1,3},{2,6},{3,1},{4,0},{5,7},{6,2},{7,5},{8,12},{9,11},{10,... | collective-permute-start | bytes 6291464 | tf_op jit(solution)/shard_map/ppermute | solution.py:53
  71.2 46.7 %collective-permute-start.7 = (bf16[512,2048]{1,0:T(8,128)(2,1)S(1)}, bf16[512,2048]{1,0:T(8,128)(2,1)}, u32[]{:S(2)}, u32[]{:S(2)}) collective-permute-start(bf16[512,2048]{1,0:T(8,128)(2,1)S(1)} %slice.34.refs_5_.refs_7_.refs_8_), channel_id=1, source_target_pairs={{0,2},{1,5},{2,0},{3,7},{4,6},{5,1},{6,4},{7,3},{8,10},{9,13},{10,... | collective-permute-start | bytes 6291464 | tf_op jit(solution)/shard_map/ppermute | solution.py:53
  73.2 46.5 %collective-permute-start.6 = (bf16[512,2048]{1,0:T(8,128)(2,1)S(1)}, bf16[512,2048]{1,0:T(8,128)(2,1)S(1)}, u32[]{:S(2)}, u32[]{:S(2)}) collective-permute-start(bf16[512,2048]{1,0:T(8,128)(2,1)S(1)} %slice.34.refs_5_.refs_7_.refs_8_), channel_id=1, source_target_pairs={{0,1},{1,0},{2,3},{3,2},{4,5},{5,4},{6,7},{7,6},{8,9},{9,8},{10,11... | collective-permute-start | bytes 6291464 | tf_op jit(solution)/shard_map/ppermute | solution.py:53
  73.3 46.4 %collective-permute-start.1 = (bf16[864,1024]{1,0:T(8,128)(2,1)S(1)}, bf16[864,1024]{1,0:T(8,128)(2,1)S(1)}, u32[]{:S(2)}, u32[]{:S(2)}) collective-permute-start(bf16[864,1024]{1,0:T(8,128)(2,1)S(1)} %collective-permute-done.refs_1_.refs_2_), channel_id=1, source_target_pairs={{8,16},{16,24},{9,17},{17,25},{10,18},{18,26},{11,19},{19,27},{12,... | collective-permute-start | bytes 5308424 | tf_op jit(solution)/shard_map/ppermute | solution.py:33
  74.1 46.2 %collective-permute-start.4 = (bf16[864,1024]{1,0:T(8,128)(2,1)S(1)}, bf16[864,1024]{1,0:T(8,128)(2,1)S(1)}, u32[]{:S(2)}, u32[]{:S(2)}) collective-permute-start(bf16[864,1024]{1,0:T(8,128)(2,1)S(1)} %collective-permute-done.3.refs_3_.refs_4_), channel_id=1, source_target_pairs={{8,0},{16,8},{9,1},{17,9},{10,2},{18,10},{11,3},{19,11},{12,4},{20... | collective-permute-start | bytes 5308424 | tf_op jit(solution)/shard_map/ppermute | solution.py:32
  117.1 4.5 %collective-permute-start.16 = (bf16[512,2048]{1,0:T(8,128)(2,1)S(1)}, bf16[512,2048]{1,0:T(8,128)(2,1)S(1)}, u32[]{:S(2)}, u32[]{:S(2)}) collective-permute-start(bf16[512,2048]{1,0:T(8,128)(2,1)S(1)} %collective-permute-done.15.refs_9_.refs_11_.refs_4_), channel_id=1, source_target_pairs={{0,1},{1,0},{2,3},{3,2},{4,5},{5,4},{6,7},{7,6},{8,9},{9,8},{10,11... | collective-permute-start | bytes 6291464 | tf_op jit(solution)/shard_map/ppermute | solution.py:53
  118.0 26.1 %collective-permute-start.18 = (bf16[512,2048]{1,0:T(8,128)(2,1)S(1)}, bf16[512,2048]{1,0:T(8,128)(2,1)}, u32[]{:S(2)}, u32[]{:S(2)}) collective-permute-start(bf16[512,2048]{1,0:T(8,128)(2,1)S(1)} %collective-permute-done.15.refs_9_.refs_11_.refs_4_), channel_id=1, source_target_pairs={{0,2},{1,5},{2,0},{3,7},{4,6},{5,1},{6,4},{7,3},{8,10},{9,13},{10,... | collective-permute-start | bytes 6291464 | tf_op jit(solution)/shard_map/ppermute | solution.py:53
  119.8 25.7 %collective-permute-start.17 = (bf16[512,2048]{1,0:T(8,128)(2,1)}, bf16[512,2048]{1,0:T(8,128)(2,1)}, u32[]{:S(2)}, u32[]{:S(2)}) collective-permute-start(bf16[512,2048]{1,0:T(8,128)(2,1)} %collective-permute-done.14.refs_7_.refs_9_.refs_2_), channel_id=1, source_target_pairs={{0,1},{1,0},{2,3},{3,2},{4,5},{5,4},{6,7},{7,6},{8,9},{9,8},{10,11... | collective-permute-start | bytes 6291464 | tf_op jit(solution)/shard_map/ppermute | solution.py:53
  119.8 27.5 %collective-permute-start.9 = (bf16[512,2048]{1,0:T(8,128)(2,1)S(1)}, bf16[512,2048]{1,0:T(8,128)(2,1)}, u32[]{:S(2)}, u32[]{:S(2)}) collective-permute-start(bf16[512,2048]{1,0:T(8,128)(2,1)S(1)} %collective-permute-done.8.refs_9_.refs_11_.refs_12_), channel_id=1, source_target_pairs={{0,1},{1,0},{2,3},{3,2},{4,5},{5,4},{6,7},{7,6},{8,9},{9,8},{10,11... | collective-permute-start | bytes 6291464 | tf_op jit(solution)/shard_map/ppermute | solution.py:53
  120.3 46.3 %collective-permute-start.11 = (bf16[512,2048]{1,0:T(8,128)(2,1)S(1)}, bf16[512,2048]{1,0:T(8,128)(2,1)}, u32[]{:S(2)}, u32[]{:S(2)}) collective-permute-start(bf16[512,2048]{1,0:T(8,128)(2,1)S(1)} %collective-permute-done.8.refs_9_.refs_11_.refs_12_), channel_id=1, source_target_pairs={{0,2},{1,5},{2,0},{3,7},{4,6},{5,1},{6,4},{7,3},{8,10},{9,13},{10,... | collective-permute-start | bytes 6291464 | tf_op jit(solution)/shard_map/ppermute | solution.py:53
  121.6 57.6 %collective-permute-start.10 = (bf16[512,2048]{1,0:T(8,128)(2,1)}, bf16[512,2048]{1,0:T(8,128)(2,1)}, u32[]{:S(2)}, u32[]{:S(2)}) collective-permute-start(bf16[512,2048]{1,0:T(8,128)(2,1)} %collective-permute-done.7.refs_7_.refs_9_.refs_10_), channel_id=1, source_target_pairs={{0,1},{1,0},{2,3},{3,2},{4,5},{5,4},{6,7},{7,6},{8,9},{9,8},{10,11... | collective-permute-start | bytes 6291464 | tf_op jit(solution)/shard_map/ppermute | solution.py:53
  144.1 47.8 %collective-permute-start.19 = (bf16[512,2048]{1,0:T(8,128)(2,1)}, bf16[512,2048]{1,0:T(8,128)(2,1)}, u32[]{:S(2)}, u32[]{:S(2)}) collective-permute-start(bf16[512,2048]{1,0:T(8,128)(2,1)} %collective-permute-done.18.refs_13_.refs_6_), channel_id=1, source_target_pairs={{0,1},{1,0},{2,3},{3,2},{4,5},{5,4},{6,7},{7,6},{8,9},{9,8},{10,11... | collective-permute-start | bytes 6291464 | tf_op jit(solution)/shard_map/ppermute | solution.py:53
  145.4 46.5 %collective-permute-start.2 = (bf16[864,1024]{1,0:T(8,128)(2,1)}, bf16[864,1024]{1,0:T(8,128)(2,1)}, u32[]{:S(2)}, u32[]{:S(2)}) collective-permute-start(bf16[864,1024]{1,0:T(8,128)(2,1)} %copy-done.19), channel_id=1, source_target_pairs={{16,24},{17,25},{18,26},{19,27},{20,28},{21,29},{22,30},{23,31}} | collective-permute-start | bytes 5308424 | tf_op jit(solution)/shard_map/ppermute | solution.py:33
  147.3 44.6 %collective-permute-start.5 = (bf16[864,1024]{1,0:T(8,128)(2,1)}, bf16[864,1024]{1,0:T(8,128)(2,1)}, u32[]{:S(2)}, u32[]{:S(2)}) collective-permute-start(bf16[864,1024]{1,0:T(8,128)(2,1)} %copy-done.20), channel_id=1, source_target_pairs={{8,0},{9,1},{10,2},{11,3},{12,4},{13,5},{14,6},{15,7}} | collective-permute-start | bytes 5308424 | tf_op jit(solution)/shard_map/ppermute | solution.py:32
  166.6 43.8 %collective-permute-start.12 = (bf16[512,2048]{1,0:T(8,128)(2,1)}, bf16[512,2048]{1,0:T(8,128)(2,1)}, u32[]{:S(2)}, u32[]{:S(2)}) collective-permute-start(bf16[512,2048]{1,0:T(8,128)(2,1)} %collective-permute-done.11.refs_13_.refs_14_), channel_id=1, source_target_pairs={{0,1},{1,0},{2,3},{3,2},{4,5},{5,4},{6,7},{7,6},{8,9},{9,8},{10,11... | collective-permute-start | bytes 6291464 | tf_op jit(solution)/shard_map/ppermute | solution.py:53
  227.8 10.2 %collective-permute-start.20 = (bf16[24,4096]{1,0:T(8,128)(2,1)}, bf16[24,4096]{1,0:T(8,128)(2,1)S(1)}, u32[]{:S(2)}, u32[]{:S(2)}) collective-permute-start(bf16[24,4096]{1,0:T(8,128)(2,1)} %get-tuple-element.20), channel_id=1, source_target_pairs={{0,1},{1,0},{2,3},{3,2},{4,5},{5,4},{6,7},{7,6},{8,9},{9,8},{10,11... | collective-permute-start | bytes 589832 | tf_op jit(solution)/shard_map/ppermute | solution.py:53
  228.4 9.6 %collective-permute-start.21 = (bf16[24,4096]{1,0:T(8,128)(2,1)}, bf16[24,4096]{1,0:T(8,128)(2,1)S(1)}, u32[]{:S(2)}, u32[]{:S(2)}) collective-permute-start(bf16[24,4096]{1,0:T(8,128)(2,1)} %get-tuple-element.20), channel_id=1, source_target_pairs={{0,2},{1,5},{2,0},{3,7},{4,6},{5,1},{6,4},{7,3},{8,10},{9,13},{10,... | collective-permute-start | bytes 589832 | tf_op jit(solution)/shard_map/ppermute | solution.py:53
  230.2 5.9 %collective-permute-start.22 = (bf16[24,4096]{1,0:T(8,128)(2,1)}, bf16[24,4096]{1,0:T(8,128)(2,1)S(1)}, u32[]{:S(2)}, u32[]{:S(2)}) collective-permute-start(bf16[24,4096]{1,0:T(8,128)(2,1)} %get-tuple-element.20), channel_id=1, source_target_pairs={{0,4},{1,3},{2,6},{3,1},{4,0},{5,7},{6,2},{7,5},{8,12},{9,11},{10,... | collective-permute-start | bytes 589832 | tf_op jit(solution)/shard_map/ppermute | solution.py:53
  236.1 2.0 collective-permute-start.23
  236.2 5.7 %collective-permute-start.25 = (bf16[24,4096]{1,0:T(8,128)(2,1)S(1)}, bf16[24,4096]{1,0:T(8,128)(2,1)S(1)}, u32[]{:S(2)}, u32[]{:S(2)}) collective-permute-start(bf16[24,4096]{1,0:T(8,128)(2,1)S(1)} %collective-permute-done.22), channel_id=1, source_target_pairs={{0,2},{1,5},{2,0},{3,7},{4,6},{5,1},{6,4},{7,3},{8,10},{9,13},{10,... | collective-permute-start | bytes 589832 | tf_op jit(solution)/shard_map/ppermute | solution.py:53
  238.0 3.9 collective-permute-start.24
  241.9 1.4 collective-permute-start.26
  248.8 6.5 %collective-permute-start.27 = (f32[96,96]{0,1:T(8,128)S(1)}, f32[96,96]{0,1:T(8,128)S(1)}, u32[]{:S(2)}, u32[]{:S(2)}) collective-permute-start(f32[96,96]{0,1:T(8,128)S(1)} %fusion.14), channel_id=1, source_target_pairs={{0,8},{8,16},{16,24},{24,0},{1,9},{9,17},{17,25},{25,1},{2,10},{10... | collective-permute-start | bytes 110600 | tf_op jit(solution)/shard_map/ppermute | solution.py:497
  249.4 7.0 %collective-permute-start.28 = (f32[96,96]{0,1:T(8,128)S(1)}, f32[96,96]{0,1:T(8,128)S(1)}, u32[]{:S(2)}, u32[]{:S(2)}) collective-permute-start(f32[96,96]{0,1:T(8,128)S(1)} %fusion.14), channel_id=1, source_target_pairs={{0,16},{8,24},{16,0},{24,8},{1,17},{9,25},{17,1},{25,9},{2,18},{10... | collective-permute-start | bytes 110600 | tf_op jit(solution)/shard_map/ppermute | solution.py:497
  250.6 5.8 %collective-permute-start.29 = (f32[96,96]{0,1:T(8,128)S(1)}, f32[96,96]{0,1:T(8,128)S(1)}, u32[]{:S(2)}, u32[]{:S(2)}) collective-permute-start(f32[96,96]{0,1:T(8,128)S(1)} %fusion.14), channel_id=1, source_target_pairs={{0,24},{8,0},{16,8},{24,16},{1,25},{9,1},{17,9},{25,17},{2,26},{10... | collective-permute-start | bytes 110600 | tf_op jit(solution)/shard_map/ppermute | solution.py:497
  275.9 15.0 %collective-permute-start.43 = (bf16[864,512]{1,0:T(8,128)(2,1)S(1)}, bf16[864,512]{1,0:T(8,128)(2,1)S(1)}, u32[]{:S(2)}, u32[]{:S(2)}) collective-permute-start(bf16[864,512]{1,0:T(8,128)(2,1)S(1)} %get-tuple-element.25), channel_id=1, source_target_pairs={{24,16},{25,17},{26,18},{27,19},{28,20},{29,21},{30,22},{31,23}} | collective-permute-start | bytes 2654216 | tf_op jit(solution)/shard_map/ppermute | solution.py:438
  276.6 22.9 %collective-permute-start.44 = (bf16[864,512]{1,0:T(8,128)(2,1)S(1)}, bf16[864,512]{1,0:T(8,128)(2,1)S(1)}, u32[]{:S(2)}, u32[]{:S(2)}) collective-permute-start(bf16[864,512]{1,0:T(8,128)(2,1)S(1)} %get-tuple-element.25), channel_id=1, source_target_pairs={{0,8},{1,9},{2,10},{3,11},{4,12},{5,13},{6,14},{7,15}} | collective-permute-start | bytes 2654216 | tf_op jit(solution)/shard_map/ppermute | solution.py:439
  288.8 25.0 %collective-permute-start.37 = (bf16[864,512]{1,0:T(8,128)(2,1)S(1)}, bf16[864,512]{1,0:T(8,128)(2,1)S(1)}, u32[]{:S(2)}, u32[]{:S(2)}) collective-permute-start(bf16[864,512]{1,0:T(8,128)(2,1)S(1)} %backward_first.3), channel_id=1, source_target_pairs={{24,16},{25,17},{26,18},{27,19},{28,20},{29,21},{30,22},{31,23}} | collective-permute-start | bytes 2654216 | tf_op jit(solution)/shard_map/ppermute | solution.py:438
  289.5 28.9 %collective-permute-start.38 = (bf16[864,512]{1,0:T(8,128)(2,1)S(1)}, bf16[864,512]{1,0:T(8,128)(2,1)S(1)}, u32[]{:S(2)}, u32[]{:S(2)}) collective-permute-start(bf16[864,512]{1,0:T(8,128)(2,1)S(1)} %backward_first.3), channel_id=1, source_target_pairs={{0,8},{1,9},{2,10},{3,11},{4,12},{5,13},{6,14},{7,15}} | collective-permute-start | bytes 2654216 | tf_op jit(solution)/shard_map/ppermute | solution.py:439
  307.4 24.7 %collective-permute-start.45 = (bf16[864,512]{1,0:T(8,128)(2,1)S(1)}, bf16[864,512]{1,0:T(8,128)(2,1)S(1)}, u32[]{:S(2)}, u32[]{:S(2)}) collective-permute-start(bf16[864,512]{1,0:T(8,128)(2,1)S(1)} %backward_part.10), channel_id=1, source_target_pairs={{16,8},{24,16},{17,9},{25,17},{18,10},{26,18},{19,11},{27,19},{20,... | collective-permute-start | bytes 2654216 | tf_op jit(solution)/shard_map/ppermute | solution.py:438
  308.1 29.3 %collective-permute-start.46 = (bf16[864,512]{1,0:T(8,128)(2,1)S(1)}, bf16[864,512]{1,0:T(8,128)(2,1)S(1)}, u32[]{:S(2)}, u32[]{:S(2)}) collective-permute-start(bf16[864,512]{1,0:T(8,128)(2,1)S(1)} %backward_part.10), channel_id=1, source_target_pairs={{0,8},{8,16},{1,9},{9,17},{2,10},{10,18},{3,11},{11,19},{4,12},{12... | collective-permute-start | bytes 2654216 | tf_op jit(solution)/shard_map/ppermute | solution.py:439
  326.3 29.6 %collective-permute-start.39 = (bf16[864,512]{1,0:T(8,128)(2,1)S(1)}, bf16[864,512]{1,0:T(8,128)(2,1)S(1)}, u32[]{:S(2)}, u32[]{:S(2)}) collective-permute-start(bf16[864,512]{1,0:T(8,128)(2,1)S(1)} %backward_part.7), channel_id=1, source_target_pairs={{16,8},{24,16},{17,9},{25,17},{18,10},{26,18},{19,11},{27,19},{20,... | collective-permute-start | bytes 2654216 | tf_op jit(solution)/shard_map/ppermute | solution.py:438
  327.0 29.3 %collective-permute-start.40 = (bf16[864,512]{1,0:T(8,128)(2,1)S(1)}, bf16[864,512]{1,0:T(8,128)(2,1)S(1)}, u32[]{:S(2)}, u32[]{:S(2)}) collective-permute-start(bf16[864,512]{1,0:T(8,128)(2,1)S(1)} %backward_part.7), channel_id=1, source_target_pairs={{0,8},{8,16},{1,9},{9,17},{2,10},{10,18},{3,11},{11,19},{4,12},{12... | collective-permute-start | bytes 2654216 | tf_op jit(solution)/shard_map/ppermute | solution.py:439
  349.4 40.5 %collective-permute-start.47 = (bf16[864,512]{1,0:T(8,128)(2,1)S(1)}, bf16[864,512]{1,0:T(8,128)(2,1)S(1)}, u32[]{:S(2)}, u32[]{:S(2)}) collective-permute-start(bf16[864,512]{1,0:T(8,128)(2,1)S(1)} %get-tuple-element.26), channel_id=1, source_target_pairs={{8,0},{16,8},{24,16},{9,1},{17,9},{25,17},{10,2},{18,10},{26,18},{... | collective-permute-start | bytes 2654216 | tf_op jit(solution)/shard_map/ppermute | solution.py:438
  350.7 39.2 %collective-permute-start.48 = (bf16[864,512]{1,0:T(8,128)(2,1)S(1)}, bf16[864,512]{1,0:T(8,128)(2,1)S(1)}, u32[]{:S(2)}, u32[]{:S(2)}) collective-permute-start(bf16[864,512]{1,0:T(8,128)(2,1)S(1)} %get-tuple-element.27), channel_id=1, source_target_pairs={{0,8},{8,16},{16,24},{1,9},{9,17},{17,25},{2,10},{10,18},{18,26},{... | collective-permute-start | bytes 2654216 | tf_op jit(solution)/shard_map/ppermute | solution.py:439
  368.4 22.0 %collective-permute-start.41 = (bf16[864,512]{1,0:T(8,128)(2,1)S(1)}, bf16[864,512]{1,0:T(8,128)(2,1)S(1)}, u32[]{:S(2)}, u32[]{:S(2)}) collective-permute-start(bf16[864,512]{1,0:T(8,128)(2,1)S(1)} %get-tuple-element.23), channel_id=1, source_target_pairs={{8,0},{16,8},{24,16},{9,1},{17,9},{25,17},{10,2},{18,10},{26,18},{... | collective-permute-start | bytes 2654216 | tf_op jit(solution)/shard_map/ppermute | solution.py:438
  369.7 23.3 %collective-permute-start.42 = (bf16[864,512]{1,0:T(8,128)(2,1)S(1)}, bf16[864,512]{1,0:T(8,128)(2,1)S(1)}, u32[]{:S(2)}, u32[]{:S(2)}) collective-permute-start(bf16[864,512]{1,0:T(8,128)(2,1)S(1)} %get-tuple-element.24), channel_id=1, source_target_pairs={{0,8},{8,16},{16,24},{1,9},{9,17},{17,25},{2,10},{10,18},{18,26},{... | collective-permute-start | bytes 2654216 | tf_op jit(solution)/shard_map/ppermute | solution.py:439
  (27 other events, 847.5 us)

commit v3 on v2

--- a/solution.py
+++ b/solution.py
@@ -220,9 +220,10 @@
         out_shape = [
             jax.ShapeDtypeStruct((rows, whole), jnp.bfloat16),
             jax.ShapeDtypeStruct((2 * groups, whole), jnp.float32),
-            jax.ShapeDtypeStruct((2 * groups, whole), jnp.bfloat16),
+            jax.ShapeDtypeStruct((2 * groups, width), jnp.bfloat16),
         ]
-        out_specs = [column(rows), column(2 * groups), column(2 * groups)]
+        part = pl.BlockSpec((2 * groups, tile), lambda j, *_: (0, j))
+        out_specs = [column(rows), column(2 * groups), part]
     else:
         out_shape = jax.ShapeDtypeStruct((rows, width), jnp.float32)
         out_specs = pl.BlockSpec((rows, tile), lambda j, *_: (0, j))
@@ -481,18 +482,21 @@
     if two_paths(n_rows, n_vocab):
         near = {code: block for code, block in found.items() if abs(code) < n_vocab - 1}
         soon = n_rows - 2
-    logits, filled = [], ()
+    logits, filled, gathered = [], (), []
     for i in range(halves):
         logits.append(forward(near, parts[i][:soon], plan, plans.at["soon"], half))
     for i in range(halves):
         pool = (logits[i], mask, groups, pass_rows, width, i * part_width, filled)
-        filled = forward(found, parts[i], plan, plans.at["last"], half, pool=pool)
-    slopes, totals, sparse = filled
-    all_sparse = jnp.stack(row_gather(sparse, n_rows, n_vocab))
-    all_pass = all_sparse[:, :groups].reshape(-1, width)
-    all_query = all_sparse[:, groups:].reshape(-1, width)
+        *filled, sparse = forward(found, parts[i], plan, plans.at["last"], half, pool=pool)
+        gathered.append(jnp.stack(row_gather(sparse, n_rows, n_vocab)))
+    slopes, totals = filled
+    all_pass = [block[:, :groups].reshape(-1, part_width) for block in gathered]
+    all_query = [block[:, groups:].reshape(-1, part_width) for block in gathered]
     scaling = SHARPNESS * (width * n_vocab) ** (-0.5)
-    scores = lax.dot_general(all_query, all_pass, (((1,), (1,)), ((), ())), preferred_element_type=jnp.float32)
+    scores = sum(
+        lax.dot_general(q, p, (((1,), (1,)), ((), ())), preferred_element_type=jnp.float32)
+        for q, p in zip(all_query, all_pass)
+    )
     shifted = [
         lax.ppermute(scores, "vocab", [(d, (d + s) % n_vocab) for d in range(n_vocab)]) for s in range(1, n_vocab)
     ]
@@ -508,8 +512,16 @@
         row = lax.axis_index("rows") * groups
         of_query = lax.dynamic_slice_in_dim(score_grad, row, groups, 0)
         of_pass = lax.dynamic_slice_in_dim(score_grad, row, groups, 1)
-    query_grad = jnp.dot(of_query, all_pass, preferred_element_type=jnp.float32)
-    pass_grad = lax.dot_general(of_pass, all_query, (((0,), (0,)), ((), ())), preferred_element_type=jnp.float32)
+    query_grad = jnp.concatenate(
+        [jnp.dot(of_query, p, preferred_element_type=jnp.float32) for p in all_pass], axis=1
+    )
+    pass_grad = jnp.concatenate(
+        [
+            lax.dot_general(of_pass, q, (((0,), (0,)), ((), ())), preferred_element_type=jnp.float32)
+            for q in all_query
+        ],
+        axis=1,
+    )
     root = jnp.sqrt(jnp.sqrt(totals + 1.0))
     cube = root * root * root
     factors = (pass_grad / cube[:groups], query_grad / cube[groups:], (pass_length, query_length))

time: 396 us -> 407 us (1.028)
  waiting for transfers between devices: 165 us -> 185 us
  starting transfers between devices: 69.3 us -> 61.2 us
    ppermute x3, waiting for transfers between devices: 0.01 us -> 29 us  [line_gather(): lax.ppermute(left, 'vocab', [(z, z - 1) for z in range(1, n - step + 1)])]
    ppermute x28 -> x35, waiting for transfers between devices: 141 us -> 131 us  [move(): return lax.ppermute(value, 'rows', pairs)]
    ppermute x28 -> x35, starting transfers between devices: 21.9 us -> 20.3 us  [move(): return lax.ppermute(value, 'rows', pairs)]
  transfers between devices with their start and end apart: 49 -> 56, of which waited for: 21 -> 28; matrix products, arithmetic and copies ran while one was open for 2% -> 2% of each run, Pallas kernels for 27% -> 27%
where the time goes in v3:
time: 407 us; the launch traced here: 406 us
  waiting for transfers between devices  185 us (45%)
  Pallas kernels  136 us (33%)
  starting transfers between devices  61.2 us (15%)
  local copies, waits for them, and re-layouts  13 us (3%)
  other arithmetic  6.31 us (2%)
    ppermute x35, waiting for transfers between devices, move(): return lax.ppermute(value, 'rows', pairs)  131 us
    pallas_call x4, Pallas kernels, forward(): pl.pallas_call(functools.partial(forward_kernel, spec), out_shape=out_sha...  60.4 us
    pallas_call x6, Pallas kernels, backward(): pl.pallas_call(functools.partial(backward_kernel, (at, count, spans(group...  55 us
    ppermute x3, waiting for transfers between devices, line_gather(): lax.ppermute(left, 'vocab', [(z, z - 1) for z in range(1, n - step + 1)])  29 us
    ppermute x6, starting transfers between devices, line_reduce_scatter(): lax.ppermute(to_right, 'vocab', [(d, d + 1) for d in range(step)])  22.3 us
    pallas_call x2, Pallas kernels, backward_first(): pl.pallas_call(functools.partial(first_kernel, (at, count, spans(parts),...  20.4 us
    ppermute x6, waiting for transfers between devices, line_reduce_scatter(): lax.ppermute(to_right, 'vocab', [(d, d + 1) for d in range(step)])  20.4 us
    ppermute x35, starting transfers between devices, move(): return lax.ppermute(value, 'rows', pairs)  20.3 us
  transfers between devices with their start and end apart: 56, of which 28 were waited for; matrix products, arithmetic and copies ran while one was open for 2% of the time, Pallas kernels for 27%

profile of v3, /device:TPU:0, one launch (start us, length us, event | category | flops | bytes accessed | tf_op | source)
XLA Modules:
  0.0 406.4 jit_solution(8532671296876228505)
XLA Ops:
  0.6 1.7 pad_maximum_fusion.refs_2_.refs_3_
  2.3 5.3 %collective-permute-start = (bf16[864,1024]{1,0:T(8,128)(2,1)S(1)}, bf16[864,1024]{1,0:T(8,128)(2,1)S(1)}, u32[]{:S(2)}, u32[]{:S(2)}) collective-permute-start(bf16[864,1024]{1,0:T(8,128)(2,1)S(1)} %pad_maximum_fusion.refs_2_.refs_3_), channel_id=1, source_target_pairs={{0,8},{8,16},{16,24},{1,9},{9,17},{17,25},{2,10},{10,18},{18,26},{... | collective-permute-start | bytes 5308424 | tf_op jit(solution)/shard_map/ppermute | solution.py:33
  7.7 1.7 slice.40.refs_5_.refs_7_.refs_8_
  10.8 1.6 collective-permute-start.7
  13.7 1.5 collective-permute-start.38
  15.2 21.9 %collective-permute-done.38 = s32[12]{0:T(128)S(1)} collective-permute-done((s32[12]{0:T(128)S(1)}, s32[12]{0:T(128)S(1)}, u32[]{:S(2)}, u32[]{:S(2)}) %collective-permute-start.38) | collective-permute-done | bytes 80 | tf_op jit(solution)/shard_map/ppermute | solution.py:53
  37.0 1.5 collective-permute-start.39
  38.5 2.0 collective-permute-done.39
  42.9 1.5 collective-permute-start.42
  44.4 2.1 collective-permute-done.42
  47.7 1.5 collective-permute-start.8
  49.5 2.9 collective-permute-done.3.refs_3_.refs_4_
  52.4 1.5 collective-permute-start.15
  53.9 1.5 collective-permute-start.14
  56.2 35.3 %collective-permute-done.8.refs_9_.refs_11_.refs_12_ = bf16[512,2048]{1,0:T(8,128)(2,1)} collective-permute-done((bf16[512,2048]{1,0:T(8,128)(2,1)S(1)}, bf16[512,2048]{1,0:T(8,128)(2,1)}, u32[]{:S(2)}, u32[]{:S(2)}) %collective-permute-start.8) | collective-permute-done | bytes 2097184 | tf_op jit(solution)/shard_map/ppermute | solution.py:53
  92.9 25.8 %collective-permute-done.15.refs_9_.refs_11_.refs_4_ = bf16[512,2048]{1,0:T(8,128)(2,1)} collective-permute-done((bf16[512,2048]{1,0:T(8,128)(2,1)S(1)}, bf16[512,2048]{1,0:T(8,128)(2,1)}, u32[]{:S(2)}, u32[]{:S(2)}) %collective-permute-start.15) | collective-permute-done | bytes 2097184 | tf_op jit(solution)/shard_map/ppermute | solution.py:53
  120.9 12.1 %collective-permute-done.4.refs_4_.refs_5_ = bf16[864,1024]{1,0:T(8,128)(2,1)S(1)} collective-permute-done((bf16[864,1024]{1,0:T(8,128)(2,1)S(1)}, bf16[864,1024]{1,0:T(8,128)(2,1)S(1)}, u32[]{:S(2)}, u32[]{:S(2)}) %collective-permute-start.4) | collective-permute-done | bytes 1769504 | tf_op jit(solution)/shard_map/ppermute | solution.py:32
  134.2 10.9 %collective-permute-done.18.refs_13_.refs_6_ = bf16[512,2048]{1,0:T(8,128)(2,1)} collective-permute-done((bf16[512,2048]{1,0:T(8,128)(2,1)}, bf16[512,2048]{1,0:T(8,128)(2,1)}, u32[]{:S(2)}, u32[]{:S(2)}) %collective-permute-start.18) | collective-permute-done | bytes 2097184 | tf_op jit(solution)/shard_map/ppermute | solution.py:53
  147.0 20.5 %collective-permute-done.11.refs_13_.refs_14_ = bf16[512,2048]{1,0:T(8,128)(2,1)} collective-permute-done((bf16[512,2048]{1,0:T(8,128)(2,1)}, bf16[512,2048]{1,0:T(8,128)(2,1)}, u32[]{:S(2)}, u32[]{:S(2)}) %collective-permute-start.11) | collective-permute-done | bytes 2097184 | tf_op jit(solution)/shard_map/ppermute | solution.py:53
  169.7 12.6 %forward_part.2.refs_15_ = f32[864,2048]{1,0:T(8,128)} custom-call(s32[42]{0:T(128)} %get-tuple-element.39.plan_ref, bf16[864,1024]{1,0:T(8,128)(2,1)} %copy-done.15, bf16[864,1024]{1,0:T(8,128)(2,1)} %copy-done.13, bf16[864,1024]{1,0:T(8,128)(2,1)} %copy-done.12, bf16[864,1024]{1,0:T(8,128)(2,1)} %copy-done.14, bf16[864,1024]{1,0:T(8,128)(2,1)} %copy-done.16, ...), custom_call_target="tpu_custom_call" | custom-call | flops 7247757312 | bytes 22544384 | tf_op jit(solution)/shard_map/forward_part/pallas_call | solution.py:231
  182.3 12.6 %forward_part.3.refs_15_ = f32[864,2048]{1,0:T(8,128)} custom-call(s32[42]{0:T(128)} %get-tuple-element.39.plan_ref, bf16[864,1024]{1,0:T(8,128)(2,1)} %copy-done.15, bf16[864,1024]{1,0:T(8,128)(2,1)} %copy-done.13, bf16[864,1024]{1,0:T(8,128)(2,1)} %copy-done.12, bf16[864,1024]{1,0:T(8,128)(2,1)} %copy-done.14, bf16[864,1024]{1,0:T(8,128)(2,1)} %copy-done.16, ...), custom_call_target="tpu_custom_call" | custom-call | flops 7247757312 | bytes 22544384 | tf_op jit(solution)/shard_map/forward_part/pallas_call | solution.py:231
  195.0 14.0 %collective-permute-done.5.refs_6_ = bf16[864,1024]{1,0:T(8,128)(2,1)} collective-permute-done((bf16[864,1024]{1,0:T(8,128)(2,1)}, bf16[864,1024]{1,0:T(8,128)(2,1)}, u32[]{:S(2)}, u32[]{:S(2)}) %collective-permute-start.5) | collective-permute-done | bytes 1769504 | tf_op jit(solution)/shard_map/ppermute | solution.py:32
  210.0 17.4 %forward_final.2 = (bf16[864,4096]{1,0:T(8,128)(2,1)}, f32[24,4096]{1,0:T(8,128)}, bf16[24,2048]{1,0:T(8,128)(2,1)}) custom-call(s32[42]{0:T(128)} %get-tuple-element.39.plan_ref, bf16[864,1024]{1,0:T(8,128)(2,1)} %copy-done.17, bf16[864,1024]{1,0:T(8,128)(2,1)} %copy-done.15, bf16[864,1024]{1,0:T(8,128)(2,1)} %copy-done.13, bf16[864,1024]{1,0:T(8,128)(2,1)} %copy-done.12, ...), custom_call_target="tpu_custom_call" | custom-call | flops 7247757312 | bytes 22544384 | tf_op jit(solution)/shard_map/forward_final/pallas_call | solution.py:231
  227.4 17.7 %forward_final.3 = (bf16[864,4096]{1,0:T(8,128)(2,1)}, f32[24,4096]{1,0:T(8,128)}, bf16[24,2048]{1,0:T(8,128)(2,1)}) custom-call(s32[42]{0:T(128)} %get-tuple-element.39.plan_ref, bf16[864,1024]{1,0:T(8,128)(2,1)} %copy-done.17, bf16[864,1024]{1,0:T(8,128)(2,1)} %copy-done.15, ...), custom_call_target="tpu_custom_call", output_to_operand_aliasing={{0}: (18, {}), {1}: (19, {})} | custom-call | flops 7247757312 | bytes 22544384 | tf_op jit(solution)/shard_map/forward_final/pallas_call | solution.py:231
  246.0 1.6 collective-permute-start.28
  247.6 1.5 collective-permute-start.29
  257.3 2.6 collective-permute-done.25
  263.6 1.9 reshape.78
  270.7 1.6 collective-permute-done.36
  272.2 2.2 collective-permute-done.35
  276.6 1.6 copy-done.9
  278.2 9.1 %backward_first.3 = bf16[864,512]{1,0:T(8,128)(2,1)S(1)} custom-call(s32[42]{0:T(128)S(1)} %copy-done.11, bf16[864,4096]{1,0:T(8,128)(2,1)} %get-tuple-element.18.slope_ref, f32[12,4096]{1,0:T(8,128)S(1)} %get-tuple-element.37.pass_ref, f32[12,4096]{1,0:T(8,128)S(1)} %get-tuple-element.36.query_ref, bf16[512,2048]{1,0:T(8,128)(2,1)S(1)} %copy-done.3, ...), custom_call_target="tpu_custom_call" | custom-call | flops 3623878656 | bytes 19234816 | tf_op jit(solution)/shard_map/backward_first/pallas_call | solution.py:323
  288.0 1.6 collective-permute-start.45
  289.6 11.3 %backward_first.2 = (bf16[864,4096]{1,0:T(8,128)(2,1)}, bf16[864,512]{1,0:T(8,128)(2,1)}) custom-call(s32[42]{0:T(128)S(1)} %copy-done.11, bf16[864,4096]{1,0:T(8,128)(2,1)} %get-tuple-element.18.slope_ref, f32[12,4096]{1,0:T(8,128)S(1)} %get-tuple-element.37.pass_ref, f32[12,4096]{1,0:T(8,128)S(1)} %get-tuple-element.36.query_ref, ...), custom_call_target="tpu_custom_call" | custom-call | flops 3623878656 | bytes 19234816 | tf_op jit(solution)/shard_map/backward_first/pallas_call | solution.py:323
  303.1 6.5 %collective-permute-done.45.refs_17_ = bf16[864,512]{1,0:T(8,128)(2,1)S(1)} collective-permute-done((bf16[864,512]{1,0:T(8,128)(2,1)S(1)}, bf16[864,512]{1,0:T(8,128)(2,1)S(1)}, u32[]{:S(2)}, u32[]{:S(2)}) %collective-permute-start.45) | collective-permute-done | bytes 884768 | tf_op jit(solution)/shard_map/ppermute | solution.py:440
  309.6 7.9 %backward_part.7 = bf16[864,512]{1,0:T(8,128)(2,1)S(1)} custom-call(s32[42]{0:T(128)S(1)} %copy-done.11, bf16[864,4096]{1,0:T(8,128)(2,1)} %get-tuple-element.22.slopes_ref, bf16[512,2048]{1,0:T(8,128)(2,1)S(1)} %copy-done.3, bf16[512,2048]{1,0:T(8,128)(2,1)} %copy-done.8, bf16[512,2048]{1,0:T(8,128)(2,1)} %collective-permute-done.14.refs_7_.refs_9_.refs_2_, ...), custom_call_target="tpu_custom_call" | custom-call | flops 3623878656 | bytes 12156928 | tf_op jit(solution)/shard_map/backward_part/pallas_call | solution.py:405
  318.2 5.0 %collective-permute-start.47 = (bf16[864,512]{1,0:T(8,128)(2,1)S(1)}, bf16[864,512]{1,0:T(8,128)(2,1)S(1)}, u32[]{:S(2)}, u32[]{:S(2)}) collective-permute-start(bf16[864,512]{1,0:T(8,128)(2,1)S(1)} %backward_part.7), channel_id=1, source_target_pairs={{0,8},{8,16},{1,9},{9,17},{2,10},{10,18},{3,11},{11,19},{4,12},{12... | collective-permute-start | bytes 2654216 | tf_op jit(solution)/shard_map/ppermute | solution.py:440
  323.3 5.4 %collective-permute-done.51.refs_17_ = bf16[864,512]{1,0:T(8,128)(2,1)S(1)} collective-permute-done((bf16[864,512]{1,0:T(8,128)(2,1)}, bf16[864,512]{1,0:T(8,128)(2,1)S(1)}, u32[]{:S(2)}, u32[]{:S(2)}) %collective-permute-start.51) | collective-permute-done | bytes 884768 | tf_op jit(solution)/shard_map/ppermute | solution.py:440
  328.7 7.9 %backward_part.10 = bf16[864,512]{1,0:T(8,128)(2,1)S(1)} custom-call(s32[42]{0:T(128)S(1)} %copy-done.11, bf16[864,4096]{1,0:T(8,128)(2,1)} %get-tuple-element.22.slopes_ref, bf16[512,2048]{1,0:T(8,128)(2,1)S(1)} %copy-done.3, bf16[512,2048]{1,0:T(8,128)(2,1)} %copy-done.8, bf16[512,2048]{1,0:T(8,128)(2,1)} %collective-permute-done.14.refs_7_.refs_9_.refs_2_, ...), custom_call_target="tpu_custom_call" | custom-call | flops 3623878656 | bytes 12156928 | tf_op jit(solution)/shard_map/backward_part/pallas_call | solution.py:405
  337.3 5.6 %collective-permute-start.53 = (bf16[864,512]{1,0:T(8,128)(2,1)S(1)}, bf16[864,512]{1,0:T(8,128)(2,1)S(1)}, u32[]{:S(2)}, u32[]{:S(2)}) collective-permute-start(bf16[864,512]{1,0:T(8,128)(2,1)S(1)} %backward_part.10), channel_id=1, source_target_pairs={{0,8},{8,16},{1,9},{9,17},{2,10},{10,18},{3,11},{11,19},{4,12},{12... | collective-permute-start | bytes 2654216 | tf_op jit(solution)/shard_map/ppermute | solution.py:440
  342.9 4.6 %collective-permute-done.47.refs_17_ = bf16[864,512]{1,0:T(8,128)(2,1)S(1)} collective-permute-done((bf16[864,512]{1,0:T(8,128)(2,1)S(1)}, bf16[864,512]{1,0:T(8,128)(2,1)S(1)}, u32[]{:S(2)}, u32[]{:S(2)}) %collective-permute-start.47) | collective-permute-done | bytes 884768 | tf_op jit(solution)/shard_map/ppermute | solution.py:440
  347.5 12.0 %backward_part.8 = (bf16[864,512]{1,0:T(8,128)(2,1)S(1)}, bf16[864,512]{1,0:T(8,128)(2,1)S(1)}) custom-call(s32[42]{0:T(128)S(1)} %copy-done.11, bf16[864,4096]{1,0:T(8,128)(2,1)} %get-tuple-element.22.slopes_ref, bf16[512,2048]{1,0:T(8,128)(2,1)S(1)} %copy-done.3, bf16[512,2048]{1,0:T(8,128)(2,1)} %copy-done.8, ...), custom_call_target="tpu_custom_call" | custom-call | flops 7247757312 | bytes 17235968 | tf_op jit(solution)/shard_map/backward_part/pallas_call | solution.py:405
  359.6 4.3 %collective-permute-start.49 = (bf16[864,512]{1,0:T(8,128)(2,1)S(1)}, bf16[864,512]{1,0:T(8,128)(2,1)S(1)}, u32[]{:S(2)}, u32[]{:S(2)}) collective-permute-start(bf16[864,512]{1,0:T(8,128)(2,1)S(1)} %get-tuple-element.24), channel_id=1, source_target_pairs={{0,8},{8,16},{16,24},{1,9},{9,17},{17,25},{2,10},{10,18},{18,26},{... | collective-permute-start | bytes 2654216 | tf_op jit(solution)/shard_map/ppermute | solution.py:440
  366.5 12.1 %backward_part.11 = (bf16[864,512]{1,0:T(8,128)(2,1)S(1)}, bf16[864,512]{1,0:T(8,128)(2,1)S(1)}) custom-call(s32[42]{0:T(128)S(1)} %copy-done.11, bf16[864,4096]{1,0:T(8,128)(2,1)} %get-tuple-element.22.slopes_ref, bf16[512,2048]{1,0:T(8,128)(2,1)S(1)} %copy-done.3, bf16[512,2048]{1,0:T(8,128)(2,1)} %copy-done.8, ...), custom_call_target="tpu_custom_call" | custom-call | flops 7247757312 | bytes 17235968 | tf_op jit(solution)/shard_map/backward_part/pallas_call | solution.py:405
  378.5 4.4 %collective-permute-start.55 = (bf16[864,512]{1,0:T(8,128)(2,1)S(1)}, bf16[864,512]{1,0:T(8,128)(2,1)S(1)}, u32[]{:S(2)}, u32[]{:S(2)}) collective-permute-start(bf16[864,512]{1,0:T(8,128)(2,1)S(1)} %get-tuple-element.27), channel_id=1, source_target_pairs={{0,8},{8,16},{16,24},{1,9},{9,17},{17,25},{2,10},{10,18},{18,26},{... | collective-permute-start | bytes 2654216 | tf_op jit(solution)/shard_map/ppermute | solution.py:440
  384.3 7.6 %backward_part.6 = bf16[864,512]{1,0:T(8,128)(2,1)S(1)} custom-call(s32[42]{0:T(128)S(1)} %copy-done.11, bf16[864,4096]{1,0:T(8,128)(2,1)} %get-tuple-element.22.slopes_ref, bf16[512,2048]{1,0:T(8,128)(2,1)S(1)} %copy-done.3, bf16[512,2048]{1,0:T(8,128)(2,1)S(1)} %copy-done.10, bf16[512,2048]{1,0:T(8,128)(2,1)} %collective-permute-done.14.refs_7_.refs_9_.refs_2_, ...), custom_call_target="tpu_custom_call" | custom-call | flops 3623878656 | bytes 12156928 | tf_op jit(solution)/shard_map/backward_part/pallas_call | solution.py:405
  391.9 7.4 %backward_part.9 = bf16[864,512]{1,0:T(8,128)(2,1)S(1)} custom-call(s32[42]{0:T(128)S(1)} %copy-done.11, bf16[864,4096]{1,0:T(8,128)(2,1)} %get-tuple-element.22.slopes_ref, bf16[512,2048]{1,0:T(8,128)(2,1)S(1)} %copy-done.3, bf16[512,2048]{1,0:T(8,128)(2,1)S(1)} %copy-done.10, bf16[512,2048]{1,0:T(8,128)(2,1)} %collective-permute-done.14.refs_7_.refs_9_.refs_2_, ...), custom_call_target="tpu_custom_call" | custom-call | flops 3623878656 | bytes 12156928 | tf_op jit(solution)/shard_map/backward_part/pallas_call | solution.py:405
  399.8 2.7 collective-permute-done.55
  (173 shorter events, 49.2 us)
Async XLA Ops:
  2.3 47.1 %collective-permute-start = (bf16[864,1024]{1,0:T(8,128)(2,1)S(1)}, bf16[864,1024]{1,0:T(8,128)(2,1)S(1)}, u32[]{:S(2)}, u32[]{:S(2)}) collective-permute-start(bf16[864,1024]{1,0:T(8,128)(2,1)S(1)} %pad_maximum_fusion.refs_2_.refs_3_), channel_id=1, source_target_pairs={{0,8},{8,16},{16,24},{1,9},{9,17},{17,25},{2,10},{10,18},{18,26},{... | collective-permute-start | bytes 5308424 | tf_op jit(solution)/shard_map/ppermute | solution.py:33
  9.4 44.5 %collective-permute-start.6 = (bf16[512,2048]{1,0:T(8,128)(2,1)S(1)}, bf16[512,2048]{1,0:T(8,128)(2,1)S(1)}, u32[]{:S(2)}, u32[]{:S(2)}) collective-permute-start(bf16[512,2048]{1,0:T(8,128)(2,1)S(1)} %slice.40.refs_5_.refs_7_.refs_8_), channel_id=1, source_target_pairs={{0,1},{1,0},{2,3},{3,2},{4,5},{5,4},{6,7},{7,6},{8,9},{9,8},{10,11... | collective-permute-start | bytes 6291464 | tf_op jit(solution)/shard_map/ppermute | solution.py:53
  9.5 42.9 %collective-permute-start.3 = (bf16[864,1024]{1,0:T(8,128)(2,1)S(1)}, bf16[864,1024]{1,0:T(8,128)(2,1)S(1)}, u32[]{:S(2)}, u32[]{:S(2)}) collective-permute-start(bf16[864,1024]{1,0:T(8,128)(2,1)S(1)} %pad_maximum_fusion.refs_2_.refs_3_), channel_id=1, source_target_pairs={{8,0},{16,8},{24,16},{9,1},{17,9},{25,17},{10,2},{18,10},{26,18},{... | collective-permute-start | bytes 5308424 | tf_op jit(solution)/shard_map/ppermute | solution.py:32
  10.8 44.6 %collective-permute-start.7 = (bf16[512,2048]{1,0:T(8,128)(2,1)S(1)}, bf16[512,2048]{1,0:T(8,128)(2,1)S(1)}, u32[]{:S(2)}, u32[]{:S(2)}) collective-permute-start(bf16[512,2048]{1,0:T(8,128)(2,1)S(1)} %slice.40.refs_5_.refs_7_.refs_8_), channel_id=1, source_target_pairs={{0,2},{1,5},{2,0},{3,7},{4,6},{5,1},{6,4},{7,3},{8,10},{9,13},{10,... | collective-permute-start | bytes 6291464 | tf_op jit(solution)/shard_map/ppermute | solution.py:53
  13.7 23.4 %collective-permute-start.38 = (s32[12]{0:T(128)S(1)}, s32[12]{0:T(128)S(1)}, u32[]{:S(2)}, u32[]{:S(2)}) collective-permute-start(s32[12]{0:T(128)S(1)} %copy-done.22), channel_id=1, source_target_pairs={{0,2},{1,5},{2,0},{3,7},{4,6},{5,1},{6,4},{7,3},{8,10},{9,13},{10,... | collective-permute-start | bytes 152 | tf_op jit(solution)/shard_map/ppermute | solution.py:53
  37.0 3.6 collective-permute-start.39
  42.9 3.6 collective-permute-start.42
  47.7 43.9 %collective-permute-start.8 = (bf16[512,2048]{1,0:T(8,128)(2,1)S(1)}, bf16[512,2048]{1,0:T(8,128)(2,1)}, u32[]{:S(2)}, u32[]{:S(2)}) collective-permute-start(bf16[512,2048]{1,0:T(8,128)(2,1)S(1)} %slice.40.refs_5_.refs_7_.refs_8_), channel_id=1, source_target_pairs={{0,4},{1,3},{2,6},{3,1},{4,0},{5,7},{6,2},{7,5},{8,12},{9,11},{10,... | collective-permute-start | bytes 6291464 | tf_op jit(solution)/shard_map/ppermute | solution.py:53
  49.4 43.4 %collective-permute-start.13 = (bf16[512,2048]{1,0:T(8,128)(2,1)S(1)}, bf16[512,2048]{1,0:T(8,128)(2,1)S(1)}, u32[]{:S(2)}, u32[]{:S(2)}) collective-permute-start(bf16[512,2048]{1,0:T(8,128)(2,1)S(1)} %slice.41.refs_5_.refs_7_.refs_0_), channel_id=1, source_target_pairs={{0,1},{1,0},{2,3},{3,2},{4,5},{5,4},{6,7},{7,6},{8,9},{9,8},{10,11... | collective-permute-start | bytes 6291464 | tf_op jit(solution)/shard_map/ppermute | solution.py:53
  52.4 66.3 %collective-permute-start.15 = (bf16[512,2048]{1,0:T(8,128)(2,1)S(1)}, bf16[512,2048]{1,0:T(8,128)(2,1)}, u32[]{:S(2)}, u32[]{:S(2)}) collective-permute-start(bf16[512,2048]{1,0:T(8,128)(2,1)S(1)} %slice.41.refs_5_.refs_7_.refs_0_), channel_id=1, source_target_pairs={{0,4},{1,3},{2,6},{3,1},{4,0},{5,7},{6,2},{7,5},{8,12},{9,11},{10,... | collective-permute-start | bytes 6291464 | tf_op jit(solution)/shard_map/ppermute | solution.py:53
  53.9 66.3 %collective-permute-start.14 = (bf16[512,2048]{1,0:T(8,128)(2,1)S(1)}, bf16[512,2048]{1,0:T(8,128)(2,1)}, u32[]{:S(2)}, u32[]{:S(2)}) collective-permute-start(bf16[512,2048]{1,0:T(8,128)(2,1)S(1)} %slice.41.refs_5_.refs_7_.refs_0_), channel_id=1, source_target_pairs={{0,2},{1,5},{2,0},{3,7},{4,6},{5,1},{6,4},{7,3},{8,10},{9,13},{10,... | collective-permute-start | bytes 6291464 | tf_op jit(solution)/shard_map/ppermute | solution.py:53
  55.4 64.8 %collective-permute-start.1 = (bf16[864,1024]{1,0:T(8,128)(2,1)S(1)}, bf16[864,1024]{1,0:T(8,128)(2,1)S(1)}, u32[]{:S(2)}, u32[]{:S(2)}) collective-permute-start(bf16[864,1024]{1,0:T(8,128)(2,1)S(1)} %collective-permute-done.refs_1_.refs_2_), channel_id=1, source_target_pairs={{8,16},{16,24},{9,17},{17,25},{10,18},{18,26},{11,19},{19,27},{12,... | collective-permute-start | bytes 5308424 | tf_op jit(solution)/shard_map/ppermute | solution.py:33
  91.5 41.4 %collective-permute-start.4 = (bf16[864,1024]{1,0:T(8,128)(2,1)S(1)}, bf16[864,1024]{1,0:T(8,128)(2,1)S(1)}, u32[]{:S(2)}, u32[]{:S(2)}) collective-permute-start(bf16[864,1024]{1,0:T(8,128)(2,1)S(1)} %collective-permute-done.3.refs_3_.refs_4_), channel_id=1, source_target_pairs={{8,0},{16,8},{9,1},{17,9},{10,2},{18,10},{11,3},{19,11},{12,4},{20... | collective-permute-start | bytes 5308424 | tf_op jit(solution)/shard_map/ppermute | solution.py:32
  92.8 40.2 %collective-permute-start.9 = (bf16[512,2048]{1,0:T(8,128)(2,1)}, bf16[512,2048]{1,0:T(8,128)(2,1)}, u32[]{:S(2)}, u32[]{:S(2)}) collective-permute-start(bf16[512,2048]{1,0:T(8,128)(2,1)} %collective-permute-done.8.refs_9_.refs_11_.refs_12_), channel_id=1, source_target_pairs={{0,1},{1,0},{2,3},{3,2},{4,5},{5,4},{6,7},{7,6},{8,9},{9,8},{10,11... | collective-permute-start | bytes 6291464 | tf_op jit(solution)/shard_map/ppermute | solution.py:53
  118.7 26.4 %collective-permute-start.18 = (bf16[512,2048]{1,0:T(8,128)(2,1)}, bf16[512,2048]{1,0:T(8,128)(2,1)}, u32[]{:S(2)}, u32[]{:S(2)}) collective-permute-start(bf16[512,2048]{1,0:T(8,128)(2,1)} %collective-permute-done.15.refs_9_.refs_11_.refs_4_), channel_id=1, source_target_pairs={{0,2},{1,5},{2,0},{3,7},{4,6},{5,1},{6,4},{7,3},{8,10},{9,13},{10,... | collective-permute-start | bytes 6291464 | tf_op jit(solution)/shard_map/ppermute | solution.py:53
  120.2 26.0 %collective-permute-start.10 = (bf16[512,2048]{1,0:T(8,128)(2,1)S(1)}, bf16[512,2048]{1,0:T(8,128)(2,1)}, u32[]{:S(2)}, u32[]{:S(2)}) collective-permute-start(bf16[512,2048]{1,0:T(8,128)(2,1)S(1)} %collective-permute-done.7.refs_7_.refs_9_.refs_10_), channel_id=1, source_target_pairs={{0,1},{1,0},{2,3},{3,2},{4,5},{5,4},{6,7},{7,6},{8,9},{9,8},{10,11... | collective-permute-start | bytes 6291464 | tf_op jit(solution)/shard_map/ppermute | solution.py:53
  120.3 47.3 %collective-permute-start.11 = (bf16[512,2048]{1,0:T(8,128)(2,1)}, bf16[512,2048]{1,0:T(8,128)(2,1)}, u32[]{:S(2)}, u32[]{:S(2)}) collective-permute-start(bf16[512,2048]{1,0:T(8,128)(2,1)} %collective-permute-done.8.refs_9_.refs_11_.refs_12_), channel_id=1, source_target_pairs={{0,2},{1,5},{2,0},{3,7},{4,6},{5,1},{6,4},{7,3},{8,10},{9,13},{10,... | collective-permute-start | bytes 6291464 | tf_op jit(solution)/shard_map/ppermute | solution.py:53
  133.0 36.5 %collective-permute-start.16 = (bf16[512,2048]{1,0:T(8,128)(2,1)}, bf16[512,2048]{1,0:T(8,128)(2,1)}, u32[]{:S(2)}, u32[]{:S(2)}) collective-permute-start(bf16[512,2048]{1,0:T(8,128)(2,1)} %collective-permute-done.15.refs_9_.refs_11_.refs_4_), channel_id=1, source_target_pairs={{0,1},{1,0},{2,3},{3,2},{4,5},{5,4},{6,7},{7,6},{8,9},{9,8},{10,11... | collective-permute-start | bytes 6291464 | tf_op jit(solution)/shard_map/ppermute | solution.py:53
  134.2 48.1 %collective-permute-start.17 = (bf16[512,2048]{1,0:T(8,128)(2,1)}, bf16[512,2048]{1,0:T(8,128)(2,1)}, u32[]{:S(2)}, u32[]{:S(2)}) collective-permute-start(bf16[512,2048]{1,0:T(8,128)(2,1)} %collective-permute-done.14.refs_7_.refs_9_.refs_2_), channel_id=1, source_target_pairs={{0,1},{1,0},{2,3},{3,2},{4,5},{5,4},{6,7},{7,6},{8,9},{9,8},{10,11... | collective-permute-start | bytes 6291464 | tf_op jit(solution)/shard_map/ppermute | solution.py:53
  145.1 63.9 %collective-permute-start.19 = (bf16[512,2048]{1,0:T(8,128)(2,1)}, bf16[512,2048]{1,0:T(8,128)(2,1)}, u32[]{:S(2)}, u32[]{:S(2)}) collective-permute-start(bf16[512,2048]{1,0:T(8,128)(2,1)} %collective-permute-done.18.refs_13_.refs_6_), channel_id=1, source_target_pairs={{0,1},{1,0},{2,3},{3,2},{4,5},{5,4},{6,7},{7,6},{8,9},{9,8},{10,11... | collective-permute-start | bytes 6291464 | tf_op jit(solution)/shard_map/ppermute | solution.py:53
  146.3 48.7 %collective-permute-start.2 = (bf16[864,1024]{1,0:T(8,128)(2,1)}, bf16[864,1024]{1,0:T(8,128)(2,1)S(1)}, u32[]{:S(2)}, u32[]{:S(2)}) collective-permute-start(bf16[864,1024]{1,0:T(8,128)(2,1)} %copy-done.15), channel_id=1, source_target_pairs={{16,24},{17,25},{18,26},{19,27},{20,28},{21,29},{22,30},{23,31}} | collective-permute-start | bytes 5308424 | tf_op jit(solution)/shard_map/ppermute | solution.py:33
  167.6 41.5 %collective-permute-start.5 = (bf16[864,1024]{1,0:T(8,128)(2,1)}, bf16[864,1024]{1,0:T(8,128)(2,1)}, u32[]{:S(2)}, u32[]{:S(2)}) collective-permute-start(bf16[864,1024]{1,0:T(8,128)(2,1)} %copy-done.16), channel_id=1, source_target_pairs={{8,0},{9,1},{10,2},{11,3},{12,4},{13,5},{14,6},{15,7}} | collective-permute-start | bytes 5308424 | tf_op jit(solution)/shard_map/ppermute | solution.py:32
  169.4 57.9 %collective-permute-start.12 = (bf16[512,2048]{1,0:T(8,128)(2,1)}, bf16[512,2048]{1,0:T(8,128)(2,1)}, u32[]{:S(2)}, u32[]{:S(2)}) collective-permute-start(bf16[512,2048]{1,0:T(8,128)(2,1)} %collective-permute-done.11.refs_13_.refs_14_), channel_id=1, source_target_pairs={{0,1},{1,0},{2,3},{3,2},{4,5},{5,4},{6,7},{7,6},{8,9},{9,8},{10,11... | collective-permute-start | bytes 6291464 | tf_op jit(solution)/shard_map/ppermute | solution.py:53
  246.0 3.8 collective-permute-start.27
  246.0 5.2 %collective-permute-start.28 = (bf16[24,2048]{1,0:T(8,128)(2,1)}, bf16[24,2048]{1,0:T(8,128)(2,1)S(1)}, u32[]{:S(2)}, u32[]{:S(2)}) collective-permute-start(bf16[24,2048]{1,0:T(8,128)(2,1)} %get-tuple-element.20), channel_id=1, source_target_pairs={{0,2},{1,5},{2,0},{3,7},{4,6},{5,1},{6,4},{7,3},{8,10},{9,13},{10,... | collective-permute-start | bytes 294920 | tf_op jit(solution)/shard_map/ppermute | solution.py:53
  247.6 4.9 %collective-permute-start.29 = (bf16[24,2048]{1,0:T(8,128)(2,1)}, bf16[24,2048]{1,0:T(8,128)(2,1)S(1)}, u32[]{:S(2)}, u32[]{:S(2)}) collective-permute-start(bf16[24,2048]{1,0:T(8,128)(2,1)} %get-tuple-element.20), channel_id=1, source_target_pairs={{0,4},{1,3},{2,6},{3,1},{4,0},{5,7},{6,2},{7,5},{8,12},{9,11},{10,... | collective-permute-start | bytes 294920 | tf_op jit(solution)/shard_map/ppermute | solution.py:53
  249.1 3.4 collective-permute-start.20
  249.2 5.4 %collective-permute-start.21 = (bf16[24,2048]{1,0:T(8,128)(2,1)S(1)}, bf16[24,2048]{1,0:T(8,128)(2,1)S(1)}, u32[]{:S(2)}, u32[]{:S(2)}) collective-permute-start(bf16[24,2048]{1,0:T(8,128)(2,1)S(1)} %copy-done.19), channel_id=1, source_target_pairs={{0,2},{1,5},{2,0},{3,7},{4,6},{5,1},{6,4},{7,3},{8,10},{9,13},{10,... | collective-permute-start | bytes 294920 | tf_op jit(solution)/shard_map/ppermute | solution.py:53
  249.8 5.4 %collective-permute-start.22 = (bf16[24,2048]{1,0:T(8,128)(2,1)S(1)}, bf16[24,2048]{1,0:T(8,128)(2,1)S(1)}, u32[]{:S(2)}, u32[]{:S(2)}) collective-permute-start(bf16[24,2048]{1,0:T(8,128)(2,1)S(1)} %copy-done.19), channel_id=1, source_target_pairs={{0,4},{1,3},{2,6},{3,1},{4,0},{5,7},{6,2},{7,5},{8,12},{9,11},{10,... | collective-permute-start | bytes 294920 | tf_op jit(solution)/shard_map/ppermute | solution.py:53
  251.2 6.0 %collective-permute-start.31 = (bf16[24,2048]{1,0:T(8,128)(2,1)S(1)}, bf16[24,2048]{1,0:T(8,128)(2,1)S(1)}, u32[]{:S(2)}, u32[]{:S(2)}) collective-permute-start(bf16[24,2048]{1,0:T(8,128)(2,1)S(1)} %collective-permute-done.28), channel_id=1, source_target_pairs={{0,1},{1,0},{2,3},{3,2},{4,5},{5,4},{6,7},{7,6},{8,9},{9,8},{10,11... | collective-permute-start | bytes 294920 | tf_op jit(solution)/shard_map/ppermute | solution.py:53
  252.5 4.6 %collective-permute-start.32 = (bf16[24,2048]{1,0:T(8,128)(2,1)S(1)}, bf16[24,2048]{1,0:T(8,128)(2,1)S(1)}, u32[]{:S(2)}, u32[]{:S(2)}) collective-permute-start(bf16[24,2048]{1,0:T(8,128)(2,1)S(1)} %collective-permute-done.29), channel_id=1, source_target_pairs={{0,2},{1,5},{2,0},{3,7},{4,6},{5,1},{6,4},{7,3},{8,10},{9,13},{10,... | collective-permute-start | bytes 294920 | tf_op jit(solution)/shard_map/ppermute | solution.py:53
  254.6 5.3 %collective-permute-start.24 = (bf16[24,2048]{1,0:T(8,128)(2,1)S(1)}, bf16[24,2048]{1,0:T(8,128)(2,1)S(1)}, u32[]{:S(2)}, u32[]{:S(2)}) collective-permute-start(bf16[24,2048]{1,0:T(8,128)(2,1)S(1)} %collective-permute-done.21), channel_id=1, source_target_pairs={{0,1},{1,0},{2,3},{3,2},{4,5},{5,4},{6,7},{7,6},{8,9},{9,8},{10,11... | collective-permute-start | bytes 294920 | tf_op jit(solution)/shard_map/ppermute | solution.py:53
  255.2 4.7 %collective-permute-start.25 = (bf16[24,2048]{1,0:T(8,128)(2,1)S(1)}, bf16[24,2048]{1,0:T(8,128)(2,1)S(1)}, u32[]{:S(2)}, u32[]{:S(2)}) collective-permute-start(bf16[24,2048]{1,0:T(8,128)(2,1)S(1)} %collective-permute-done.22), channel_id=1, source_target_pairs={{0,2},{1,5},{2,0},{3,7},{4,6},{5,1},{6,4},{7,3},{8,10},{9,13},{10,... | collective-permute-start | bytes 294920 | tf_op jit(solution)/shard_map/ppermute | solution.py:53
  267.2 5.1 %collective-permute-start.36 = (f32[96,96]{0,1:T(8,128)S(1)}, f32[96,96]{0,1:T(8,128)S(1)}, u32[]{:S(2)}, u32[]{:S(2)}) collective-permute-start(f32[96,96]{0,1:T(8,128)S(1)} %convolution_add_fusion), channel_id=1, source_target_pairs={{0,24},{8,0},{16,8},{24,16},{1,25},{9,1},{17,9},{25,17},{2,26},{10... | collective-permute-start | bytes 110600 | tf_op jit(solution)/shard_map/ppermute | solution.py:501
  267.3 7.2 %collective-permute-start.35 = (f32[96,96]{0,1:T(8,128)S(1)}, f32[96,96]{0,1:T(8,128)S(1)}, u32[]{:S(2)}, u32[]{:S(2)}) collective-permute-start(f32[96,96]{0,1:T(8,128)S(1)} %convolution_add_fusion), channel_id=1, source_target_pairs={{0,16},{8,24},{16,0},{24,8},{1,17},{9,25},{17,1},{25,9},{2,18},{10... | collective-permute-start | bytes 110600 | tf_op jit(solution)/shard_map/ppermute | solution.py:501
  268.3 6.2 %collective-permute-start.34 = (f32[96,96]{0,1:T(8,128)S(1)}, f32[96,96]{0,1:T(8,128)S(1)}, u32[]{:S(2)}, u32[]{:S(2)}) collective-permute-start(f32[96,96]{0,1:T(8,128)S(1)} %convolution_add_fusion), channel_id=1, source_target_pairs={{0,8},{8,16},{16,24},{24,0},{1,9},{9,17},{17,25},{25,1},{2,10},{10... | collective-permute-start | bytes 110600 | tf_op jit(solution)/shard_map/ppermute | solution.py:501
  287.3 15.8 %collective-permute-start.44 = (bf16[864,512]{1,0:T(8,128)(2,1)S(1)}, bf16[864,512]{1,0:T(8,128)(2,1)S(1)}, u32[]{:S(2)}, u32[]{:S(2)}) collective-permute-start(bf16[864,512]{1,0:T(8,128)(2,1)S(1)} %backward_first.3), channel_id=1, source_target_pairs={{24,16},{25,17},{26,18},{27,19},{28,20},{29,21},{30,22},{31,23}} | collective-permute-start | bytes 2654216 | tf_op jit(solution)/shard_map/ppermute | solution.py:439
  288.0 21.6 %collective-permute-start.45 = (bf16[864,512]{1,0:T(8,128)(2,1)S(1)}, bf16[864,512]{1,0:T(8,128)(2,1)S(1)}, u32[]{:S(2)}, u32[]{:S(2)}) collective-permute-start(bf16[864,512]{1,0:T(8,128)(2,1)S(1)} %backward_first.3), channel_id=1, source_target_pairs={{0,8},{1,9},{2,10},{3,11},{4,12},{5,13},{6,14},{7,15}} | collective-permute-start | bytes 2654216 | tf_op jit(solution)/shard_map/ppermute | solution.py:440
  301.0 22.3 %collective-permute-start.50 = (bf16[864,512]{1,0:T(8,128)(2,1)}, bf16[864,512]{1,0:T(8,128)(2,1)S(1)}, u32[]{:S(2)}, u32[]{:S(2)}) collective-permute-start(bf16[864,512]{1,0:T(8,128)(2,1)} %get-tuple-element.25), channel_id=1, source_target_pairs={{24,16},{25,17},{26,18},{27,19},{28,20},{29,21},{30,22},{31,23}} | collective-permute-start | bytes 2654216 | tf_op jit(solution)/shard_map/ppermute | solution.py:439
  301.7 27.0 %collective-permute-start.51 = (bf16[864,512]{1,0:T(8,128)(2,1)}, bf16[864,512]{1,0:T(8,128)(2,1)S(1)}, u32[]{:S(2)}, u32[]{:S(2)}) collective-permute-start(bf16[864,512]{1,0:T(8,128)(2,1)} %get-tuple-element.25), channel_id=1, source_target_pairs={{0,8},{1,9},{2,10},{3,11},{4,12},{5,13},{6,14},{7,15}} | collective-permute-start | bytes 2654216 | tf_op jit(solution)/shard_map/ppermute | solution.py:440
  317.5 25.4 %collective-permute-start.46 = (bf16[864,512]{1,0:T(8,128)(2,1)S(1)}, bf16[864,512]{1,0:T(8,128)(2,1)S(1)}, u32[]{:S(2)}, u32[]{:S(2)}) collective-permute-start(bf16[864,512]{1,0:T(8,128)(2,1)S(1)} %backward_part.7), channel_id=1, source_target_pairs={{16,8},{24,16},{17,9},{25,17},{18,10},{26,18},{19,11},{27,19},{20,... | collective-permute-start | bytes 2654216 | tf_op jit(solution)/shard_map/ppermute | solution.py:439
  318.2 29.3 %collective-permute-start.47 = (bf16[864,512]{1,0:T(8,128)(2,1)S(1)}, bf16[864,512]{1,0:T(8,128)(2,1)S(1)}, u32[]{:S(2)}, u32[]{:S(2)}) collective-permute-start(bf16[864,512]{1,0:T(8,128)(2,1)S(1)} %backward_part.7), channel_id=1, source_target_pairs={{0,8},{8,16},{1,9},{9,17},{2,10},{10,18},{3,11},{11,19},{4,12},{12... | collective-permute-start | bytes 2654216 | tf_op jit(solution)/shard_map/ppermute | solution.py:440
  336.6 28.7 %collective-permute-start.52 = (bf16[864,512]{1,0:T(8,128)(2,1)S(1)}, bf16[864,512]{1,0:T(8,128)(2,1)S(1)}, u32[]{:S(2)}, u32[]{:S(2)}) collective-permute-start(bf16[864,512]{1,0:T(8,128)(2,1)S(1)} %backward_part.10), channel_id=1, source_target_pairs={{16,8},{24,16},{17,9},{25,17},{18,10},{26,18},{19,11},{27,19},{20,... | collective-permute-start | bytes 2654216 | tf_op jit(solution)/shard_map/ppermute | solution.py:439
  337.3 29.2 %collective-permute-start.53 = (bf16[864,512]{1,0:T(8,128)(2,1)S(1)}, bf16[864,512]{1,0:T(8,128)(2,1)S(1)}, u32[]{:S(2)}, u32[]{:S(2)}) collective-permute-start(bf16[864,512]{1,0:T(8,128)(2,1)S(1)} %backward_part.10), channel_id=1, source_target_pairs={{0,8},{8,16},{1,9},{9,17},{2,10},{10,18},{3,11},{11,19},{4,12},{12... | collective-permute-start | bytes 2654216 | tf_op jit(solution)/shard_map/ppermute | solution.py:440
  359.6 39.8 %collective-permute-start.49 = (bf16[864,512]{1,0:T(8,128)(2,1)S(1)}, bf16[864,512]{1,0:T(8,128)(2,1)S(1)}, u32[]{:S(2)}, u32[]{:S(2)}) collective-permute-start(bf16[864,512]{1,0:T(8,128)(2,1)S(1)} %get-tuple-element.24), channel_id=1, source_target_pairs={{0,8},{8,16},{16,24},{1,9},{9,17},{17,25},{2,10},{10,18},{18,26},{... | collective-permute-start | bytes 2654216 | tf_op jit(solution)/shard_map/ppermute | solution.py:440
  363.9 35.5 %collective-permute-start.48 = (bf16[864,512]{1,0:T(8,128)(2,1)S(1)}, bf16[864,512]{1,0:T(8,128)(2,1)S(1)}, u32[]{:S(2)}, u32[]{:S(2)}) collective-permute-start(bf16[864,512]{1,0:T(8,128)(2,1)S(1)} %get-tuple-element.23), channel_id=1, source_target_pairs={{8,0},{16,8},{24,16},{9,1},{17,9},{25,17},{10,2},{18,10},{26,18},{... | collective-permute-start | bytes 2654216 | tf_op jit(solution)/shard_map/ppermute | solution.py:439
  378.5 24.0 %collective-permute-start.55 = (bf16[864,512]{1,0:T(8,128)(2,1)S(1)}, bf16[864,512]{1,0:T(8,128)(2,1)S(1)}, u32[]{:S(2)}, u32[]{:S(2)}) collective-permute-start(bf16[864,512]{1,0:T(8,128)(2,1)S(1)} %get-tuple-element.27), channel_id=1, source_target_pairs={{0,8},{8,16},{16,24},{1,9},{9,17},{17,25},{2,10},{10,18},{18,26},{... | collective-permute-start | bytes 2654216 | tf_op jit(solution)/shard_map/ppermute | solution.py:440
  383.0 21.0 %collective-permute-start.54 = (bf16[864,512]{1,0:T(8,128)(2,1)S(1)}, bf16[864,512]{1,0:T(8,128)(2,1)S(1)}, u32[]{:S(2)}, u32[]{:S(2)}) collective-permute-start(bf16[864,512]{1,0:T(8,128)(2,1)S(1)} %get-tuple-element.26), channel_id=1, source_target_pairs={{8,0},{16,8},{24,16},{9,1},{17,9},{25,17},{10,2},{18,10},{26,18},{... | collective-permute-start | bytes 2654216 | tf_op jit(solution)/shard_map/ppermute | solution.py:439
  (31 other events, 907.0 us)

commit v4 on v3

--- a/solution.py
+++ b/solution.py
@@ -40,7 +40,7 @@
     return chip_grid(n_rows) == (2, 2) and n_rows == CORES * n_vocab
 
 
-def row_gather(block, n_rows, n_vocab):
+def row_gather(block, n_rows, n_vocab, late=False):
     if not two_paths(n_rows, n_vocab):
         whole = lax.all_gather(block, "rows", axis=0)
         return [whole[r] for r in range(n_rows)]
@@ -59,6 +59,8 @@
     main_twin = move(by_main, twin)
     side_twin = move(by_side, twin)
     far_twin = move(far, twin)
+    if late:
+        block, side_twin = lax.optimization_barrier((block, side_twin))
     return [block, own_twin, by_main, side_twin, by_side, main_twin, far, far_twin]
 
 
@@ -440,8 +442,12 @@
             right[i] = lax.ppermute(to_right, "vocab", [(d, d + 1) for d in range(step)])
     terms = []
     for i in range(share):
-        own = product(f"own_{i}", (), ((),))[0]
-        terms.append(own.astype(jnp.float32) + left[i].astype(jnp.float32) + right[i].astype(jnp.float32))
+        early = i + 1 < share
+        running = (left[i], right[i]) if early else ()
+        own = product(f"own_{i}", running, (tuple(range(len(running))),))[0]
+        if not early:
+            own = own.astype(jnp.float32) + left[i].astype(jnp.float32) + right[i].astype(jnp.float32)
+        terms.append(own.astype(jnp.bfloat16))
     return terms
 
 
@@ -488,7 +494,7 @@
     for i in range(halves):
         pool = (logits[i], mask, groups, pass_rows, width, i * part_width, filled)
         *filled, sparse = forward(found, parts[i], plan, plans.at["last"], half, pool=pool)
-        gathered.append(jnp.stack(row_gather(sparse, n_rows, n_vocab)))
+        gathered.append(jnp.stack(row_gather(sparse, n_rows, n_vocab, late=True)))
     slopes, totals = filled
     all_pass = [block[:, :groups].reshape(-1, part_width) for block in gathered]
     all_query = [block[:, groups:].reshape(-1, part_width) for block in gathered]
@@ -537,7 +543,7 @@
         return backward(logit_grad[0], parts, plan, plans.at[name], running, adds)
 
     summed = line_reduce_scatter(first, product, n_vocab, share)
-    summed = jnp.concatenate(summed, axis=1).astype(jnp.bfloat16)
+    summed = jnp.concatenate(summed, axis=1)
     return (
         summed[:pass_rows].reshape(groups, pass_length, part),
         summed[pass_rows:].reshape(groups, query_length, part),

time: 407 us -> 404 us (level)
  waiting for transfers between devices: 185 us -> 173 us
  starting transfers between devices: 61.2 us -> 66.3 us
    ppermute x35, waiting for transfers between devices: 131 us -> 98.4 us  [move(): return lax.ppermute(value, 'rows', pairs)]
    ppermute x3, waiting for transfers between devices: 0.01 us -> 31.2 us  [line_gather(): lax.ppermute(right, 'vocab', [(z, z + 1) for z in range(step - 1, n - 1)])]
    ppermute x3, waiting for transfers between devices: 29 us -> 18.8 us  [line_gather(): lax.ppermute(left, 'vocab', [(z, z - 1) for z in range(1, n - step + 1)])]
  transfers between devices with their start and end apart: 56 -> 56, of which waited for: 28 -> 24; matrix products, arithmetic and copies ran while one was open for 2% -> 2% of each run, Pallas kernels for 27% -> 32%
where the time goes in v4:
time: 404 us; the launch traced here: 403 us
  waiting for transfers between devices  173 us (43%)
  Pallas kernels  136 us (34%)
  starting transfers between devices  66.3 us (16%)
  local copies, waits for them, and re-layouts  16.7 us (4%)
  other arithmetic  5.9 us (1%)
    ppermute x35, waiting for transfers between devices, move(): return lax.ppermute(value, 'rows', pairs)  98.4 us
    pallas_call x4, Pallas kernels, forward(): pl.pallas_call(functools.partial(forward_kernel, spec), out_shape=out_sha...  60.5 us
    pallas_call x6, Pallas kernels, backward(): pl.pallas_call(functools.partial(backward_kernel, (at, count, spans(group...  55.5 us
    ppermute x3, waiting for transfers between devices, line_gather(): lax.ppermute(right, 'vocab', [(z, z + 1) for z in range(step - 1, n - 1)])  31.2 us
    ppermute x6, starting transfers between devices, line_reduce_scatter(): lax.ppermute(to_right, 'vocab', [(d, d + 1) for d in range(step)])  22.9 us
    ppermute x35, starting transfers between devices, move(): return lax.ppermute(value, 'rows', pairs)  22.7 us
    pallas_call x2, Pallas kernels, backward_first(): pl.pallas_call(functools.partial(first_kernel, (at, count, spans(parts),...  20.4 us
    ppermute x6, waiting for transfers between devices, line_reduce_scatter(): lax.ppermute(to_right, 'vocab', [(d, d + 1) for d in range(step)])  20.2 us
  transfers between devices with their start and end apart: 56, of which 24 were waited for; matrix products, arithmetic and copies ran while one was open for 2% of the time, Pallas kernels for 32%

profile of v4, /device:TPU:0, one launch (start us, length us, event | category | flops | bytes accessed | tf_op | source)
XLA Modules:
  0.0 403.4 jit_solution(10653597099610549476)
XLA Ops:
  0.6 1.7 pad_maximum_fusion.refs_2_.refs_3_
  2.3 5.3 %collective-permute-start = (bf16[864,1024]{1,0:T(8,128)(2,1)S(1)}, bf16[864,1024]{1,0:T(8,128)(2,1)S(1)}, u32[]{:S(2)}, u32[]{:S(2)}) collective-permute-start(bf16[864,1024]{1,0:T(8,128)(2,1)S(1)} %pad_maximum_fusion.refs_2_.refs_3_), channel_id=1, source_target_pairs={{0,8},{8,16},{16,24},{1,9},{9,17},{17,25},{2,10},{10,18},{18,26},{... | collective-permute-start | bytes 5308424 | tf_op jit(solution)/shard_map/ppermute | solution.py:33
  7.7 1.7 slice.40.refs_5_.refs_7_.refs_8_
  10.8 1.6 collective-permute-start.7
  12.4 1.5 collective-permute-start.8
  14.2 31.2 %collective-permute-done.refs_1_.refs_2_ = bf16[864,1024]{1,0:T(8,128)(2,1)S(1)} collective-permute-done((bf16[864,1024]{1,0:T(8,128)(2,1)S(1)}, bf16[864,1024]{1,0:T(8,128)(2,1)S(1)}, u32[]{:S(2)}, u32[]{:S(2)}) %collective-permute-start) | collective-permute-done | bytes 1769504 | tf_op jit(solution)/shard_map/ppermute | solution.py:33
  45.4 7.0 %collective-permute-done.3.refs_3_.refs_4_ = bf16[864,1024]{1,0:T(8,128)(2,1)S(1)} collective-permute-done((bf16[864,1024]{1,0:T(8,128)(2,1)S(1)}, bf16[864,1024]{1,0:T(8,128)(2,1)S(1)}, u32[]{:S(2)}, u32[]{:S(2)}) %collective-permute-start.3) | collective-permute-done | bytes 1769504 | tf_op jit(solution)/shard_map/ppermute | solution.py:32
  52.4 1.5 collective-permute-start.15
  55.4 3.2 collective-permute-done.7.refs_7_.refs_9_.refs_10_
  58.6 1.9 collective-permute-start.1
  62.3 41.6 %collective-permute-done.15.refs_9_.refs_11_.refs_4_ = bf16[512,2048]{1,0:T(8,128)(2,1)S(1)} collective-permute-done((bf16[512,2048]{1,0:T(8,128)(2,1)S(1)}, bf16[512,2048]{1,0:T(8,128)(2,1)S(1)}, u32[]{:S(2)}, u32[]{:S(2)}) %collective-permute-start.15) | collective-permute-done | bytes 2097184 | tf_op jit(solution)/shard_map/ppermute | solution.py:53
  107.3 22.7 %collective-permute-done.18.refs_13_.refs_6_ = bf16[512,2048]{1,0:T(8,128)(2,1)} collective-permute-done((bf16[512,2048]{1,0:T(8,128)(2,1)S(1)}, bf16[512,2048]{1,0:T(8,128)(2,1)}, u32[]{:S(2)}, u32[]{:S(2)}) %collective-permute-start.18) | collective-permute-done | bytes 2097184 | tf_op jit(solution)/shard_map/ppermute | solution.py:53
  130.0 1.9 collective-permute-start.2
  131.9 20.5 %collective-permute-done.11.refs_13_.refs_14_ = bf16[512,2048]{1,0:T(8,128)(2,1)S(1)} collective-permute-done((bf16[512,2048]{1,0:T(8,128)(2,1)S(1)}, bf16[512,2048]{1,0:T(8,128)(2,1)S(1)}, u32[]{:S(2)}, u32[]{:S(2)}) %collective-permute-start.11) | collective-permute-done | bytes 2097184 | tf_op jit(solution)/shard_map/ppermute | solution.py:53
  155.5 12.7 %forward_part.2.refs_15_ = f32[864,2048]{1,0:T(8,128)} custom-call(s32[42]{0:T(128)} %get-tuple-element.47.plan_ref, bf16[864,1024]{1,0:T(8,128)(2,1)} %collective-permute-done.1.refs_0_.refs_1_, bf16[864,1024]{1,0:T(8,128)(2,1)} %copy-done.19, bf16[864,1024]{1,0:T(8,128)(2,1)} %copy-done.18, bf16[864,1024]{1,0:T(8,128)(2,1)} %copy-done.20, ...), custom_call_target="tpu_custom_call" | custom-call | flops 7247757312 | bytes 22544384 | tf_op jit(solution)/shard_map/forward_part/pallas_call | solution.py:233
  168.8 12.6 %forward_part.3.refs_15_ = f32[864,2048]{1,0:T(8,128)} custom-call(s32[42]{0:T(128)} %get-tuple-element.47.plan_ref, bf16[864,1024]{1,0:T(8,128)(2,1)} %collective-permute-done.1.refs_0_.refs_1_, bf16[864,1024]{1,0:T(8,128)(2,1)} %copy-done.19, bf16[864,1024]{1,0:T(8,128)(2,1)} %copy-done.18, bf16[864,1024]{1,0:T(8,128)(2,1)} %copy-done.20, ...), custom_call_target="tpu_custom_call" | custom-call | flops 7247757312 | bytes 22544384 | tf_op jit(solution)/shard_map/forward_part/pallas_call | solution.py:233
  181.4 1.6 collective-permute-start.38
  183.0 11.8 %collective-permute-done.5.refs_6_ = bf16[864,1024]{1,0:T(8,128)(2,1)} collective-permute-done((bf16[864,1024]{1,0:T(8,128)(2,1)}, bf16[864,1024]{1,0:T(8,128)(2,1)}, u32[]{:S(2)}, u32[]{:S(2)}) %collective-permute-start.5) | collective-permute-done | bytes 1769504 | tf_op jit(solution)/shard_map/ppermute | solution.py:32
  196.9 17.5 %forward_final.2 = (bf16[864,4096]{1,0:T(8,128)(2,1)}, f32[24,4096]{1,0:T(8,128)}, bf16[24,2048]{1,0:T(8,128)(2,1)}) custom-call(s32[42]{0:T(128)} %get-tuple-element.47.plan_ref, bf16[864,1024]{1,0:T(8,128)(2,1)} %collective-permute-done.2.refs_0_, bf16[864,1024]{1,0:T(8,128)(2,1)} %collective-permute-done.1.refs_0_.refs_1_, bf16[864,1024]{1,0:T(8,128)(2,1)} %copy-done.19, ...), custom_call_target="tpu_custom_call" | custom-call | flops 7247757312 | bytes 22544384 | tf_op jit(solution)/shard_map/forward_final/pallas_call | solution.py:233
  214.4 17.7 %forward_final.3 = (bf16[864,4096]{1,0:T(8,128)(2,1)}, f32[24,4096]{1,0:T(8,128)}, bf16[24,2048]{1,0:T(8,128)(2,1)}) custom-call(s32[42]{0:T(128)} %get-tuple-element.47.plan_ref, bf16[864,1024]{1,0:T(8,128)(2,1)} %collective-permute-done.2.refs_0_, ...), custom_call_target="tpu_custom_call", output_to_operand_aliasing={{0}: (18, {}), {1}: (19, {})} | custom-call | flops 7247757312 | bytes 22544384 | tf_op jit(solution)/shard_map/forward_final/pallas_call | solution.py:233
  234.2 2.8 collective-permute-done.27
  237.7 1.5 collective-permute-start.42
  239.2 2.1 collective-permute-done.42
  249.4 1.9 collective-permute-done.32
  256.1 1.9 reshape.78
  263.1 1.6 collective-permute-done.36
  264.7 2.2 collective-permute-done.35
  269.1 1.6 copy-done.9
  270.7 1.6 copy-done.11
  272.3 1.6 copy-done.13
  273.9 1.6 copy-done.15
  275.4 9.1 %backward_first.3 = bf16[864,512]{1,0:T(8,128)(2,1)S(1)} custom-call(s32[42]{0:T(128)S(1)} %copy-done.16, bf16[864,4096]{1,0:T(8,128)(2,1)} %get-tuple-element.22.slope_ref, f32[12,4096]{1,0:T(8,128)S(1)} %get-tuple-element.45.pass_ref, f32[12,4096]{1,0:T(8,128)S(1)} %get-tuple-element.44.query_ref, bf16[512,2048]{1,0:T(8,128)(2,1)S(1)} %copy-done.3, ...), custom_call_target="tpu_custom_call" | custom-call | flops 3623878656 | bytes 19234816 | tf_op jit(solution)/shard_map/backward_first/pallas_call | solution.py:325
  285.2 1.6 collective-permute-start.45
  286.9 11.3 %backward_first.2 = (bf16[864,4096]{1,0:T(8,128)(2,1)}, bf16[864,512]{1,0:T(8,128)(2,1)}) custom-call(s32[42]{0:T(128)S(1)} %copy-done.16, bf16[864,4096]{1,0:T(8,128)(2,1)} %get-tuple-element.22.slope_ref, f32[12,4096]{1,0:T(8,128)S(1)} %get-tuple-element.45.pass_ref, f32[12,4096]{1,0:T(8,128)S(1)} %get-tuple-element.44.query_ref, ...), custom_call_target="tpu_custom_call" | custom-call | flops 3623878656 | bytes 19234816 | tf_op jit(solution)/shard_map/backward_first/pallas_call | solution.py:325
  300.3 6.5 %collective-permute-done.45.refs_17_ = bf16[864,512]{1,0:T(8,128)(2,1)S(1)} collective-permute-done((bf16[864,512]{1,0:T(8,128)(2,1)S(1)}, bf16[864,512]{1,0:T(8,128)(2,1)S(1)}, u32[]{:S(2)}, u32[]{:S(2)}) %collective-permute-start.45) | collective-permute-done | bytes 884768 | tf_op jit(solution)/shard_map/ppermute | solution.py:442
  306.8 7.9 %backward_part.6 = bf16[864,512]{1,0:T(8,128)(2,1)S(1)} custom-call(s32[42]{0:T(128)S(1)} %copy-done.16, bf16[864,4096]{1,0:T(8,128)(2,1)} %get-tuple-element.30.slopes_ref, bf16[512,2048]{1,0:T(8,128)(2,1)S(1)} %copy-done.3, bf16[512,2048]{1,0:T(8,128)(2,1)} %collective-permute-done.13.refs_6_.refs_8_.refs_1_, ...), custom_call_target="tpu_custom_call" | custom-call | flops 3623878656 | bytes 12156928 | tf_op jit(solution)/shard_map/backward_part/pallas_call | solution.py:407
  315.5 5.0 %collective-permute-start.47 = (bf16[864,512]{1,0:T(8,128)(2,1)S(1)}, bf16[864,512]{1,0:T(8,128)(2,1)S(1)}, u32[]{:S(2)}, u32[]{:S(2)}) collective-permute-start(bf16[864,512]{1,0:T(8,128)(2,1)S(1)} %backward_part.6), channel_id=1, source_target_pairs={{0,8},{8,16},{1,9},{9,17},{2,10},{10,18},{3,11},{11,19},{4,12},{12... | collective-permute-start | bytes 2654216 | tf_op jit(solution)/shard_map/ppermute | solution.py:442
  320.5 5.4 %collective-permute-done.51.refs_17_ = bf16[864,512]{1,0:T(8,128)(2,1)S(1)} collective-permute-done((bf16[864,512]{1,0:T(8,128)(2,1)}, bf16[864,512]{1,0:T(8,128)(2,1)S(1)}, u32[]{:S(2)}, u32[]{:S(2)}) %collective-permute-start.51) | collective-permute-done | bytes 884768 | tf_op jit(solution)/shard_map/ppermute | solution.py:442
  325.9 7.9 %backward_part.10 = bf16[864,512]{1,0:T(8,128)(2,1)S(1)} custom-call(s32[42]{0:T(128)S(1)} %copy-done.16, bf16[864,4096]{1,0:T(8,128)(2,1)} %get-tuple-element.30.slopes_ref, bf16[512,2048]{1,0:T(8,128)(2,1)S(1)} %copy-done.3, bf16[512,2048]{1,0:T(8,128)(2,1)} %collective-permute-done.13.refs_6_.refs_8_.refs_1_, ...), custom_call_target="tpu_custom_call" | custom-call | flops 3623878656 | bytes 12156928 | tf_op jit(solution)/shard_map/backward_part/pallas_call | solution.py:407
  334.5 5.6 %collective-permute-start.53 = (bf16[864,512]{1,0:T(8,128)(2,1)S(1)}, bf16[864,512]{1,0:T(8,128)(2,1)S(1)}, u32[]{:S(2)}, u32[]{:S(2)}) collective-permute-start(bf16[864,512]{1,0:T(8,128)(2,1)S(1)} %backward_part.10), channel_id=1, source_target_pairs={{0,8},{8,16},{1,9},{9,17},{2,10},{10,18},{3,11},{11,19},{4,12},{12... | collective-permute-start | bytes 2654216 | tf_op jit(solution)/shard_map/ppermute | solution.py:442
  340.1 4.6 %collective-permute-done.47.refs_17_ = bf16[864,512]{1,0:T(8,128)(2,1)S(1)} collective-permute-done((bf16[864,512]{1,0:T(8,128)(2,1)S(1)}, bf16[864,512]{1,0:T(8,128)(2,1)S(1)}, u32[]{:S(2)}, u32[]{:S(2)}) %collective-permute-start.47) | collective-permute-done | bytes 884768 | tf_op jit(solution)/shard_map/ppermute | solution.py:442
  344.7 12.1 %backward_part.7 = (bf16[864,512]{1,0:T(8,128)(2,1)S(1)}, bf16[864,512]{1,0:T(8,128)(2,1)S(1)}) custom-call(s32[42]{0:T(128)S(1)} %copy-done.16, bf16[864,4096]{1,0:T(8,128)(2,1)} %get-tuple-element.30.slopes_ref, bf16[512,2048]{1,0:T(8,128)(2,1)S(1)} %copy-done.3, bf16[512,2048]{1,0:T(8,128)(2,1)} %collective-permute-done.13.refs_6_.refs_8_.refs_1_, ...), custom_call_target="tpu_custom_call" | custom-call | flops 7247757312 | bytes 17235968 | tf_op jit(solution)/shard_map/backward_part/pallas_call | solution.py:407
  358.1 4.9 %collective-permute-start.49 = (bf16[864,512]{1,0:T(8,128)(2,1)S(1)}, bf16[864,512]{1,0:T(8,128)(2,1)S(1)}, u32[]{:S(2)}, u32[]{:S(2)}) collective-permute-start(bf16[864,512]{1,0:T(8,128)(2,1)S(1)} %get-tuple-element.32), channel_id=1, source_target_pairs={{0,8},{8,16},{16,24},{1,9},{9,17},{17,25},{2,10},{10,18},{18,26},{... | collective-permute-start | bytes 2654216 | tf_op jit(solution)/shard_map/ppermute | solution.py:442
  363.7 12.1 %backward_part.11 = (bf16[864,512]{1,0:T(8,128)(2,1)S(1)}, bf16[864,512]{1,0:T(8,128)(2,1)S(1)}) custom-call(s32[42]{0:T(128)S(1)} %copy-done.16, bf16[864,4096]{1,0:T(8,128)(2,1)} %get-tuple-element.30.slopes_ref, bf16[512,2048]{1,0:T(8,128)(2,1)S(1)} %copy-done.3, bf16[512,2048]{1,0:T(8,128)(2,1)} %collective-permute-done.13.refs_6_.refs_8_.refs_1_, ...), custom_call_target="tpu_custom_call" | custom-call | flops 7247757312 | bytes 17235968 | tf_op jit(solution)/shard_map/backward_part/pallas_call | solution.py:407
  375.8 4.4 %collective-permute-start.55 = (bf16[864,512]{1,0:T(8,128)(2,1)S(1)}, bf16[864,512]{1,0:T(8,128)(2,1)S(1)}, u32[]{:S(2)}, u32[]{:S(2)}) collective-permute-start(bf16[864,512]{1,0:T(8,128)(2,1)S(1)} %get-tuple-element.35), channel_id=1, source_target_pairs={{0,8},{8,16},{16,24},{1,9},{9,17},{17,25},{2,10},{10,18},{18,26},{... | collective-permute-start | bytes 2654216 | tf_op jit(solution)/shard_map/ppermute | solution.py:442
  381.5 7.8 %backward_part.9 = bf16[864,512]{1,0:T(8,128)(2,1)S(1)} custom-call(s32[42]{0:T(128)S(1)} %copy-done.16, bf16[864,4096]{1,0:T(8,128)(2,1)} %get-tuple-element.30.slopes_ref, bf16[512,2048]{1,0:T(8,128)(2,1)S(1)} %copy-done.3, bf16[512,2048]{1,0:T(8,128)(2,1)} %collective-permute-done.13.refs_6_.refs_8_.refs_1_, ...), custom_call_target="tpu_custom_call" | custom-call | flops 3623878656 | bytes 12156928 | tf_op jit(solution)/shard_map/backward_part/pallas_call | solution.py:407
  389.3 7.8 %backward_part.8 = bf16[864,512]{1,0:T(8,128)(2,1)S(1)} custom-call(s32[42]{0:T(128)S(1)} %copy-done.16, bf16[864,4096]{1,0:T(8,128)(2,1)} %get-tuple-element.30.slopes_ref, bf16[512,2048]{1,0:T(8,128)(2,1)S(1)} %copy-done.3, bf16[512,2048]{1,0:T(8,128)(2,1)} %collective-permute-done.13.refs_6_.refs_8_.refs_1_, ...), custom_call_target="tpu_custom_call" | custom-call | flops 3623878656 | bytes 12156928 | tf_op jit(solution)/shard_map/backward_part/pallas_call | solution.py:407
  397.1 3.0 collective-permute-done.55
  (178 shorter events, 47.6 us)
Async XLA Ops:
  2.3 43.1 %collective-permute-start = (bf16[864,1024]{1,0:T(8,128)(2,1)S(1)}, bf16[864,1024]{1,0:T(8,128)(2,1)S(1)}, u32[]{:S(2)}, u32[]{:S(2)}) collective-permute-start(bf16[864,1024]{1,0:T(8,128)(2,1)S(1)} %pad_maximum_fusion.refs_2_.refs_3_), channel_id=1, source_target_pairs={{0,8},{8,16},{16,24},{1,9},{9,17},{17,25},{2,10},{10,18},{18,26},{... | collective-permute-start | bytes 5308424 | tf_op jit(solution)/shard_map/ppermute | solution.py:33
  9.4 44.5 %collective-permute-start.6 = (bf16[512,2048]{1,0:T(8,128)(2,1)S(1)}, bf16[512,2048]{1,0:T(8,128)(2,1)S(1)}, u32[]{:S(2)}, u32[]{:S(2)}) collective-permute-start(bf16[512,2048]{1,0:T(8,128)(2,1)S(1)} %slice.40.refs_5_.refs_7_.refs_8_), channel_id=1, source_target_pairs={{0,1},{1,0},{2,3},{3,2},{4,5},{5,4},{6,7},{7,6},{8,9},{9,8},{10,11... | collective-permute-start | bytes 6291464 | tf_op jit(solution)/shard_map/ppermute | solution.py:53
  9.5 42.9 %collective-permute-start.3 = (bf16[864,1024]{1,0:T(8,128)(2,1)S(1)}, bf16[864,1024]{1,0:T(8,128)(2,1)S(1)}, u32[]{:S(2)}, u32[]{:S(2)}) collective-permute-start(bf16[864,1024]{1,0:T(8,128)(2,1)S(1)} %pad_maximum_fusion.refs_2_.refs_3_), channel_id=1, source_target_pairs={{8,0},{16,8},{24,16},{9,1},{17,9},{25,17},{10,2},{18,10},{26,18},{... | collective-permute-start | bytes 5308424 | tf_op jit(solution)/shard_map/ppermute | solution.py:32
  10.8 47.8 %collective-permute-start.7 = (bf16[512,2048]{1,0:T(8,128)(2,1)S(1)}, bf16[512,2048]{1,0:T(8,128)(2,1)S(1)}, u32[]{:S(2)}, u32[]{:S(2)}) collective-permute-start(bf16[512,2048]{1,0:T(8,128)(2,1)S(1)} %slice.40.refs_5_.refs_7_.refs_8_), channel_id=1, source_target_pairs={{0,2},{1,5},{2,0},{3,7},{4,6},{5,1},{6,4},{7,3},{8,10},{9,13},{10,... | collective-permute-start | bytes 6291464 | tf_op jit(solution)/shard_map/ppermute | solution.py:53
  12.4 48.5 %collective-permute-start.8 = (bf16[512,2048]{1,0:T(8,128)(2,1)S(1)}, bf16[512,2048]{1,0:T(8,128)(2,1)S(1)}, u32[]{:S(2)}, u32[]{:S(2)}) collective-permute-start(bf16[512,2048]{1,0:T(8,128)(2,1)S(1)} %slice.40.refs_5_.refs_7_.refs_8_), channel_id=1, source_target_pairs={{0,4},{1,3},{2,6},{3,1},{4,0},{5,7},{6,2},{7,5},{8,12},{9,11},{10,... | collective-permute-start | bytes 6291464 | tf_op jit(solution)/shard_map/ppermute | solution.py:53
  45.4 16.8 %collective-permute-start.13 = (bf16[512,2048]{1,0:T(8,128)(2,1)S(1)}, bf16[512,2048]{1,0:T(8,128)(2,1)}, u32[]{:S(2)}, u32[]{:S(2)}) collective-permute-start(bf16[512,2048]{1,0:T(8,128)(2,1)S(1)} %slice.41.refs_5_.refs_7_.refs_0_), channel_id=1, source_target_pairs={{0,1},{1,0},{2,3},{3,2},{4,5},{5,4},{6,7},{7,6},{8,9},{9,8},{10,11... | collective-permute-start | bytes 6291464 | tf_op jit(solution)/shard_map/ppermute | solution.py:53
  52.4 51.4 %collective-permute-start.15 = (bf16[512,2048]{1,0:T(8,128)(2,1)S(1)}, bf16[512,2048]{1,0:T(8,128)(2,1)S(1)}, u32[]{:S(2)}, u32[]{:S(2)}) collective-permute-start(bf16[512,2048]{1,0:T(8,128)(2,1)S(1)} %slice.41.refs_5_.refs_7_.refs_0_), channel_id=1, source_target_pairs={{0,4},{1,3},{2,6},{3,1},{4,0},{5,7},{6,2},{7,5},{8,12},{9,11},{10,... | collective-permute-start | bytes 6291464 | tf_op jit(solution)/shard_map/ppermute | solution.py:53
  53.9 51.4 %collective-permute-start.14 = (bf16[512,2048]{1,0:T(8,128)(2,1)S(1)}, bf16[512,2048]{1,0:T(8,128)(2,1)}, u32[]{:S(2)}, u32[]{:S(2)}) collective-permute-start(bf16[512,2048]{1,0:T(8,128)(2,1)S(1)} %slice.41.refs_5_.refs_7_.refs_0_), channel_id=1, source_target_pairs={{0,2},{1,5},{2,0},{3,7},{4,6},{5,1},{6,4},{7,3},{8,10},{9,13},{10,... | collective-permute-start | bytes 6291464 | tf_op jit(solution)/shard_map/ppermute | solution.py:53
  58.6 46.7 %collective-permute-start.1 = (bf16[864,1024]{1,0:T(8,128)(2,1)S(1)}, bf16[864,1024]{1,0:T(8,128)(2,1)}, u32[]{:S(2)}, u32[]{:S(2)}) collective-permute-start(bf16[864,1024]{1,0:T(8,128)(2,1)S(1)} %collective-permute-done.refs_1_.refs_2_), channel_id=1, source_target_pairs={{8,16},{16,24},{9,17},{17,25},{10,18},{18,26},{11,19},{19,27},{12,... | collective-permute-start | bytes 5308424 | tf_op jit(solution)/shard_map/ppermute | solution.py:33
  60.9 45.9 %collective-permute-start.4 = (bf16[864,1024]{1,0:T(8,128)(2,1)S(1)}, bf16[864,1024]{1,0:T(8,128)(2,1)}, u32[]{:S(2)}, u32[]{:S(2)}) collective-permute-start(bf16[864,1024]{1,0:T(8,128)(2,1)S(1)} %collective-permute-done.3.refs_3_.refs_4_), channel_id=1, source_target_pairs={{8,0},{16,8},{9,1},{17,9},{10,2},{18,10},{11,3},{19,11},{12,4},{20... | collective-permute-start | bytes 5308424 | tf_op jit(solution)/shard_map/ppermute | solution.py:32
  62.2 44.9 %collective-permute-start.9 = (bf16[512,2048]{1,0:T(8,128)(2,1)S(1)}, bf16[512,2048]{1,0:T(8,128)(2,1)S(1)}, u32[]{:S(2)}, u32[]{:S(2)}) collective-permute-start(bf16[512,2048]{1,0:T(8,128)(2,1)S(1)} %collective-permute-done.8.refs_9_.refs_11_.refs_12_), channel_id=1, source_target_pairs={{0,1},{1,0},{2,3},{3,2},{4,5},{5,4},{6,7},{7,6},{8,9},{9,8},{10,11... | collective-permute-start | bytes 6291464 | tf_op jit(solution)/shard_map/ppermute | solution.py:53
  103.8 26.1 %collective-permute-start.18 = (bf16[512,2048]{1,0:T(8,128)(2,1)S(1)}, bf16[512,2048]{1,0:T(8,128)(2,1)}, u32[]{:S(2)}, u32[]{:S(2)}) collective-permute-start(bf16[512,2048]{1,0:T(8,128)(2,1)S(1)} %collective-permute-done.15.refs_9_.refs_11_.refs_4_), channel_id=1, source_target_pairs={{0,2},{1,5},{2,0},{3,7},{4,6},{5,1},{6,4},{7,3},{8,10},{9,13},{10,... | collective-permute-start | bytes 6291464 | tf_op jit(solution)/shard_map/ppermute | solution.py:53
  105.3 24.6 %collective-permute-start.10 = (bf16[512,2048]{1,0:T(8,128)(2,1)S(1)}, bf16[512,2048]{1,0:T(8,128)(2,1)S(1)}, u32[]{:S(2)}, u32[]{:S(2)}) collective-permute-start(bf16[512,2048]{1,0:T(8,128)(2,1)S(1)} %collective-permute-done.7.refs_7_.refs_9_.refs_10_), channel_id=1, source_target_pairs={{0,1},{1,0},{2,3},{3,2},{4,5},{5,4},{6,7},{7,6},{8,9},{9,8},{10,11... | collective-permute-start | bytes 6291464 | tf_op jit(solution)/shard_map/ppermute | solution.py:53
  105.4 47.0 %collective-permute-start.11 = (bf16[512,2048]{1,0:T(8,128)(2,1)S(1)}, bf16[512,2048]{1,0:T(8,128)(2,1)S(1)}, u32[]{:S(2)}, u32[]{:S(2)}) collective-permute-start(bf16[512,2048]{1,0:T(8,128)(2,1)S(1)} %collective-permute-done.8.refs_9_.refs_11_.refs_12_), channel_id=1, source_target_pairs={{0,2},{1,5},{2,0},{3,7},{4,6},{5,1},{6,4},{7,3},{8,10},{9,13},{10,... | collective-permute-start | bytes 6291464 | tf_op jit(solution)/shard_map/ppermute | solution.py:53
  106.8 47.4 %collective-permute-start.16 = (bf16[512,2048]{1,0:T(8,128)(2,1)S(1)}, bf16[512,2048]{1,0:T(8,128)(2,1)}, u32[]{:S(2)}, u32[]{:S(2)}) collective-permute-start(bf16[512,2048]{1,0:T(8,128)(2,1)S(1)} %collective-permute-done.15.refs_9_.refs_11_.refs_4_), channel_id=1, source_target_pairs={{0,1},{1,0},{2,3},{3,2},{4,5},{5,4},{6,7},{7,6},{8,9},{9,8},{10,11... | collective-permute-start | bytes 6291464 | tf_op jit(solution)/shard_map/ppermute | solution.py:53
  107.1 61.1 %collective-permute-start.17 = (bf16[512,2048]{1,0:T(8,128)(2,1)}, bf16[512,2048]{1,0:T(8,128)(2,1)}, u32[]{:S(2)}, u32[]{:S(2)}) collective-permute-start(bf16[512,2048]{1,0:T(8,128)(2,1)} %collective-permute-done.14.refs_7_.refs_9_.refs_2_), channel_id=1, source_target_pairs={{0,1},{1,0},{2,3},{3,2},{4,5},{5,4},{6,7},{7,6},{8,9},{9,8},{10,11... | collective-permute-start | bytes 6291464 | tf_op jit(solution)/shard_map/ppermute | solution.py:53
  130.0 65.9 %collective-permute-start.19 = (bf16[512,2048]{1,0:T(8,128)(2,1)}, bf16[512,2048]{1,0:T(8,128)(2,1)}, u32[]{:S(2)}, u32[]{:S(2)}) collective-permute-start(bf16[512,2048]{1,0:T(8,128)(2,1)} %collective-permute-done.18.refs_13_.refs_6_), channel_id=1, source_target_pairs={{0,1},{1,0},{2,3},{3,2},{4,5},{5,4},{6,7},{7,6},{8,9},{9,8},{10,11... | collective-permute-start | bytes 6291464 | tf_op jit(solution)/shard_map/ppermute | solution.py:53
  130.0 51.4 %collective-permute-start.2 = (bf16[864,1024]{1,0:T(8,128)(2,1)}, bf16[864,1024]{1,0:T(8,128)(2,1)}, u32[]{:S(2)}, u32[]{:S(2)}) collective-permute-start(bf16[864,1024]{1,0:T(8,128)(2,1)} %collective-permute-done.1.refs_0_.refs_1_), channel_id=1, source_target_pairs={{16,24},{17,25},{18,26},{19,27},{20,28},{21,29},{22,30},{23,31}} | collective-permute-start | bytes 5308424 | tf_op jit(solution)/shard_map/ppermute | solution.py:33
  152.4 42.5 %collective-permute-start.5 = (bf16[864,1024]{1,0:T(8,128)(2,1)}, bf16[864,1024]{1,0:T(8,128)(2,1)}, u32[]{:S(2)}, u32[]{:S(2)}) collective-permute-start(bf16[864,1024]{1,0:T(8,128)(2,1)} %collective-permute-done.4.refs_4_.refs_5_), channel_id=1, source_target_pairs={{8,0},{9,1},{10,2},{11,3},{12,4},{13,5},{14,6},{15,7}} | collective-permute-start | bytes 5308424 | tf_op jit(solution)/shard_map/ppermute | solution.py:32
  154.1 60.2 %collective-permute-start.12 = (bf16[512,2048]{1,0:T(8,128)(2,1)}, bf16[512,2048]{1,0:T(8,128)(2,1)}, u32[]{:S(2)}, u32[]{:S(2)}) collective-permute-start(bf16[512,2048]{1,0:T(8,128)(2,1)} %copy-done.17), channel_id=1, source_target_pairs={{0,1},{1,0},{2,3},{3,2},{4,5},{5,4},{6,7},{7,6},{8,9},{9,8},{10,11... | collective-permute-start | bytes 6291464 | tf_op jit(solution)/shard_map/ppermute | solution.py:53
  168.3 69.5 %collective-permute-start.37 = (s32[12]{0:T(128)S(1)}, s32[12]{0:T(128)S(1)}, u32[]{:S(2)}, u32[]{:S(2)}) collective-permute-start(s32[12]{0:T(128)S(1)} %copy-done.25), channel_id=1, source_target_pairs={{0,1},{1,0},{2,3},{3,2},{4,5},{5,4},{6,7},{7,6},{8,9},{9,8},{10,11... | collective-permute-start | bytes 152 | tf_op jit(solution)/shard_map/ppermute | solution.py:53
  181.4 57.8 %collective-permute-start.38 = (s32[12]{0:T(128)S(1)}, s32[12]{0:T(128)S(1)}, u32[]{:S(2)}, u32[]{:S(2)}) collective-permute-start(s32[12]{0:T(128)S(1)} %copy-done.25), channel_id=1, source_target_pairs={{0,2},{1,5},{2,0},{3,7},{4,6},{5,1},{6,4},{7,3},{8,10},{9,13},{10,... | collective-permute-start | bytes 152 | tf_op jit(solution)/shard_map/ppermute | solution.py:53
  194.8 42.3 %collective-permute-start.39 = (s32[12]{0:T(128)S(1)}, s32[12]{0:T(128)S(1)}, u32[]{:S(2)}, u32[]{:S(2)}) collective-permute-start(s32[12]{0:T(128)S(1)} %copy-done.25), channel_id=1, source_target_pairs={{0,4},{1,3},{2,6},{3,1},{4,0},{5,7},{6,2},{7,5},{8,12},{9,11},{10,... | collective-permute-start | bytes 152 | tf_op jit(solution)/shard_map/ppermute | solution.py:53
  232.1 4.9 %collective-permute-start.27 = (bf16[24,2048]{1,0:T(8,128)(2,1)}, bf16[24,2048]{1,0:T(8,128)(2,1)S(1)}, u32[]{:S(2)}, u32[]{:S(2)}) collective-permute-start(bf16[24,2048]{1,0:T(8,128)(2,1)} %get-tuple-element.27), channel_id=1, source_target_pairs={{0,4},{1,3},{2,6},{3,1},{4,0},{5,7},{6,2},{7,5},{8,12},{9,11},{10,... | collective-permute-start | bytes 294920 | tf_op jit(solution)/shard_map/ppermute | solution.py:53
  233.1 11.2 %collective-permute-start.20 = (bf16[24,2048]{1,0:T(8,128)(2,1)S(1)}, bf16[24,2048]{1,0:T(8,128)(2,1)S(1)}, u32[]{:S(2)}, u32[]{:S(2)}) collective-permute-start(bf16[24,2048]{1,0:T(8,128)(2,1)S(1)} %copy-done.22), channel_id=1, source_target_pairs={{0,4},{1,3},{2,6},{3,1},{4,0},{5,7},{6,2},{7,5},{8,12},{9,11},{10,... | collective-permute-start | bytes 294920 | tf_op jit(solution)/shard_map/ppermute | solution.py:53
  237.0 8.4 %collective-permute-start.28 = (bf16[24,2048]{1,0:T(8,128)(2,1)S(1)}, bf16[24,2048]{1,0:T(8,128)(2,1)S(1)}, u32[]{:S(2)}, u32[]{:S(2)}) collective-permute-start(bf16[24,2048]{1,0:T(8,128)(2,1)S(1)} %collective-permute-done.27), channel_id=1, source_target_pairs={{0,1},{1,0},{2,3},{3,2},{4,5},{5,4},{6,7},{7,6},{8,9},{9,8},{10,11... | collective-permute-start | bytes 294920 | tf_op jit(solution)/shard_map/ppermute | solution.py:53
  237.1 4.2 %collective-permute-start.40 = (s32[12]{0:T(128)S(1)}, s32[12]{0:T(128)S(1)}, u32[]{:S(2)}, u32[]{:S(2)}) collective-permute-start(s32[12]{0:T(128)S(1)} %collective-permute-done.39), channel_id=1, source_target_pairs={{0,1},{1,0},{2,3},{3,2},{4,5},{5,4},{6,7},{7,6},{8,9},{9,8},{10,11... | collective-permute-start | bytes 152 | tf_op jit(solution)/shard_map/ppermute | solution.py:53
  242.6 5.0 %collective-permute-start.29 = (bf16[24,2048]{1,0:T(8,128)(2,1)}, bf16[24,2048]{1,0:T(8,128)(2,1)S(1)}, u32[]{:S(2)}, u32[]{:S(2)}) collective-permute-start(bf16[24,2048]{1,0:T(8,128)(2,1)} %get-tuple-element.27), channel_id=1, source_target_pairs={{0,1},{1,0},{2,3},{3,2},{4,5},{5,4},{6,7},{7,6},{8,9},{9,8},{10,11... | collective-permute-start | bytes 294920 | tf_op jit(solution)/shard_map/ppermute | solution.py:53
  242.7 6.1 %collective-permute-start.30 = (bf16[24,2048]{1,0:T(8,128)(2,1)}, bf16[24,2048]{1,0:T(8,128)(2,1)S(1)}, u32[]{:S(2)}, u32[]{:S(2)}) collective-permute-start(bf16[24,2048]{1,0:T(8,128)(2,1)} %get-tuple-element.27), channel_id=1, source_target_pairs={{0,2},{1,5},{2,0},{3,7},{4,6},{5,1},{6,4},{7,3},{8,10},{9,13},{10,... | collective-permute-start | bytes 294920 | tf_op jit(solution)/shard_map/ppermute | solution.py:53
  244.2 5.1 %collective-permute-start.22 = (bf16[24,2048]{1,0:T(8,128)(2,1)S(1)}, bf16[24,2048]{1,0:T(8,128)(2,1)S(1)}, u32[]{:S(2)}, u32[]{:S(2)}) collective-permute-start(bf16[24,2048]{1,0:T(8,128)(2,1)S(1)} %copy-done.22), channel_id=1, source_target_pairs={{0,1},{1,0},{2,3},{3,2},{4,5},{5,4},{6,7},{7,6},{8,9},{9,8},{10,11... | collective-permute-start | bytes 294920 | tf_op jit(solution)/shard_map/ppermute | solution.py:53
  244.2 4.6 %collective-permute-start.23 = (bf16[24,2048]{1,0:T(8,128)(2,1)S(1)}, bf16[24,2048]{1,0:T(8,128)(2,1)S(1)}, u32[]{:S(2)}, u32[]{:S(2)}) collective-permute-start(bf16[24,2048]{1,0:T(8,128)(2,1)S(1)} %copy-done.22), channel_id=1, source_target_pairs={{0,2},{1,5},{2,0},{3,7},{4,6},{5,1},{6,4},{7,3},{8,10},{9,13},{10,... | collective-permute-start | bytes 294920 | tf_op jit(solution)/shard_map/ppermute | solution.py:53
  246.7 4.6 %collective-permute-start.32 = (bf16[24,2048]{1,0:T(8,128)(2,1)S(1)}, bf16[24,2048]{1,0:T(8,128)(2,1)S(1)}, u32[]{:S(2)}, u32[]{:S(2)}) collective-permute-start(bf16[24,2048]{1,0:T(8,128)(2,1)S(1)} %collective-permute-done.27), channel_id=1, source_target_pairs={{0,2},{1,5},{2,0},{3,7},{4,6},{5,1},{6,4},{7,3},{8,10},{9,13},{10,... | collective-permute-start | bytes 294920 | tf_op jit(solution)/shard_map/ppermute | solution.py:53
  247.6 4.8 %collective-permute-start.25 = (bf16[24,2048]{1,0:T(8,128)(2,1)S(1)}, bf16[24,2048]{1,0:T(8,128)(2,1)S(1)}, u32[]{:S(2)}, u32[]{:S(2)}) collective-permute-start(bf16[24,2048]{1,0:T(8,128)(2,1)S(1)} %collective-permute-done.20), channel_id=1, source_target_pairs={{0,2},{1,5},{2,0},{3,7},{4,6},{5,1},{6,4},{7,3},{8,10},{9,13},{10,... | collective-permute-start | bytes 294920 | tf_op jit(solution)/shard_map/ppermute | solution.py:53
  259.6 5.0 %collective-permute-start.36 = (f32[96,96]{0,1:T(8,128)S(1)}, f32[96,96]{0,1:T(8,128)S(1)}, u32[]{:S(2)}, u32[]{:S(2)}) collective-permute-start(f32[96,96]{0,1:T(8,128)S(1)} %convolution_add_fusion), channel_id=1, source_target_pairs={{0,24},{8,0},{16,8},{24,16},{1,25},{9,1},{17,9},{25,17},{2,26},{10... | collective-permute-start | bytes 110600 | tf_op jit(solution)/shard_map/ppermute | solution.py:507
  259.7 7.2 %collective-permute-start.35 = (f32[96,96]{0,1:T(8,128)S(1)}, f32[96,96]{0,1:T(8,128)S(1)}, u32[]{:S(2)}, u32[]{:S(2)}) collective-permute-start(f32[96,96]{0,1:T(8,128)S(1)} %convolution_add_fusion), channel_id=1, source_target_pairs={{0,16},{8,24},{16,0},{24,8},{1,17},{9,25},{17,1},{25,9},{2,18},{10... | collective-permute-start | bytes 110600 | tf_op jit(solution)/shard_map/ppermute | solution.py:507
  260.7 6.2 %collective-permute-start.34 = (f32[96,96]{0,1:T(8,128)S(1)}, f32[96,96]{0,1:T(8,128)S(1)}, u32[]{:S(2)}, u32[]{:S(2)}) collective-permute-start(f32[96,96]{0,1:T(8,128)S(1)} %convolution_add_fusion), channel_id=1, source_target_pairs={{0,8},{8,16},{16,24},{24,0},{1,9},{9,17},{17,25},{25,1},{2,10},{10... | collective-permute-start | bytes 110600 | tf_op jit(solution)/shard_map/ppermute | solution.py:507
  284.5 15.8 %collective-permute-start.44 = (bf16[864,512]{1,0:T(8,128)(2,1)S(1)}, bf16[864,512]{1,0:T(8,128)(2,1)S(1)}, u32[]{:S(2)}, u32[]{:S(2)}) collective-permute-start(bf16[864,512]{1,0:T(8,128)(2,1)S(1)} %backward_first.3), channel_id=1, source_target_pairs={{24,16},{25,17},{26,18},{27,19},{28,20},{29,21},{30,22},{31,23}} | collective-permute-start | bytes 2654216 | tf_op jit(solution)/shard_map/ppermute | solution.py:441
  285.2 21.6 %collective-permute-start.45 = (bf16[864,512]{1,0:T(8,128)(2,1)S(1)}, bf16[864,512]{1,0:T(8,128)(2,1)S(1)}, u32[]{:S(2)}, u32[]{:S(2)}) collective-permute-start(bf16[864,512]{1,0:T(8,128)(2,1)S(1)} %backward_first.3), channel_id=1, source_target_pairs={{0,8},{1,9},{2,10},{3,11},{4,12},{5,13},{6,14},{7,15}} | collective-permute-start | bytes 2654216 | tf_op jit(solution)/shard_map/ppermute | solution.py:442
  298.2 22.3 %collective-permute-start.50 = (bf16[864,512]{1,0:T(8,128)(2,1)}, bf16[864,512]{1,0:T(8,128)(2,1)S(1)}, u32[]{:S(2)}, u32[]{:S(2)}) collective-permute-start(bf16[864,512]{1,0:T(8,128)(2,1)} %get-tuple-element.33), channel_id=1, source_target_pairs={{24,16},{25,17},{26,18},{27,19},{28,20},{29,21},{30,22},{31,23}} | collective-permute-start | bytes 2654216 | tf_op jit(solution)/shard_map/ppermute | solution.py:441
  298.9 27.0 %collective-permute-start.51 = (bf16[864,512]{1,0:T(8,128)(2,1)}, bf16[864,512]{1,0:T(8,128)(2,1)S(1)}, u32[]{:S(2)}, u32[]{:S(2)}) collective-permute-start(bf16[864,512]{1,0:T(8,128)(2,1)} %get-tuple-element.33), channel_id=1, source_target_pairs={{0,8},{1,9},{2,10},{3,11},{4,12},{5,13},{6,14},{7,15}} | collective-permute-start | bytes 2654216 | tf_op jit(solution)/shard_map/ppermute | solution.py:442
  314.7 25.4 %collective-permute-start.46 = (bf16[864,512]{1,0:T(8,128)(2,1)S(1)}, bf16[864,512]{1,0:T(8,128)(2,1)S(1)}, u32[]{:S(2)}, u32[]{:S(2)}) collective-permute-start(bf16[864,512]{1,0:T(8,128)(2,1)S(1)} %backward_part.6), channel_id=1, source_target_pairs={{16,8},{24,16},{17,9},{25,17},{18,10},{26,18},{19,11},{27,19},{20,... | collective-permute-start | bytes 2654216 | tf_op jit(solution)/shard_map/ppermute | solution.py:441
  315.5 29.3 %collective-permute-start.47 = (bf16[864,512]{1,0:T(8,128)(2,1)S(1)}, bf16[864,512]{1,0:T(8,128)(2,1)S(1)}, u32[]{:S(2)}, u32[]{:S(2)}) collective-permute-start(bf16[864,512]{1,0:T(8,128)(2,1)S(1)} %backward_part.6), channel_id=1, source_target_pairs={{0,8},{8,16},{1,9},{9,17},{2,10},{10,18},{3,11},{11,19},{4,12},{12... | collective-permute-start | bytes 2654216 | tf_op jit(solution)/shard_map/ppermute | solution.py:442
  333.8 29.2 %collective-permute-start.52 = (bf16[864,512]{1,0:T(8,128)(2,1)S(1)}, bf16[864,512]{1,0:T(8,128)(2,1)S(1)}, u32[]{:S(2)}, u32[]{:S(2)}) collective-permute-start(bf16[864,512]{1,0:T(8,128)(2,1)S(1)} %backward_part.10), channel_id=1, source_target_pairs={{16,8},{24,16},{17,9},{25,17},{18,10},{26,18},{19,11},{27,19},{20,... | collective-permute-start | bytes 2654216 | tf_op jit(solution)/shard_map/ppermute | solution.py:441
  334.5 29.2 %collective-permute-start.53 = (bf16[864,512]{1,0:T(8,128)(2,1)S(1)}, bf16[864,512]{1,0:T(8,128)(2,1)S(1)}, u32[]{:S(2)}, u32[]{:S(2)}) collective-permute-start(bf16[864,512]{1,0:T(8,128)(2,1)S(1)} %backward_part.10), channel_id=1, source_target_pairs={{0,8},{8,16},{1,9},{9,17},{2,10},{10,18},{3,11},{11,19},{4,12},{12... | collective-permute-start | bytes 2654216 | tf_op jit(solution)/shard_map/ppermute | solution.py:442
  356.8 32.5 %collective-permute-start.48 = (bf16[864,512]{1,0:T(8,128)(2,1)S(1)}, bf16[864,512]{1,0:T(8,128)(2,1)S(1)}, u32[]{:S(2)}, u32[]{:S(2)}) collective-permute-start(bf16[864,512]{1,0:T(8,128)(2,1)S(1)} %get-tuple-element.31), channel_id=1, source_target_pairs={{8,0},{16,8},{24,16},{9,1},{17,9},{25,17},{10,2},{18,10},{26,18},{... | collective-permute-start | bytes 2654216 | tf_op jit(solution)/shard_map/ppermute | solution.py:441
  358.1 31.2 %collective-permute-start.49 = (bf16[864,512]{1,0:T(8,128)(2,1)S(1)}, bf16[864,512]{1,0:T(8,128)(2,1)S(1)}, u32[]{:S(2)}, u32[]{:S(2)}) collective-permute-start(bf16[864,512]{1,0:T(8,128)(2,1)S(1)} %get-tuple-element.32), channel_id=1, source_target_pairs={{0,8},{8,16},{16,24},{1,9},{9,17},{17,25},{2,10},{10,18},{18,26},{... | collective-permute-start | bytes 2654216 | tf_op jit(solution)/shard_map/ppermute | solution.py:442
  375.8 24.3 %collective-permute-start.55 = (bf16[864,512]{1,0:T(8,128)(2,1)S(1)}, bf16[864,512]{1,0:T(8,128)(2,1)S(1)}, u32[]{:S(2)}, u32[]{:S(2)}) collective-permute-start(bf16[864,512]{1,0:T(8,128)(2,1)S(1)} %get-tuple-element.35), channel_id=1, source_target_pairs={{0,8},{8,16},{16,24},{1,9},{9,17},{17,25},{2,10},{10,18},{18,26},{... | collective-permute-start | bytes 2654216 | tf_op jit(solution)/shard_map/ppermute | solution.py:442
  380.2 20.8 %collective-permute-start.54 = (bf16[864,512]{1,0:T(8,128)(2,1)S(1)}, bf16[864,512]{1,0:T(8,128)(2,1)S(1)}, u32[]{:S(2)}, u32[]{:S(2)}) collective-permute-start(bf16[864,512]{1,0:T(8,128)(2,1)S(1)} %get-tuple-element.34), channel_id=1, source_target_pairs={{8,0},{16,8},{24,16},{9,1},{17,9},{25,17},{10,2},{18,10},{26,18},{... | collective-permute-start | bytes 2654216 | tf_op jit(solution)/shard_map/ppermute | solution.py:441
  (34 other events, 954.4 us)

commit v5 on v4

--- a/solution.py
+++ b/solution.py
@@ -503,11 +503,13 @@
         lax.dot_general(q, p, (((1,), (1,)), ((), ())), preferred_element_type=jnp.float32)
         for q, p in zip(all_query, all_pass)
     )
-    shifted = [
-        lax.ppermute(scores, "vocab", [(d, (d + s) % n_vocab) for d in range(n_vocab)]) for s in range(1, n_vocab)
-    ]
-    for other in shifted:
-        scores = scores + other
+    if n_vocab & (n_vocab - 1) == 0:
+        hop = 1
+        while hop < n_vocab:
+            scores = scores + lax.ppermute(scores, "vocab", [(d, d ^ hop) for d in range(n_vocab)])
+            hop *= 2
+    else:
+        scores = lax.psum(scores, "vocab")
     scores = scores * scaling
     positive = jnp.sum(scores * onehot, axis=1, keepdims=True)
     weights = jax.nn.sigmoid(MARGIN + scores - positive) * (1.0 - onehot)

time: 404 us -> 415 us (1.027)
  waiting for transfers between devices: 173 us -> 189 us
  starting transfers between devices: 66.3 us -> 62 us
    ppermute x35, waiting for transfers between devices: 98.4 us -> 113 us  [move(): return lax.ppermute(value, 'rows', pairs)]
    ppermute x35, starting transfers between devices: 22.7 us -> 18.3 us  [move(): return lax.ppermute(value, 'rows', pairs)]
  transfers between devices with their start and end apart: 56 -> 55, of which waited for: 24 -> 24; matrix products, arithmetic and copies ran while one was open for 2% -> 2% of each run, Pallas kernels for 32% -> 27%
where the time goes in v5:
time: 415 us; the launch traced here: 413 us
  waiting for transfers between devices  189 us (46%)
  Pallas kernels  137 us (33%)
  starting transfers between devices  62 us (15%)
  local copies, waits for them, and re-layouts  15 us (4%)
  other arithmetic  5.91 us (1%)
    ppermute x35, waiting for transfers between devices, move(): return lax.ppermute(value, 'rows', pairs)  113 us
    pallas_call x4, Pallas kernels, forward(): pl.pallas_call(functools.partial(forward_kernel, spec), out_shape=out_sha...  60.5 us
    pallas_call x6, Pallas kernels, backward(): pl.pallas_call(functools.partial(backward_kernel, (at, count, spans(group...  55.5 us
    ppermute x3, waiting for transfers between devices, line_gather(): lax.ppermute(right, 'vocab', [(z, z + 1) for z in range(step - 1, n - 1)])  31.2 us
    ppermute x6, starting transfers between devices, line_reduce_scatter(): lax.ppermute(to_right, 'vocab', [(d, d + 1) for d in range(step)])  25 us
    ppermute x3, waiting for transfers between devices, line_gather(): lax.ppermute(left, 'vocab', [(z, z - 1) for z in range(1, n - step + 1)])  21 us
    pallas_call x2, Pallas kernels, backward_first(): pl.pallas_call(functools.partial(first_kernel, (at, count, spans(parts),...  20.6 us
    ppermute x6, waiting for transfers between devices, line_reduce_scatter(): lax.ppermute(to_right, 'vocab', [(d, d + 1) for d in range(step)])  20 us
  transfers between devices with their start and end apart: 55, of which 24 were waited for; matrix products, arithmetic and copies ran while one was open for 2% of the time, Pallas kernels for 27%

profile of v5, /device:TPU:0, one launch (start us, length us, event | category | flops | bytes accessed | tf_op | source)
XLA Modules:
  0.0 413.4 jit_solution(5642678763140316265)
XLA Ops:
  0.6 1.7 pad_maximum_fusion.refs_2_.refs_3_
  2.3 5.3 %collective-permute-start = (bf16[864,1024]{1,0:T(8,128)(2,1)S(1)}, bf16[864,1024]{1,0:T(8,128)(2,1)S(1)}, u32[]{:S(2)}, u32[]{:S(2)}) collective-permute-start(bf16[864,1024]{1,0:T(8,128)(2,1)S(1)} %pad_maximum_fusion.refs_2_.refs_3_), channel_id=1, source_target_pairs={{0,8},{8,16},{16,24},{1,9},{9,17},{17,25},{2,10},{10,18},{18,26},{... | collective-permute-start | bytes 5308424 | tf_op jit(solution)/shard_map/ppermute | solution.py:33
  7.7 1.7 slice.40.refs_5_.refs_7_.refs_8_
  10.8 1.6 collective-permute-start.7
  12.4 1.5 collective-permute-start.8
  14.2 31.2 %collective-permute-done.refs_1_.refs_2_ = bf16[864,1024]{1,0:T(8,128)(2,1)S(1)} collective-permute-done((bf16[864,1024]{1,0:T(8,128)(2,1)S(1)}, bf16[864,1024]{1,0:T(8,128)(2,1)S(1)}, u32[]{:S(2)}, u32[]{:S(2)}) %collective-permute-start) | collective-permute-done | bytes 1769504 | tf_op jit(solution)/shard_map/ppermute | solution.py:33
  45.4 7.0 %collective-permute-done.3.refs_3_.refs_4_ = bf16[864,1024]{1,0:T(8,128)(2,1)S(1)} collective-permute-done((bf16[864,1024]{1,0:T(8,128)(2,1)S(1)}, bf16[864,1024]{1,0:T(8,128)(2,1)S(1)}, u32[]{:S(2)}, u32[]{:S(2)}) %collective-permute-start.3) | collective-permute-done | bytes 1769504 | tf_op jit(solution)/shard_map/ppermute | solution.py:32
  52.4 1.5 collective-permute-start.15
  55.4 3.2 collective-permute-done.7.refs_7_.refs_9_.refs_10_
  58.6 1.9 collective-permute-start.1
  62.3 41.6 %collective-permute-done.15.refs_9_.refs_11_.refs_4_ = bf16[512,2048]{1,0:T(8,128)(2,1)S(1)} collective-permute-done((bf16[512,2048]{1,0:T(8,128)(2,1)S(1)}, bf16[512,2048]{1,0:T(8,128)(2,1)S(1)}, u32[]{:S(2)}, u32[]{:S(2)}) %collective-permute-start.15) | collective-permute-done | bytes 2097184 | tf_op jit(solution)/shard_map/ppermute | solution.py:53
  107.3 22.7 %collective-permute-done.18.refs_13_.refs_6_ = bf16[512,2048]{1,0:T(8,128)(2,1)} collective-permute-done((bf16[512,2048]{1,0:T(8,128)(2,1)S(1)}, bf16[512,2048]{1,0:T(8,128)(2,1)}, u32[]{:S(2)}, u32[]{:S(2)}) %collective-permute-start.18) | collective-permute-done | bytes 2097184 | tf_op jit(solution)/shard_map/ppermute | solution.py:53
  130.0 1.9 collective-permute-start.2
  131.9 20.5 %collective-permute-done.11.refs_13_.refs_14_ = bf16[512,2048]{1,0:T(8,128)(2,1)S(1)} collective-permute-done((bf16[512,2048]{1,0:T(8,128)(2,1)S(1)}, bf16[512,2048]{1,0:T(8,128)(2,1)S(1)}, u32[]{:S(2)}, u32[]{:S(2)}) %collective-permute-start.11) | collective-permute-done | bytes 2097184 | tf_op jit(solution)/shard_map/ppermute | solution.py:53
  155.4 12.7 %forward_part.2.refs_15_ = f32[864,2048]{1,0:T(8,128)} custom-call(s32[42]{0:T(128)} %get-tuple-element.45.plan_ref, bf16[864,1024]{1,0:T(8,128)(2,1)} %collective-permute-done.1.refs_0_.refs_1_, bf16[864,1024]{1,0:T(8,128)(2,1)} %copy-done.19, bf16[864,1024]{1,0:T(8,128)(2,1)} %copy-done.18, bf16[864,1024]{1,0:T(8,128)(2,1)} %copy-done.20, ...), custom_call_target="tpu_custom_call" | custom-call | flops 7247757312 | bytes 22544384 | tf_op jit(solution)/shard_map/forward_part/pallas_call | solution.py:233
  168.1 12.7 %forward_part.3.refs_15_ = f32[864,2048]{1,0:T(8,128)} custom-call(s32[42]{0:T(128)} %get-tuple-element.45.plan_ref, bf16[864,1024]{1,0:T(8,128)(2,1)} %collective-permute-done.1.refs_0_.refs_1_, bf16[864,1024]{1,0:T(8,128)(2,1)} %copy-done.19, bf16[864,1024]{1,0:T(8,128)(2,1)} %copy-done.18, bf16[864,1024]{1,0:T(8,128)(2,1)} %copy-done.20, ...), custom_call_target="tpu_custom_call" | custom-call | flops 7247757312 | bytes 22544384 | tf_op jit(solution)/shard_map/forward_part/pallas_call | solution.py:233
  180.8 14.0 %collective-permute-done.5.refs_6_ = bf16[864,1024]{1,0:T(8,128)(2,1)} collective-permute-done((bf16[864,1024]{1,0:T(8,128)(2,1)}, bf16[864,1024]{1,0:T(8,128)(2,1)}, u32[]{:S(2)}, u32[]{:S(2)}) %collective-permute-start.5) | collective-permute-done | bytes 1769504 | tf_op jit(solution)/shard_map/ppermute | solution.py:32
  195.7 17.5 %forward_final.2 = (bf16[864,4096]{1,0:T(8,128)(2,1)}, f32[24,4096]{1,0:T(8,128)}, bf16[24,2048]{1,0:T(8,128)(2,1)}) custom-call(s32[42]{0:T(128)} %get-tuple-element.45.plan_ref, bf16[864,1024]{1,0:T(8,128)(2,1)} %collective-permute-done.2.refs_0_, bf16[864,1024]{1,0:T(8,128)(2,1)} %collective-permute-done.1.refs_0_.refs_1_, bf16[864,1024]{1,0:T(8,128)(2,1)} %copy-done.19, ...), custom_call_target="tpu_custom_call" | custom-call | flops 7247757312 | bytes 22544384 | tf_op jit(solution)/shard_map/forward_final/pallas_call | solution.py:233
  213.3 17.7 %forward_final.3 = (bf16[864,4096]{1,0:T(8,128)(2,1)}, f32[24,4096]{1,0:T(8,128)}, bf16[24,2048]{1,0:T(8,128)(2,1)}) custom-call(s32[42]{0:T(128)} %get-tuple-element.45.plan_ref, bf16[864,1024]{1,0:T(8,128)(2,1)} %collective-permute-done.2.refs_0_, ...), custom_call_target="tpu_custom_call", output_to_operand_aliasing={{0}: (18, {}), {1}: (19, {})} | custom-call | flops 7247757312 | bytes 22544384 | tf_op jit(solution)/shard_map/forward_final/pallas_call | solution.py:233
  235.9 3.5 collective-permute-done.20
  241.9 3.9 collective-permute-done.30
  246.3 4.1 %collective-permute-done.23 = bf16[24,2048]{1,0:T(8,128)(2,1)S(1)} collective-permute-done((bf16[24,2048]{1,0:T(8,128)(2,1)S(1)}, bf16[24,2048]{1,0:T(8,128)(2,1)S(1)}, u32[]{:S(2)}, u32[]{:S(2)}) %collective-permute-start.23) | collective-permute-done | bytes 98336 | tf_op jit(solution)/shard_map/ppermute | solution.py:53
  251.0 4.1 collective-permute-done.32
  255.5 4.2 %collective-permute-done.25 = bf16[24,2048]{1,0:T(8,128)(2,1)S(1)} collective-permute-done((bf16[24,2048]{1,0:T(8,128)(2,1)S(1)}, bf16[24,2048]{1,0:T(8,128)(2,1)S(1)}, u32[]{:S(2)}, u32[]{:S(2)}) %collective-permute-start.25) | collective-permute-done | bytes 98336 | tf_op jit(solution)/shard_map/ppermute | solution.py:53
  265.2 2.6 collective-permute-done.41
  270.6 3.6 collective-permute-done.35
  276.3 1.6 copy-done.7
  277.9 1.6 copy-done.9
  279.5 1.6 copy-done.11
  281.1 1.6 copy-done.13
  282.7 1.6 copy-done.15
  284.3 9.3 %backward_first.3 = bf16[864,512]{1,0:T(8,128)(2,1)S(1)} custom-call(s32[42]{0:T(128)S(1)} %copy-done.16, bf16[864,4096]{1,0:T(8,128)(2,1)} %get-tuple-element.22.slope_ref, f32[12,4096]{1,0:T(8,128)S(1)} %get-tuple-element.43.pass_ref, f32[12,4096]{1,0:T(8,128)S(1)} %get-tuple-element.42.query_ref, bf16[512,2048]{1,0:T(8,128)(2,1)S(1)} %copy-done.3, ...), custom_call_target="tpu_custom_call" | custom-call | flops 3623878656 | bytes 19234816 | tf_op jit(solution)/shard_map/backward_first/pallas_call | solution.py:325
  294.3 3.7 collective-permute-start.44
  298.0 11.3 %backward_first.2 = (bf16[864,4096]{1,0:T(8,128)(2,1)}, bf16[864,512]{1,0:T(8,128)(2,1)}) custom-call(s32[42]{0:T(128)S(1)} %copy-done.16, bf16[864,4096]{1,0:T(8,128)(2,1)} %get-tuple-element.22.slope_ref, f32[12,4096]{1,0:T(8,128)S(1)} %get-tuple-element.43.pass_ref, f32[12,4096]{1,0:T(8,128)S(1)} %get-tuple-element.42.query_ref, ...), custom_call_target="tpu_custom_call" | custom-call | flops 3623878656 | bytes 19234816 | tf_op jit(solution)/shard_map/backward_first/pallas_call | solution.py:325
  311.4 6.5 %collective-permute-done.44.refs_17_ = bf16[864,512]{1,0:T(8,128)(2,1)S(1)} collective-permute-done((bf16[864,512]{1,0:T(8,128)(2,1)S(1)}, bf16[864,512]{1,0:T(8,128)(2,1)S(1)}, u32[]{:S(2)}, u32[]{:S(2)}) %collective-permute-start.44) | collective-permute-done | bytes 884768 | tf_op jit(solution)/shard_map/ppermute | solution.py:442
  318.0 7.9 %backward_part.6 = bf16[864,512]{1,0:T(8,128)(2,1)S(1)} custom-call(s32[42]{0:T(128)S(1)} %copy-done.16, bf16[864,4096]{1,0:T(8,128)(2,1)} %get-tuple-element.30.slopes_ref, bf16[512,2048]{1,0:T(8,128)(2,1)S(1)} %copy-done.3, bf16[512,2048]{1,0:T(8,128)(2,1)} %collective-permute-done.13.refs_6_.refs_8_.refs_1_, ...), custom_call_target="tpu_custom_call" | custom-call | flops 3623878656 | bytes 12156928 | tf_op jit(solution)/shard_map/backward_part/pallas_call | solution.py:407
  326.6 5.0 %collective-permute-start.46 = (bf16[864,512]{1,0:T(8,128)(2,1)S(1)}, bf16[864,512]{1,0:T(8,128)(2,1)S(1)}, u32[]{:S(2)}, u32[]{:S(2)}) collective-permute-start(bf16[864,512]{1,0:T(8,128)(2,1)S(1)} %backward_part.6), channel_id=1, source_target_pairs={{0,8},{8,16},{1,9},{9,17},{2,10},{10,18},{3,11},{11,19},{4,12},{12... | collective-permute-start | bytes 2654216 | tf_op jit(solution)/shard_map/ppermute | solution.py:442
  331.6 5.4 %collective-permute-done.50.refs_17_ = bf16[864,512]{1,0:T(8,128)(2,1)S(1)} collective-permute-done((bf16[864,512]{1,0:T(8,128)(2,1)}, bf16[864,512]{1,0:T(8,128)(2,1)S(1)}, u32[]{:S(2)}, u32[]{:S(2)}) %collective-permute-start.50) | collective-permute-done | bytes 884768 | tf_op jit(solution)/shard_map/ppermute | solution.py:442
  337.0 7.9 %backward_part.10 = bf16[864,512]{1,0:T(8,128)(2,1)S(1)} custom-call(s32[42]{0:T(128)S(1)} %copy-done.16, bf16[864,4096]{1,0:T(8,128)(2,1)} %get-tuple-element.30.slopes_ref, bf16[512,2048]{1,0:T(8,128)(2,1)S(1)} %copy-done.3, bf16[512,2048]{1,0:T(8,128)(2,1)} %collective-permute-done.13.refs_6_.refs_8_.refs_1_, ...), custom_call_target="tpu_custom_call" | custom-call | flops 3623878656 | bytes 12156928 | tf_op jit(solution)/shard_map/backward_part/pallas_call | solution.py:407
  345.7 5.6 %collective-permute-start.52 = (bf16[864,512]{1,0:T(8,128)(2,1)S(1)}, bf16[864,512]{1,0:T(8,128)(2,1)S(1)}, u32[]{:S(2)}, u32[]{:S(2)}) collective-permute-start(bf16[864,512]{1,0:T(8,128)(2,1)S(1)} %backward_part.10), channel_id=1, source_target_pairs={{0,8},{8,16},{1,9},{9,17},{2,10},{10,18},{3,11},{11,19},{4,12},{12... | collective-permute-start | bytes 2654216 | tf_op jit(solution)/shard_map/ppermute | solution.py:442
  351.3 4.6 %collective-permute-done.46.refs_17_ = bf16[864,512]{1,0:T(8,128)(2,1)S(1)} collective-permute-done((bf16[864,512]{1,0:T(8,128)(2,1)S(1)}, bf16[864,512]{1,0:T(8,128)(2,1)S(1)}, u32[]{:S(2)}, u32[]{:S(2)}) %collective-permute-start.46) | collective-permute-done | bytes 884768 | tf_op jit(solution)/shard_map/ppermute | solution.py:442
  355.9 12.1 %backward_part.7 = (bf16[864,512]{1,0:T(8,128)(2,1)S(1)}, bf16[864,512]{1,0:T(8,128)(2,1)S(1)}) custom-call(s32[42]{0:T(128)S(1)} %copy-done.16, bf16[864,4096]{1,0:T(8,128)(2,1)} %get-tuple-element.30.slopes_ref, bf16[512,2048]{1,0:T(8,128)(2,1)S(1)} %copy-done.3, bf16[512,2048]{1,0:T(8,128)(2,1)} %collective-permute-done.13.refs_6_.refs_8_.refs_1_, ...), custom_call_target="tpu_custom_call" | custom-call | flops 7247757312 | bytes 17235968 | tf_op jit(solution)/shard_map/backward_part/pallas_call | solution.py:407
  369.2 4.9 %collective-permute-start.48 = (bf16[864,512]{1,0:T(8,128)(2,1)S(1)}, bf16[864,512]{1,0:T(8,128)(2,1)S(1)}, u32[]{:S(2)}, u32[]{:S(2)}) collective-permute-start(bf16[864,512]{1,0:T(8,128)(2,1)S(1)} %get-tuple-element.32), channel_id=1, source_target_pairs={{0,8},{8,16},{16,24},{1,9},{9,17},{17,25},{2,10},{10,18},{18,26},{... | collective-permute-start | bytes 2654216 | tf_op jit(solution)/shard_map/ppermute | solution.py:442
  374.8 12.1 %backward_part.11 = (bf16[864,512]{1,0:T(8,128)(2,1)S(1)}, bf16[864,512]{1,0:T(8,128)(2,1)S(1)}) custom-call(s32[42]{0:T(128)S(1)} %copy-done.16, bf16[864,4096]{1,0:T(8,128)(2,1)} %get-tuple-element.30.slopes_ref, bf16[512,2048]{1,0:T(8,128)(2,1)S(1)} %copy-done.3, bf16[512,2048]{1,0:T(8,128)(2,1)} %collective-permute-done.13.refs_6_.refs_8_.refs_1_, ...), custom_call_target="tpu_custom_call" | custom-call | flops 7247757312 | bytes 17235968 | tf_op jit(solution)/shard_map/backward_part/pallas_call | solution.py:407
  386.9 4.4 %collective-permute-start.54 = (bf16[864,512]{1,0:T(8,128)(2,1)S(1)}, bf16[864,512]{1,0:T(8,128)(2,1)S(1)}, u32[]{:S(2)}, u32[]{:S(2)}) collective-permute-start(bf16[864,512]{1,0:T(8,128)(2,1)S(1)} %get-tuple-element.35), channel_id=1, source_target_pairs={{0,8},{8,16},{16,24},{1,9},{9,17},{17,25},{2,10},{10,18},{18,26},{... | collective-permute-start | bytes 2654216 | tf_op jit(solution)/shard_map/ppermute | solution.py:442
  392.6 7.8 %backward_part.9 = bf16[864,512]{1,0:T(8,128)(2,1)S(1)} custom-call(s32[42]{0:T(128)S(1)} %copy-done.16, bf16[864,4096]{1,0:T(8,128)(2,1)} %get-tuple-element.30.slopes_ref, bf16[512,2048]{1,0:T(8,128)(2,1)S(1)} %copy-done.3, bf16[512,2048]{1,0:T(8,128)(2,1)} %collective-permute-done.13.refs_6_.refs_8_.refs_1_, ...), custom_call_target="tpu_custom_call" | custom-call | flops 3623878656 | bytes 12156928 | tf_op jit(solution)/shard_map/backward_part/pallas_call | solution.py:407
  400.5 7.8 %backward_part.8 = bf16[864,512]{1,0:T(8,128)(2,1)S(1)} custom-call(s32[42]{0:T(128)S(1)} %copy-done.16, bf16[864,4096]{1,0:T(8,128)(2,1)} %get-tuple-element.30.slopes_ref, bf16[512,2048]{1,0:T(8,128)(2,1)S(1)} %copy-done.3, bf16[512,2048]{1,0:T(8,128)(2,1)} %collective-permute-done.13.refs_6_.refs_8_.refs_1_, ...), custom_call_target="tpu_custom_call" | custom-call | flops 3623878656 | bytes 12156928 | tf_op jit(solution)/shard_map/backward_part/pallas_call | solution.py:407
  408.2 2.8 collective-permute-done.54
  (177 shorter events, 41.2 us)
Async XLA Ops:
  2.3 43.1 %collective-permute-start = (bf16[864,1024]{1,0:T(8,128)(2,1)S(1)}, bf16[864,1024]{1,0:T(8,128)(2,1)S(1)}, u32[]{:S(2)}, u32[]{:S(2)}) collective-permute-start(bf16[864,1024]{1,0:T(8,128)(2,1)S(1)} %pad_maximum_fusion.refs_2_.refs_3_), channel_id=1, source_target_pairs={{0,8},{8,16},{16,24},{1,9},{9,17},{17,25},{2,10},{10,18},{18,26},{... | collective-permute-start | bytes 5308424 | tf_op jit(solution)/shard_map/ppermute | solution.py:33
  9.4 44.5 %collective-permute-start.6 = (bf16[512,2048]{1,0:T(8,128)(2,1)S(1)}, bf16[512,2048]{1,0:T(8,128)(2,1)S(1)}, u32[]{:S(2)}, u32[]{:S(2)}) collective-permute-start(bf16[512,2048]{1,0:T(8,128)(2,1)S(1)} %slice.40.refs_5_.refs_7_.refs_8_), channel_id=1, source_target_pairs={{0,1},{1,0},{2,3},{3,2},{4,5},{5,4},{6,7},{7,6},{8,9},{9,8},{10,11... | collective-permute-start | bytes 6291464 | tf_op jit(solution)/shard_map/ppermute | solution.py:53
  9.5 42.9 %collective-permute-start.3 = (bf16[864,1024]{1,0:T(8,128)(2,1)S(1)}, bf16[864,1024]{1,0:T(8,128)(2,1)S(1)}, u32[]{:S(2)}, u32[]{:S(2)}) collective-permute-start(bf16[864,1024]{1,0:T(8,128)(2,1)S(1)} %pad_maximum_fusion.refs_2_.refs_3_), channel_id=1, source_target_pairs={{8,0},{16,8},{24,16},{9,1},{17,9},{25,17},{10,2},{18,10},{26,18},{... | collective-permute-start | bytes 5308424 | tf_op jit(solution)/shard_map/ppermute | solution.py:32
  10.8 47.8 %collective-permute-start.7 = (bf16[512,2048]{1,0:T(8,128)(2,1)S(1)}, bf16[512,2048]{1,0:T(8,128)(2,1)S(1)}, u32[]{:S(2)}, u32[]{:S(2)}) collective-permute-start(bf16[512,2048]{1,0:T(8,128)(2,1)S(1)} %slice.40.refs_5_.refs_7_.refs_8_), channel_id=1, source_target_pairs={{0,2},{1,5},{2,0},{3,7},{4,6},{5,1},{6,4},{7,3},{8,10},{9,13},{10,... | collective-permute-start | bytes 6291464 | tf_op jit(solution)/shard_map/ppermute | solution.py:53
  12.4 48.5 %collective-permute-start.8 = (bf16[512,2048]{1,0:T(8,128)(2,1)S(1)}, bf16[512,2048]{1,0:T(8,128)(2,1)S(1)}, u32[]{:S(2)}, u32[]{:S(2)}) collective-permute-start(bf16[512,2048]{1,0:T(8,128)(2,1)S(1)} %slice.40.refs_5_.refs_7_.refs_8_), channel_id=1, source_target_pairs={{0,4},{1,3},{2,6},{3,1},{4,0},{5,7},{6,2},{7,5},{8,12},{9,11},{10,... | collective-permute-start | bytes 6291464 | tf_op jit(solution)/shard_map/ppermute | solution.py:53
  45.4 16.8 %collective-permute-start.13 = (bf16[512,2048]{1,0:T(8,128)(2,1)S(1)}, bf16[512,2048]{1,0:T(8,128)(2,1)}, u32[]{:S(2)}, u32[]{:S(2)}) collective-permute-start(bf16[512,2048]{1,0:T(8,128)(2,1)S(1)} %slice.41.refs_5_.refs_7_.refs_0_), channel_id=1, source_target_pairs={{0,1},{1,0},{2,3},{3,2},{4,5},{5,4},{6,7},{7,6},{8,9},{9,8},{10,11... | collective-permute-start | bytes 6291464 | tf_op jit(solution)/shard_map/ppermute | solution.py:53
  52.4 51.4 %collective-permute-start.15 = (bf16[512,2048]{1,0:T(8,128)(2,1)S(1)}, bf16[512,2048]{1,0:T(8,128)(2,1)S(1)}, u32[]{:S(2)}, u32[]{:S(2)}) collective-permute-start(bf16[512,2048]{1,0:T(8,128)(2,1)S(1)} %slice.41.refs_5_.refs_7_.refs_0_), channel_id=1, source_target_pairs={{0,4},{1,3},{2,6},{3,1},{4,0},{5,7},{6,2},{7,5},{8,12},{9,11},{10,... | collective-permute-start | bytes 6291464 | tf_op jit(solution)/shard_map/ppermute | solution.py:53
  53.9 51.4 %collective-permute-start.14 = (bf16[512,2048]{1,0:T(8,128)(2,1)S(1)}, bf16[512,2048]{1,0:T(8,128)(2,1)}, u32[]{:S(2)}, u32[]{:S(2)}) collective-permute-start(bf16[512,2048]{1,0:T(8,128)(2,1)S(1)} %slice.41.refs_5_.refs_7_.refs_0_), channel_id=1, source_target_pairs={{0,2},{1,5},{2,0},{3,7},{4,6},{5,1},{6,4},{7,3},{8,10},{9,13},{10,... | collective-permute-start | bytes 6291464 | tf_op jit(solution)/shard_map/ppermute | solution.py:53
  58.6 46.7 %collective-permute-start.1 = (bf16[864,1024]{1,0:T(8,128)(2,1)S(1)}, bf16[864,1024]{1,0:T(8,128)(2,1)}, u32[]{:S(2)}, u32[]{:S(2)}) collective-permute-start(bf16[864,1024]{1,0:T(8,128)(2,1)S(1)} %collective-permute-done.refs_1_.refs_2_), channel_id=1, source_target_pairs={{8,16},{16,24},{9,17},{17,25},{10,18},{18,26},{11,19},{19,27},{12,... | collective-permute-start | bytes 5308424 | tf_op jit(solution)/shard_map/ppermute | solution.py:33
  60.9 45.9 %collective-permute-start.4 = (bf16[864,1024]{1,0:T(8,128)(2,1)S(1)}, bf16[864,1024]{1,0:T(8,128)(2,1)}, u32[]{:S(2)}, u32[]{:S(2)}) collective-permute-start(bf16[864,1024]{1,0:T(8,128)(2,1)S(1)} %collective-permute-done.3.refs_3_.refs_4_), channel_id=1, source_target_pairs={{8,0},{16,8},{9,1},{17,9},{10,2},{18,10},{11,3},{19,11},{12,4},{20... | collective-permute-start | bytes 5308424 | tf_op jit(solution)/shard_map/ppermute | solution.py:32
  62.2 44.9 %collective-permute-start.9 = (bf16[512,2048]{1,0:T(8,128)(2,1)S(1)}, bf16[512,2048]{1,0:T(8,128)(2,1)S(1)}, u32[]{:S(2)}, u32[]{:S(2)}) collective-permute-start(bf16[512,2048]{1,0:T(8,128)(2,1)S(1)} %collective-permute-done.8.refs_9_.refs_11_.refs_12_), channel_id=1, source_target_pairs={{0,1},{1,0},{2,3},{3,2},{4,5},{5,4},{6,7},{7,6},{8,9},{9,8},{10,11... | collective-permute-start | bytes 6291464 | tf_op jit(solution)/shard_map/ppermute | solution.py:53
  103.8 26.1 %collective-permute-start.18 = (bf16[512,2048]{1,0:T(8,128)(2,1)S(1)}, bf16[512,2048]{1,0:T(8,128)(2,1)}, u32[]{:S(2)}, u32[]{:S(2)}) collective-permute-start(bf16[512,2048]{1,0:T(8,128)(2,1)S(1)} %collective-permute-done.15.refs_9_.refs_11_.refs_4_), channel_id=1, source_target_pairs={{0,2},{1,5},{2,0},{3,7},{4,6},{5,1},{6,4},{7,3},{8,10},{9,13},{10,... | collective-permute-start | bytes 6291464 | tf_op jit(solution)/shard_map/ppermute | solution.py:53
  105.3 24.6 %collective-permute-start.10 = (bf16[512,2048]{1,0:T(8,128)(2,1)S(1)}, bf16[512,2048]{1,0:T(8,128)(2,1)S(1)}, u32[]{:S(2)}, u32[]{:S(2)}) collective-permute-start(bf16[512,2048]{1,0:T(8,128)(2,1)S(1)} %collective-permute-done.7.refs_7_.refs_9_.refs_10_), channel_id=1, source_target_pairs={{0,1},{1,0},{2,3},{3,2},{4,5},{5,4},{6,7},{7,6},{8,9},{9,8},{10,11... | collective-permute-start | bytes 6291464 | tf_op jit(solution)/shard_map/ppermute | solution.py:53
  105.4 47.0 %collective-permute-start.11 = (bf16[512,2048]{1,0:T(8,128)(2,1)S(1)}, bf16[512,2048]{1,0:T(8,128)(2,1)S(1)}, u32[]{:S(2)}, u32[]{:S(2)}) collective-permute-start(bf16[512,2048]{1,0:T(8,128)(2,1)S(1)} %collective-permute-done.8.refs_9_.refs_11_.refs_12_), channel_id=1, source_target_pairs={{0,2},{1,5},{2,0},{3,7},{4,6},{5,1},{6,4},{7,3},{8,10},{9,13},{10,... | collective-permute-start | bytes 6291464 | tf_op jit(solution)/shard_map/ppermute | solution.py:53
  106.8 47.4 %collective-permute-start.16 = (bf16[512,2048]{1,0:T(8,128)(2,1)S(1)}, bf16[512,2048]{1,0:T(8,128)(2,1)}, u32[]{:S(2)}, u32[]{:S(2)}) collective-permute-start(bf16[512,2048]{1,0:T(8,128)(2,1)S(1)} %collective-permute-done.15.refs_9_.refs_11_.refs_4_), channel_id=1, source_target_pairs={{0,1},{1,0},{2,3},{3,2},{4,5},{5,4},{6,7},{7,6},{8,9},{9,8},{10,11... | collective-permute-start | bytes 6291464 | tf_op jit(solution)/shard_map/ppermute | solution.py:53
  107.1 61.0 %collective-permute-start.17 = (bf16[512,2048]{1,0:T(8,128)(2,1)}, bf16[512,2048]{1,0:T(8,128)(2,1)}, u32[]{:S(2)}, u32[]{:S(2)}) collective-permute-start(bf16[512,2048]{1,0:T(8,128)(2,1)} %collective-permute-done.14.refs_7_.refs_9_.refs_2_), channel_id=1, source_target_pairs={{0,1},{1,0},{2,3},{3,2},{4,5},{5,4},{6,7},{7,6},{8,9},{9,8},{10,11... | collective-permute-start | bytes 6291464 | tf_op jit(solution)/shard_map/ppermute | solution.py:53
  130.0 64.8 %collective-permute-start.19 = (bf16[512,2048]{1,0:T(8,128)(2,1)}, bf16[512,2048]{1,0:T(8,128)(2,1)}, u32[]{:S(2)}, u32[]{:S(2)}) collective-permute-start(bf16[512,2048]{1,0:T(8,128)(2,1)} %collective-permute-done.18.refs_13_.refs_6_), channel_id=1, source_target_pairs={{0,1},{1,0},{2,3},{3,2},{4,5},{5,4},{6,7},{7,6},{8,9},{9,8},{10,11... | collective-permute-start | bytes 6291464 | tf_op jit(solution)/shard_map/ppermute | solution.py:53
  130.0 50.8 %collective-permute-start.2 = (bf16[864,1024]{1,0:T(8,128)(2,1)}, bf16[864,1024]{1,0:T(8,128)(2,1)}, u32[]{:S(2)}, u32[]{:S(2)}) collective-permute-start(bf16[864,1024]{1,0:T(8,128)(2,1)} %collective-permute-done.1.refs_0_.refs_1_), channel_id=1, source_target_pairs={{16,24},{17,25},{18,26},{19,27},{20,28},{21,29},{22,30},{23,31}} | collective-permute-start | bytes 5308424 | tf_op jit(solution)/shard_map/ppermute | solution.py:33
  152.4 42.5 %collective-permute-start.5 = (bf16[864,1024]{1,0:T(8,128)(2,1)}, bf16[864,1024]{1,0:T(8,128)(2,1)}, u32[]{:S(2)}, u32[]{:S(2)}) collective-permute-start(bf16[864,1024]{1,0:T(8,128)(2,1)} %collective-permute-done.4.refs_4_.refs_5_), channel_id=1, source_target_pairs={{8,0},{9,1},{10,2},{11,3},{12,4},{13,5},{14,6},{15,7}} | collective-permute-start | bytes 5308424 | tf_op jit(solution)/shard_map/ppermute | solution.py:32
  154.1 59.1 %collective-permute-start.12 = (bf16[512,2048]{1,0:T(8,128)(2,1)}, bf16[512,2048]{1,0:T(8,128)(2,1)}, u32[]{:S(2)}, u32[]{:S(2)}) collective-permute-start(bf16[512,2048]{1,0:T(8,128)(2,1)} %copy-done.17), channel_id=1, source_target_pairs={{0,1},{1,0},{2,3},{3,2},{4,5},{5,4},{6,7},{7,6},{8,9},{9,8},{10,11... | collective-permute-start | bytes 6291464 | tf_op jit(solution)/shard_map/ppermute | solution.py:53
  231.0 4.9 %collective-permute-start.27 = (bf16[24,2048]{1,0:T(8,128)(2,1)}, bf16[24,2048]{1,0:T(8,128)(2,1)S(1)}, u32[]{:S(2)}, u32[]{:S(2)}) collective-permute-start(bf16[24,2048]{1,0:T(8,128)(2,1)} %get-tuple-element.27), channel_id=1, source_target_pairs={{0,4},{1,3},{2,6},{3,1},{4,0},{5,7},{6,2},{7,5},{8,12},{9,11},{10,... | collective-permute-start | bytes 294920 | tf_op jit(solution)/shard_map/ppermute | solution.py:53
  232.2 35.6 %collective-permute-start.36 = (s32[12]{0:T(128)S(1)}, s32[12]{0:T(128)S(1)}, u32[]{:S(2)}, u32[]{:S(2)}) collective-permute-start(s32[12]{0:T(128)S(1)} %copy-done.25), channel_id=1, source_target_pairs={{0,1},{1,0},{2,3},{3,2},{4,5},{5,4},{6,7},{7,6},{8,9},{9,8},{10,11... | collective-permute-start | bytes 152 | tf_op jit(solution)/shard_map/ppermute | solution.py:53
  232.2 32.4 %collective-permute-start.37 = (s32[12]{0:T(128)S(1)}, s32[12]{0:T(128)S(1)}, u32[]{:S(2)}, u32[]{:S(2)}) collective-permute-start(s32[12]{0:T(128)S(1)} %copy-done.25), channel_id=1, source_target_pairs={{0,2},{1,5},{2,0},{3,7},{4,6},{5,1},{6,4},{7,3},{8,10},{9,13},{10,... | collective-permute-start | bytes 152 | tf_op jit(solution)/shard_map/ppermute | solution.py:53
  233.7 30.3 %collective-permute-start.38 = (s32[12]{0:T(128)S(1)}, s32[12]{0:T(128)S(1)}, u32[]{:S(2)}, u32[]{:S(2)}) collective-permute-start(s32[12]{0:T(128)S(1)} %copy-done.25), channel_id=1, source_target_pairs={{0,4},{1,3},{2,6},{3,1},{4,0},{5,7},{6,2},{7,5},{8,12},{9,11},{10,... | collective-permute-start | bytes 152 | tf_op jit(solution)/shard_map/ppermute | solution.py:53
  234.8 4.6 %collective-permute-start.20 = (bf16[24,2048]{1,0:T(8,128)(2,1)S(1)}, bf16[24,2048]{1,0:T(8,128)(2,1)S(1)}, u32[]{:S(2)}, u32[]{:S(2)}) collective-permute-start(bf16[24,2048]{1,0:T(8,128)(2,1)S(1)} %copy-done.22), channel_id=1, source_target_pairs={{0,4},{1,3},{2,6},{3,1},{4,0},{5,7},{6,2},{7,5},{8,12},{9,11},{10,... | collective-permute-start | bytes 294920 | tf_op jit(solution)/shard_map/ppermute | solution.py:53
  241.0 4.8 %collective-permute-start.30 = (bf16[24,2048]{1,0:T(8,128)(2,1)}, bf16[24,2048]{1,0:T(8,128)(2,1)S(1)}, u32[]{:S(2)}, u32[]{:S(2)}) collective-permute-start(bf16[24,2048]{1,0:T(8,128)(2,1)} %get-tuple-element.27), channel_id=1, source_target_pairs={{0,2},{1,5},{2,0},{3,7},{4,6},{5,1},{6,4},{7,3},{8,10},{9,13},{10,... | collective-permute-start | bytes 294920 | tf_op jit(solution)/shard_map/ppermute | solution.py:53
  241.4 4.8 %collective-permute-start.22 = (bf16[24,2048]{1,0:T(8,128)(2,1)S(1)}, bf16[24,2048]{1,0:T(8,128)(2,1)S(1)}, u32[]{:S(2)}, u32[]{:S(2)}) collective-permute-start(bf16[24,2048]{1,0:T(8,128)(2,1)S(1)} %copy-done.22), channel_id=1, source_target_pairs={{0,1},{1,0},{2,3},{3,2},{4,5},{5,4},{6,7},{7,6},{8,9},{9,8},{10,11... | collective-permute-start | bytes 294920 | tf_op jit(solution)/shard_map/ppermute | solution.py:53
  245.9 4.6 %collective-permute-start.23 = (bf16[24,2048]{1,0:T(8,128)(2,1)S(1)}, bf16[24,2048]{1,0:T(8,128)(2,1)S(1)}, u32[]{:S(2)}, u32[]{:S(2)}) collective-permute-start(bf16[24,2048]{1,0:T(8,128)(2,1)S(1)} %copy-done.22), channel_id=1, source_target_pairs={{0,2},{1,5},{2,0},{3,7},{4,6},{5,1},{6,4},{7,3},{8,10},{9,13},{10,... | collective-permute-start | bytes 294920 | tf_op jit(solution)/shard_map/ppermute | solution.py:53
  246.2 4.6 %collective-permute-start.31 = (bf16[24,2048]{1,0:T(8,128)(2,1)S(1)}, bf16[24,2048]{1,0:T(8,128)(2,1)S(1)}, u32[]{:S(2)}, u32[]{:S(2)}) collective-permute-start(bf16[24,2048]{1,0:T(8,128)(2,1)S(1)} %collective-permute-done.30), channel_id=1, source_target_pairs={{0,1},{1,0},{2,3},{3,2},{4,5},{5,4},{6,7},{7,6},{8,9},{9,8},{10,11... | collective-permute-start | bytes 294920 | tf_op jit(solution)/shard_map/ppermute | solution.py:53
  250.5 4.6 %collective-permute-start.32 = (bf16[24,2048]{1,0:T(8,128)(2,1)S(1)}, bf16[24,2048]{1,0:T(8,128)(2,1)S(1)}, u32[]{:S(2)}, u32[]{:S(2)}) collective-permute-start(bf16[24,2048]{1,0:T(8,128)(2,1)S(1)} %collective-permute-done.27), channel_id=1, source_target_pairs={{0,2},{1,5},{2,0},{3,7},{4,6},{5,1},{6,4},{7,3},{8,10},{9,13},{10,... | collective-permute-start | bytes 294920 | tf_op jit(solution)/shard_map/ppermute | solution.py:53
  250.9 4.6 %collective-permute-start.24 = (bf16[24,2048]{1,0:T(8,128)(2,1)S(1)}, bf16[24,2048]{1,0:T(8,128)(2,1)S(1)}, u32[]{:S(2)}, u32[]{:S(2)}) collective-permute-start(bf16[24,2048]{1,0:T(8,128)(2,1)S(1)} %collective-permute-done.23), channel_id=1, source_target_pairs={{0,1},{1,0},{2,3},{3,2},{4,5},{5,4},{6,7},{7,6},{8,9},{9,8},{10,11... | collective-permute-start | bytes 294920 | tf_op jit(solution)/shard_map/ppermute | solution.py:53
  255.1 4.6 %collective-permute-start.25 = (bf16[24,2048]{1,0:T(8,128)(2,1)S(1)}, bf16[24,2048]{1,0:T(8,128)(2,1)S(1)}, u32[]{:S(2)}, u32[]{:S(2)}) collective-permute-start(bf16[24,2048]{1,0:T(8,128)(2,1)S(1)} %collective-permute-done.20), channel_id=1, source_target_pairs={{0,2},{1,5},{2,0},{3,7},{4,6},{5,1},{6,4},{7,3},{8,10},{9,13},{10,... | collective-permute-start | bytes 294920 | tf_op jit(solution)/shard_map/ppermute | solution.py:53
  255.5 4.3 %collective-permute-start.33 = (bf16[24,2048]{1,0:T(8,128)(2,1)S(1)}, bf16[24,2048]{1,0:T(8,128)(2,1)S(1)}, u32[]{:S(2)}, u32[]{:S(2)}) collective-permute-start(bf16[24,2048]{1,0:T(8,128)(2,1)S(1)} %collective-permute-done.32), channel_id=1, source_target_pairs={{0,1},{1,0},{2,3},{3,2},{4,5},{5,4},{6,7},{7,6},{8,9},{9,8},{10,11... | collective-permute-start | bytes 294920 | tf_op jit(solution)/shard_map/ppermute | solution.py:53
  263.8 5.3 %collective-permute-start.34 = (f32[96,96]{0,1:T(8,128)S(1)}, f32[96,96]{0,1:T(8,128)S(1)}, u32[]{:S(2)}, u32[]{:S(2)}) collective-permute-start(f32[96,96]{0,1:T(8,128)S(1)} %convolution_add_fusion), channel_id=1, source_target_pairs={{0,8},{8,0},{16,24},{24,16},{1,9},{9,1},{17,25},{25,17},{2,10},{10... | collective-permute-start | bytes 110600 | tf_op jit(solution)/shard_map/ppermute | solution.py:509
  264.0 3.8 collective-permute-start.39
  269.1 5.1 %collective-permute-start.35 = (f32[96,96]{0,1:T(8,128)S(1)}, f32[96,96]{0,1:T(8,128)S(1)}, u32[]{:S(2)}, u32[]{:S(2)}) collective-permute-start(f32[96,96]{0,1:T(8,128)S(1)} %add.56), channel_id=1, source_target_pairs={{0,16},{8,24},{16,0},{24,8},{1,17},{9,25},{17,1},{25,9},{2,18},{10... | collective-permute-start | bytes 110600 | tf_op jit(solution)/shard_map/ppermute | solution.py:509
  293.6 17.8 %collective-permute-start.43 = (bf16[864,512]{1,0:T(8,128)(2,1)S(1)}, bf16[864,512]{1,0:T(8,128)(2,1)S(1)}, u32[]{:S(2)}, u32[]{:S(2)}) collective-permute-start(bf16[864,512]{1,0:T(8,128)(2,1)S(1)} %backward_first.3), channel_id=1, source_target_pairs={{24,16},{25,17},{26,18},{27,19},{28,20},{29,21},{30,22},{31,23}} | collective-permute-start | bytes 2654216 | tf_op jit(solution)/shard_map/ppermute | solution.py:441
  294.3 23.6 %collective-permute-start.44 = (bf16[864,512]{1,0:T(8,128)(2,1)S(1)}, bf16[864,512]{1,0:T(8,128)(2,1)S(1)}, u32[]{:S(2)}, u32[]{:S(2)}) collective-permute-start(bf16[864,512]{1,0:T(8,128)(2,1)S(1)} %backward_first.3), channel_id=1, source_target_pairs={{0,8},{1,9},{2,10},{3,11},{4,12},{5,13},{6,14},{7,15}} | collective-permute-start | bytes 2654216 | tf_op jit(solution)/shard_map/ppermute | solution.py:442
  309.3 22.3 %collective-permute-start.49 = (bf16[864,512]{1,0:T(8,128)(2,1)}, bf16[864,512]{1,0:T(8,128)(2,1)S(1)}, u32[]{:S(2)}, u32[]{:S(2)}) collective-permute-start(bf16[864,512]{1,0:T(8,128)(2,1)} %get-tuple-element.33), channel_id=1, source_target_pairs={{24,16},{25,17},{26,18},{27,19},{28,20},{29,21},{30,22},{31,23}} | collective-permute-start | bytes 2654216 | tf_op jit(solution)/shard_map/ppermute | solution.py:441
  310.0 27.0 %collective-permute-start.50 = (bf16[864,512]{1,0:T(8,128)(2,1)}, bf16[864,512]{1,0:T(8,128)(2,1)S(1)}, u32[]{:S(2)}, u32[]{:S(2)}) collective-permute-start(bf16[864,512]{1,0:T(8,128)(2,1)} %get-tuple-element.33), channel_id=1, source_target_pairs={{0,8},{1,9},{2,10},{3,11},{4,12},{5,13},{6,14},{7,15}} | collective-permute-start | bytes 2654216 | tf_op jit(solution)/shard_map/ppermute | solution.py:442
  325.9 25.4 %collective-permute-start.45 = (bf16[864,512]{1,0:T(8,128)(2,1)S(1)}, bf16[864,512]{1,0:T(8,128)(2,1)S(1)}, u32[]{:S(2)}, u32[]{:S(2)}) collective-permute-start(bf16[864,512]{1,0:T(8,128)(2,1)S(1)} %backward_part.6), channel_id=1, source_target_pairs={{16,8},{24,16},{17,9},{25,17},{18,10},{26,18},{19,11},{27,19},{20,... | collective-permute-start | bytes 2654216 | tf_op jit(solution)/shard_map/ppermute | solution.py:441
  326.6 29.3 %collective-permute-start.46 = (bf16[864,512]{1,0:T(8,128)(2,1)S(1)}, bf16[864,512]{1,0:T(8,128)(2,1)S(1)}, u32[]{:S(2)}, u32[]{:S(2)}) collective-permute-start(bf16[864,512]{1,0:T(8,128)(2,1)S(1)} %backward_part.6), channel_id=1, source_target_pairs={{0,8},{8,16},{1,9},{9,17},{2,10},{10,18},{3,11},{11,19},{4,12},{12... | collective-permute-start | bytes 2654216 | tf_op jit(solution)/shard_map/ppermute | solution.py:442
  344.9 29.2 %collective-permute-start.51 = (bf16[864,512]{1,0:T(8,128)(2,1)S(1)}, bf16[864,512]{1,0:T(8,128)(2,1)S(1)}, u32[]{:S(2)}, u32[]{:S(2)}) collective-permute-start(bf16[864,512]{1,0:T(8,128)(2,1)S(1)} %backward_part.10), channel_id=1, source_target_pairs={{16,8},{24,16},{17,9},{25,17},{18,10},{26,18},{19,11},{27,19},{20,... | collective-permute-start | bytes 2654216 | tf_op jit(solution)/shard_map/ppermute | solution.py:441
  345.7 29.2 %collective-permute-start.52 = (bf16[864,512]{1,0:T(8,128)(2,1)S(1)}, bf16[864,512]{1,0:T(8,128)(2,1)S(1)}, u32[]{:S(2)}, u32[]{:S(2)}) collective-permute-start(bf16[864,512]{1,0:T(8,128)(2,1)S(1)} %backward_part.10), channel_id=1, source_target_pairs={{0,8},{8,16},{1,9},{9,17},{2,10},{10,18},{3,11},{11,19},{4,12},{12... | collective-permute-start | bytes 2654216 | tf_op jit(solution)/shard_map/ppermute | solution.py:442
  367.9 32.5 %collective-permute-start.47 = (bf16[864,512]{1,0:T(8,128)(2,1)S(1)}, bf16[864,512]{1,0:T(8,128)(2,1)S(1)}, u32[]{:S(2)}, u32[]{:S(2)}) collective-permute-start(bf16[864,512]{1,0:T(8,128)(2,1)S(1)} %get-tuple-element.31), channel_id=1, source_target_pairs={{8,0},{16,8},{24,16},{9,1},{17,9},{25,17},{10,2},{18,10},{26,18},{... | collective-permute-start | bytes 2654216 | tf_op jit(solution)/shard_map/ppermute | solution.py:441
  369.2 31.2 %collective-permute-start.48 = (bf16[864,512]{1,0:T(8,128)(2,1)S(1)}, bf16[864,512]{1,0:T(8,128)(2,1)S(1)}, u32[]{:S(2)}, u32[]{:S(2)}) collective-permute-start(bf16[864,512]{1,0:T(8,128)(2,1)S(1)} %get-tuple-element.32), channel_id=1, source_target_pairs={{0,8},{8,16},{16,24},{1,9},{9,17},{17,25},{2,10},{10,18},{18,26},{... | collective-permute-start | bytes 2654216 | tf_op jit(solution)/shard_map/ppermute | solution.py:442
  386.9 24.1 %collective-permute-start.54 = (bf16[864,512]{1,0:T(8,128)(2,1)S(1)}, bf16[864,512]{1,0:T(8,128)(2,1)S(1)}, u32[]{:S(2)}, u32[]{:S(2)}) collective-permute-start(bf16[864,512]{1,0:T(8,128)(2,1)S(1)} %get-tuple-element.35), channel_id=1, source_target_pairs={{0,8},{8,16},{16,24},{1,9},{9,17},{17,25},{2,10},{10,18},{18,26},{... | collective-permute-start | bytes 2654216 | tf_op jit(solution)/shard_map/ppermute | solution.py:442
  391.3 19.7 %collective-permute-start.53 = (bf16[864,512]{1,0:T(8,128)(2,1)S(1)}, bf16[864,512]{1,0:T(8,128)(2,1)S(1)}, u32[]{:S(2)}, u32[]{:S(2)}) collective-permute-start(bf16[864,512]{1,0:T(8,128)(2,1)S(1)} %get-tuple-element.34), channel_id=1, source_target_pairs={{8,0},{16,8},{24,16},{9,1},{17,9},{25,17},{10,2},{18,10},{26,18},{... | collective-permute-start | bytes 2654216 | tf_op jit(solution)/shard_map/ppermute | solution.py:441
  (33 other events, 953.0 us)
